TPU v7x, 32 devices: a whole 2x2x4 slice. The times are simulated.
32 devices in a mesh: groups: 2 (over x), context: 16 (over z, y, core).
Axes of the slice: x: 2, y: 2, z: 4, core: 2. Of those that a mesh axis runs over, the one named last changes fastest.
Arguments:
- queries: bfloat16 [4096, 16, 128], P(('groups', 'context')), parts along dimension 0, may hold values from -24 to 24
- keys: bfloat16 [4096, 8, 128], P(('groups', 'context')), parts along dimension 0, may hold values from -24 to 24
- values: bfloat16 [4096, 8, 128], P(('groups', 'context')), parts along dimension 0, may hold values from -6 to 6
- grad_out: bfloat16 [4096, 16, 128], P(('groups', 'context')), parts along dimension 0, may hold values from -24 to 24
- readout: float32 [16, 128], replicated, may hold values from -4 to 4
- segments: int32 [4096], P(('groups', 'context')), parts along dimension 0, may hold values from 0 to 3, never falling along the last dimension, each value on 1 to 1024 neighbouring positions
- loss_mask: int32 [4096], P(('groups', 'context')), parts along dimension 0, may hold values from 0 to 1, as said below
- labels: int32 [4096], P(('groups', 'context')), parts along dimension 0, may hold values 0 or 1
Outputs:
- grad_queries: bfloat16 [4096, 16, 128], P(('groups', 'context')), parts along dimension 0
- grad_keys: bfloat16 [4096, 8, 128], P(('groups', 'context')), parts along dimension 0
- grad_values: bfloat16 [4096, 8, 128], P(('groups', 'context')), parts along dimension 0
There are 2 independent parts, one for each index of `groups`. A program takes and returns all parts, laid end to end along the dimension named above; an argument that names none is the same for every part. Nothing has to cross between parts.
Inputs may be any that keep to these rules, and one draw needn't show every extreme that they name: `loss_mask`: every entry of the first 128 positions is 0.
All inputs are finite; a program needn't handle non-finite values. No bound on the sum of `labels` on one device may be relied on, other than what follows from the above.
Results may differ from a plain program's by a relative error of at most 0.025.
Values may be sent and summed in bfloat16 or wider, within the bound.
No kernel may reach another device: no remote copies, remote signals or barrier semaphores. Data moves between devices by JAX's collectives and lax.ppermute only.
A program may use at most 128 MiB of HBM per device.

v0:
```python
import jax
import jax.numpy as jnp
from jax import lax
from jax.sharding import PartitionSpec as P

WINDOW = 1024


SCALE = 168.0 ** (-0.5)
NEGATIVE = -1e30


def from_behind(block, axis, distance):
    devices = range(lax.axis_size(axis))
    route = [(i - distance, i) for i in devices if i - distance in devices]
    return lax.ppermute(block, axis, route)


def masked_scores(query_group, key_part, mask):
    scores = (
        jnp.einsum("qgrd,kgd->grqk", query_group, key_part, preferred_element_type=jnp.float32)
        * SCALE
    )
    return jnp.where(mask, scores, NEGATIVE)


def normalize(scores, mask):
    row_max = jnp.max(scores, axis=-1, keepdims=True)
    row_total = jnp.sum(jnp.where(mask, jnp.exp(scores - row_max), 0.0), axis=-1, keepdims=True)
    log_total = row_max + jnp.log(row_total)
    return jnp.where(mask, jnp.exp(scores - log_total), 0.0)


def local(queries, keys, values, grad_out, readout, segments, loss_mask, labels):
    row_count = queries.shape[0]
    head_count = queries.shape[1]
    kv_count = keys.shape[1]
    head_dim = queries.shape[2]
    ratio = head_count // kv_count
    kv_group = 2
    halo_depth = WINDOW // row_count
    my_index = lax.axis_index("context")
    seg_wire = segments.astype(jnp.bfloat16)
    fetched = [
        from_behind((keys, values, seg_wire), "context", offset)
        for offset in range(1, halo_depth + 1)
    ]
    ordered = fetched[::-1]
    key_window = jnp.concatenate([piece[0] for piece in ordered] + [keys], axis=0)
    value_window = jnp.concatenate([piece[1] for piece in ordered] + [values], axis=0)
    seg_window = jnp.concatenate(
        [piece[2].astype(jnp.int32) for piece in ordered] + [segments], axis=0
    )
    query_pos = my_index * row_count + jnp.arange(row_count, dtype=jnp.int32)
    key_pos = (my_index - halo_depth) * row_count + jnp.arange(
        row_count * (halo_depth + 1), dtype=jnp.int32
    )
    distance = query_pos[:, None] - key_pos[None, :]
    allowed = (
        (distance >= 0)
        & (distance < WINDOW)
        & (key_pos[None, :] >= 0)
        & (segments[:, None] == seg_window[None, :])
    )
    mask = allowed[None, None]
    spans = [
        (slice(start, start + kv_group), slice(start * ratio, (start + kv_group) * ratio))
        for start in range(0, kv_count, kv_group)
    ]

    def split_heads(array):
        return array.reshape(row_count, kv_group, ratio, head_dim)

    probs = []
    outputs = []
    for kv_span, q_span in spans:
        prob = normalize(
            masked_scores(split_heads(queries[:, q_span]), key_window[:, kv_span], mask), mask
        )
        prob_low = prob.astype(jnp.bfloat16)
        out = jnp.einsum(
            "grqk,kgd->qgrd", prob_low, value_window[:, kv_span], preferred_element_type=jnp.float32
        )
        outputs.append(out.reshape(row_count, kv_group * ratio, head_dim))
        probs.append((prob, prob_low))
    attn_out = jnp.concatenate(outputs, axis=1)
    reward = jnp.sum(attn_out * readout[None], axis=(1, 2))
    live_rows = loss_mask.astype(jnp.float32)
    probe_grad = live_rows * (jax.nn.sigmoid(reward) - labels.astype(jnp.float32))
    grad_attn = (
        live_rows[:, None, None] * grad_out.astype(jnp.float32)
        + probe_grad[:, None, None] * readout[None]
    ).astype(jnp.bfloat16)
    delta = jnp.sum(grad_attn.astype(jnp.float32) * attn_out, axis=-1)
    query_parts = []
    key_parts = []
    value_parts = []
    for (kv_span, q_span), (prob, prob_low) in zip(spans, probs):
        grad_part = split_heads(grad_attn[:, q_span])
        query_group = split_heads(queries[:, q_span])
        grad_prob = jnp.einsum(
            "qgrd,kgd->grqk",
            grad_part,
            value_window[:, kv_span],
            preferred_element_type=jnp.float32,
        )
        delta_part = delta[:, q_span].reshape(row_count, kv_group, ratio)
        grad_score = (prob * (grad_prob - jnp.transpose(delta_part, (1, 2, 0))[..., None])).astype(
            jnp.bfloat16
        )
        query_grad = (
            jnp.einsum(
                "grqk,kgd->qgrd",
                grad_score,
                key_window[:, kv_span],
                preferred_element_type=jnp.float32,
            )
            * SCALE
        )
        query_parts.append(query_grad.reshape(row_count, kv_group * ratio, head_dim))
        key_parts.append(
            jnp.einsum(
                "grqk,qgrd->kgd", grad_score, query_group, preferred_element_type=jnp.float32
            )
            * SCALE
        )
        value_parts.append(
            jnp.einsum("grqk,qgrd->kgd", prob_low, grad_part, preferred_element_type=jnp.float32)
        )
    grad_queries = jnp.concatenate(query_parts, axis=1).astype(jnp.bfloat16)
    grad_queries, key_grads, value_grads = (
        grad_queries,
        jnp.concatenate(key_parts, axis=1),
        jnp.concatenate(value_parts, axis=1),
    )

    def block_of(array, offset):
        start = (halo_depth - offset) * row_count
        return array[start : start + row_count]

    key_total = block_of(key_grads, 0)
    value_total = block_of(value_grads, 0)
    for offset in range(1, halo_depth + 1):
        got_keys, got_values = from_behind(
            (block_of(key_grads, offset), block_of(value_grads, offset)), "context", -offset
        )
        key_total = key_total + got_keys
        value_total = value_total + got_values
    return (grad_queries, key_total.astype(jnp.bfloat16), value_total.astype(jnp.bfloat16))


def solution(mesh):
    in_specs = (
        P(("groups", "context"), None, None),
        P(("groups", "context"), None, None),
        P(("groups", "context"), None, None),
        P(("groups", "context"), None, None),
        P(),
        P(("groups", "context")),
        P(("groups", "context")),
        P(("groups", "context")),
    )
    out_specs = (
        P(("groups", "context"), None, None),
        P(("groups", "context"), None, None),
        P(("groups", "context"), None, None),
    )
    return jax.shard_map(local, mesh=mesh, in_specs=in_specs, out_specs=out_specs, check_vma=False)
```

profile of v0, /device:TPU:12, one launch (start us, length us, event | category | flops | bytes accessed | tf_op | source)
XLA Modules:
  0.0 461.2 jit_solution(8193998955481126626)
XLA Ops:
  3.3 3.4 collective-permute-start.14
  6.7 4.4 collective-permute-start.13
  22.3 5.6 %collective-permute-start.10 = (bf16[128]{0:T(256)(128)(2,1)S(1)}, bf16[128]{0:T(256)(128)(2,1)S(1)}, u32[]{:S(2)}, u32[]{:S(2)}) collective-permute-start(bf16[128]{0:T(256)(128)(2,1)S(1)} %convert_element_type.73), channel_id=1, source_target_pairs={{0,6},{1,7},{2,8},{3,9},{4,10},{5,11},{6,12},{7,13},{8,14},{9,15},... | collective-permute-start | bytes 776 | tf_op jit(solution)/shard_map/ppermute | solution.py:16
  29.2 3.1 collective-permute-start.11
  32.3 2.7 collective-permute-done.11
  34.9 2.9 collective-permute-start.7
  37.9 6.5 %collective-permute-start.6 = (bf16[128,8,128]{2,0,1:T(8,128)(2,1)S(1)}, bf16[128,8,128]{2,0,1:T(8,128)(2,1)S(1)}, u32[]{:S(2)}, u32[]{:S(2)}) collective-permute-start(bf16[128,8,128]{2,0,1:T(8,128)(2,1)S(1)} %copy.135), channel_id=1, source_target_pairs={{0,2},{1,3},{2,4},{3,5},{4,6},{5,7},{6,8},{7,9},{8,10},{9,11},{10,... | collective-permute-start | bytes 786440 | tf_op jit(solution)/shard_map/ppermute | solution.py:16
  50.1 37.5 %collective-permute-done.16 = bf16[128,8,128]{0,2,1:T(8,128)(2,1)S(1)} collective-permute-done((bf16[128,8,128]{0,2,1:T(8,128)(2,1)S(1)}, bf16[128,8,128]{0,2,1:T(8,128)(2,1)S(1)}, u32[]{:S(2)}, u32[]{:S(2)}) %collective-permute-start.16) | collective-permute-done | bytes 262176 | tf_op jit(solution)/shard_map/ppermute | solution.py:16
  89.6 5.6 %collective-permute-start.20 = (bf16[128,8,128]{0,2,1:T(8,128)(2,1)S(1)}, bf16[128,8,128]{0,2,1:T(8,128)(2,1)S(1)}, u32[]{:S(2)}, u32[]{:S(2)}) collective-permute-start(bf16[128,8,128]{0,2,1:T(8,128)(2,1)S(1)} %copy.145), channel_id=1, source_target_pairs={{0,4},{1,5},{2,6},{3,7},{4,8},{5,9},{6,10},{7,11},{8,12},{9,13},{1... | collective-permute-start | bytes 786440 | tf_op jit(solution)/shard_map/ppermute | solution.py:16
  95.2 2.8 collective-permute-start.21
  100.2 2.5 collective-permute-done.20
  104.6 2.9 collective-permute-done.21
  109.8 3.3 collective-permute-done.22
  114.5 7.9 %collective-permute-start.1 = (bf16[128,8,128]{2,0,1:T(8,128)(2,1)S(1)}, bf16[128,8,128]{2,0,1:T(8,128)(2,1)S(1)}, u32[]{:S(2)}, u32[]{:S(2)}) collective-permute-start(bf16[128,8,128]{2,0,1:T(8,128)(2,1)S(1)} %copy.135), channel_id=1, source_target_pairs={{0,7},{1,8},{2,9},{3,10},{4,11},{5,12},{6,13},{7,14},{8,15},{16,23... | collective-permute-start | bytes 786440 | tf_op jit(solution)/shard_map/ppermute | solution.py:16
  122.5 18.7 %collective-permute-done = bf16[128,8,128]{2,0,1:T(8,128)(2,1)S(1)} collective-permute-done((bf16[128,8,128]{2,0,1:T(8,128)(2,1)S(1)}, bf16[128,8,128]{2,0,1:T(8,128)(2,1)S(1)}, u32[]{:S(2)}, u32[]{:S(2)}) %collective-permute-start) | collective-permute-done | bytes 262176 | tf_op jit(solution)/shard_map/ppermute | solution.py:16
  143.2 6.5 %collective-permute-done.1 = bf16[128,8,128]{2,0,1:T(8,128)(2,1)S(1)} collective-permute-done((bf16[128,8,128]{2,0,1:T(8,128)(2,1)S(1)}, bf16[128,8,128]{2,0,1:T(8,128)(2,1)S(1)}, u32[]{:S(2)}, u32[]{:S(2)}) %collective-permute-start.1) | collective-permute-done | bytes 262176 | tf_op jit(solution)/shard_map/ppermute | solution.py:16
  149.7 6.6 %collective-permute-start.4 = (bf16[128,8,128]{2,0,1:T(8,128)(2,1)S(1)}, bf16[128,8,128]{2,0,1:T(8,128)(2,1)S(1)}, u32[]{:S(2)}, u32[]{:S(2)}) collective-permute-start(bf16[128,8,128]{2,0,1:T(8,128)(2,1)S(1)} %copy.135), channel_id=1, source_target_pairs={{0,4},{1,5},{2,6},{3,7},{4,8},{5,9},{6,10},{7,11},{8,12},{9,13},{1... | collective-permute-start | bytes 786440 | tf_op jit(solution)/shard_map/ppermute | solution.py:16
  158.6 4.5 collective-permute-done.4
  163.1 5.6 %collective-permute-done.5 = bf16[128,8,128]{2,0,1:T(8,128)(2,1)S(1)} collective-permute-done((bf16[128,8,128]{2,0,1:T(8,128)(2,1)S(1)}, bf16[128,8,128]{2,0,1:T(8,128)(2,1)S(1)}, u32[]{:S(2)}, u32[]{:S(2)}) %collective-permute-start.5) | collective-permute-done | bytes 262176 | tf_op jit(solution)/shard_map/ppermute | solution.py:16
  173.6 2.4 fusion.57
  176.8 2.4 fusion.56
  189.4 2.4 convolution_bitcast_fusion.4
  217.8 10.1 %collective-permute-done.31 = f32[128,8,128]{2,0,1:T(8,128)S(1)} collective-permute-done((f32[128,8,128]{2,0,1:T(8,128)}, f32[128,8,128]{2,0,1:T(8,128)S(1)}, u32[]{:S(2)}, u32[]{:S(2)}) %collective-permute-start.31) | collective-permute-done | bytes 524320 | tf_op jit(solution)/shard_map/ppermute | solution.py:16
  227.9 16.4 %collective-permute-start.26 = (f32[128,8,128]{2,0,1:T(8,128)S(1)}, f32[128,8,128]{2,0,1:T(8,128)S(1)}, u32[]{:S(2)}, u32[]{:S(2)}) collective-permute-start(f32[128,8,128]{2,0,1:T(8,128)S(1)} %get-tuple-element.32), channel_id=1, source_target_pairs={{3,0},{4,1},{5,2},{6,3},{7,4},{8,5},{9,6},{10,7},{11,8},{12,9},{13... | collective-permute-start | bytes 1572872 | tf_op jit(solution)/shard_map/ppermute | solution.py:16
  244.3 24.4 %collective-permute-start.25 = (f32[128,8,128]{2,0,1:T(8,128)S(1)}, f32[128,8,128]{2,0,1:T(8,128)S(1)}, u32[]{:S(2)}, u32[]{:S(2)}) collective-permute-start(f32[128,8,128]{2,0,1:T(8,128)S(1)} %get-tuple-element.33), channel_id=1, source_target_pairs={{2,0},{3,1},{4,2},{5,3},{6,4},{7,5},{8,6},{9,7},{10,8},{11,9},{12,... | collective-permute-start | bytes 1572872 | tf_op jit(solution)/shard_map/ppermute | solution.py:16
  268.7 10.9 %collective-permute-start.32 = (f32[128,8,128]{0,2,1:T(8,128)S(1)}, f32[128,8,128]{0,2,1:T(8,128)S(1)}, u32[]{:S(2)}, u32[]{:S(2)}) collective-permute-start(f32[128,8,128]{0,2,1:T(8,128)S(1)} %get-tuple-element.18), channel_id=1, source_target_pairs={{1,0},{2,1},{3,2},{4,3},{5,4},{6,5},{7,6},{8,7},{9,8},{10,9},{11,1... | collective-permute-start | bytes 1572872 | tf_op jit(solution)/shard_map/ppermute | solution.py:16
  280.9 16.5 %collective-permute-done.27 = f32[128,8,128]{2,0,1:T(8,128)S(1)} collective-permute-done((f32[128,8,128]{2,0,1:T(8,128)S(1)}, f32[128,8,128]{2,0,1:T(8,128)S(1)}, u32[]{:S(2)}, u32[]{:S(2)}) %collective-permute-start.27) | collective-permute-done | bytes 524320 | tf_op jit(solution)/shard_map/ppermute | solution.py:16
  300.1 47.3 %collective-permute-done.26 = f32[128,8,128]{2,0,1:T(8,128)S(1)} collective-permute-done((f32[128,8,128]{2,0,1:T(8,128)S(1)}, f32[128,8,128]{2,0,1:T(8,128)S(1)}, u32[]{:S(2)}, u32[]{:S(2)}) %collective-permute-start.26) | collective-permute-done | bytes 524320 | tf_op jit(solution)/shard_map/ppermute | solution.py:16
  349.3 28.2 %collective-permute-done.25 = f32[128,8,128]{2,0,1:T(8,128)S(1)} collective-permute-done((f32[128,8,128]{2,0,1:T(8,128)S(1)}, f32[128,8,128]{2,0,1:T(8,128)S(1)}, u32[]{:S(2)}, u32[]{:S(2)}) %collective-permute-start.25) | collective-permute-done | bytes 524320 | tf_op jit(solution)/shard_map/ppermute | solution.py:16
  383.4 3.0 collective-permute-start.33
  395.5 42.0 %collective-permute-done.34 = f32[128,8,128]{0,2,1:T(8,128)} collective-permute-done((f32[128,8,128]{0,2,1:T(8,128)}, f32[128,8,128]{0,2,1:T(8,128)}, u32[]{:S(2)}, u32[]{:S(2)}) %collective-permute-start.34) | collective-permute-done | bytes 524320 | tf_op jit(solution)/shard_map/ppermute | solution.py:16
  437.5 20.7 %collective-permute-done.33 = f32[128,8,128]{0,2,1:T(8,128)} collective-permute-done((f32[128,8,128]{0,2,1:T(8,128)S(1)}, f32[128,8,128]{0,2,1:T(8,128)}, u32[]{:S(2)}, u32[]{:S(2)}) %collective-permute-start.33) | collective-permute-done | bytes 524320 | tf_op jit(solution)/shard_map/ppermute | solution.py:16
  (222 shorter events, 99.6 us)
Async XLA Ops:
  1.4 46.3 %collective-permute-start.15 = (bf16[128]{0:T(256)(128)(2,1)S(1)}, bf16[128]{0:T(256)(128)(2,1)S(1)}, u32[]{:S(2)}, u32[]{:S(2)}) collective-permute-start(bf16[128]{0:T(256)(128)(2,1)S(1)} %convert_element_type.73), channel_id=1, source_target_pairs={{0,1},{1,2},{2,3},{3,4},{4,5},{5,6},{6,7},{7,8},{8,9},{9,10},{10,1... | collective-permute-start | bytes 776 | tf_op jit(solution)/shard_map/ppermute | solution.py:16
  3.3 43.1 %collective-permute-start.14 = (bf16[128]{0:T(256)(128)(2,1)S(1)}, bf16[128]{0:T(256)(128)(2,1)S(1)}, u32[]{:S(2)}, u32[]{:S(2)}) collective-permute-start(bf16[128]{0:T(256)(128)(2,1)S(1)} %convert_element_type.73), channel_id=1, source_target_pairs={{0,2},{1,3},{2,4},{3,5},{4,6},{5,7},{6,8},{7,9},{8,10},{9,11},{10,... | collective-permute-start | bytes 776 | tf_op jit(solution)/shard_map/ppermute | solution.py:16
  6.7 37.7 %collective-permute-start.13 = (bf16[128]{0:T(256)(128)(2,1)S(1)}, bf16[128]{0:T(256)(128)(2,1)S(1)}, u32[]{:S(2)}, u32[]{:S(2)}) collective-permute-start(bf16[128]{0:T(256)(128)(2,1)S(1)} %convert_element_type.73), channel_id=1, source_target_pairs={{0,3},{1,4},{2,5},{3,6},{4,7},{5,8},{6,9},{7,10},{8,11},{9,12},{10... | collective-permute-start | bytes 776 | tf_op jit(solution)/shard_map/ppermute | solution.py:16
  11.1 26.8 %collective-permute-start.12 = (bf16[128]{0:T(256)(128)(2,1)S(1)}, bf16[128]{0:T(256)(128)(2,1)S(1)}, u32[]{:S(2)}, u32[]{:S(2)}) collective-permute-start(bf16[128]{0:T(256)(128)(2,1)S(1)} %convert_element_type.73), channel_id=1, source_target_pairs={{0,4},{1,5},{2,6},{3,7},{4,8},{5,9},{6,10},{7,11},{8,12},{9,13},{1... | collective-permute-start | bytes 776 | tf_op jit(solution)/shard_map/ppermute | solution.py:16
  34.9 133.8 %collective-permute-start.7 = (bf16[128,8,128]{2,0,1:T(8,128)(2,1)S(1)}, bf16[128,8,128]{2,0,1:T(8,128)(2,1)S(1)}, u32[]{:S(2)}, u32[]{:S(2)}) collective-permute-start(bf16[128,8,128]{2,0,1:T(8,128)(2,1)S(1)} %copy.135), channel_id=1, source_target_pairs={{0,1},{1,2},{2,3},{3,4},{4,5},{5,6},{6,7},{7,8},{8,9},{9,10},{10,1... | collective-permute-start | bytes 786440 | tf_op jit(solution)/shard_map/ppermute | solution.py:16
  37.9 130.8 %collective-permute-start.6 = (bf16[128,8,128]{2,0,1:T(8,128)(2,1)S(1)}, bf16[128,8,128]{2,0,1:T(8,128)(2,1)S(1)}, u32[]{:S(2)}, u32[]{:S(2)}) collective-permute-start(bf16[128,8,128]{2,0,1:T(8,128)(2,1)S(1)} %copy.135), channel_id=1, source_target_pairs={{0,2},{1,3},{2,4},{3,5},{4,6},{5,7},{6,8},{7,9},{8,10},{9,11},{10,... | collective-permute-start | bytes 786440 | tf_op jit(solution)/shard_map/ppermute | solution.py:16
  44.4 50.9 %collective-permute-start.18 = (bf16[128,8,128]{0,2,1:T(8,128)(2,1)S(1)}, bf16[128,8,128]{0,2,1:T(8,128)(2,1)S(1)}, u32[]{:S(2)}, u32[]{:S(2)}) collective-permute-start(bf16[128,8,128]{0,2,1:T(8,128)(2,1)S(1)} %copy.145), channel_id=1, source_target_pairs={{0,6},{1,7},{2,8},{3,9},{4,10},{5,11},{6,12},{7,13},{8,14},{9,15},... | collective-permute-start | bytes 786440 | tf_op jit(solution)/shard_map/ppermute | solution.py:16
  46.3 43.2 %collective-permute-start.17 = (bf16[128,8,128]{0,2,1:T(8,128)(2,1)S(1)}, bf16[128,8,128]{0,2,1:T(8,128)(2,1)S(1)}, u32[]{:S(2)}, u32[]{:S(2)}) collective-permute-start(bf16[128,8,128]{0,2,1:T(8,128)(2,1)S(1)} %copy.145), channel_id=1, source_target_pairs={{0,7},{1,8},{2,9},{3,10},{4,11},{5,12},{6,13},{7,14},{8,15},{16,23... | collective-permute-start | bytes 786440 | tf_op jit(solution)/shard_map/ppermute | solution.py:16
  47.7 39.9 %collective-permute-start.16 = (bf16[128,8,128]{0,2,1:T(8,128)(2,1)S(1)}, bf16[128,8,128]{0,2,1:T(8,128)(2,1)S(1)}, u32[]{:S(2)}, u32[]{:S(2)}) collective-permute-start(bf16[128,8,128]{0,2,1:T(8,128)(2,1)S(1)} %copy.145), channel_id=1, source_target_pairs={{0,8},{1,9},{2,10},{3,11},{4,12},{5,13},{6,14},{7,15},{16,24},{17,... | collective-permute-start | bytes 786440 | tf_op jit(solution)/shard_map/ppermute | solution.py:16
  89.6 13.1 %collective-permute-start.20 = (bf16[128,8,128]{0,2,1:T(8,128)(2,1)S(1)}, bf16[128,8,128]{0,2,1:T(8,128)(2,1)S(1)}, u32[]{:S(2)}, u32[]{:S(2)}) collective-permute-start(bf16[128,8,128]{0,2,1:T(8,128)(2,1)S(1)} %copy.145), channel_id=1, source_target_pairs={{0,4},{1,5},{2,6},{3,7},{4,8},{5,9},{6,10},{7,11},{8,12},{9,13},{1... | collective-permute-start | bytes 786440 | tf_op jit(solution)/shard_map/ppermute | solution.py:16
  98.2 14.9 %collective-permute-start.22 = (bf16[128,8,128]{0,2,1:T(8,128)(2,1)S(1)}, bf16[128,8,128]{0,2,1:T(8,128)(2,1)S(1)}, u32[]{:S(2)}, u32[]{:S(2)}) collective-permute-start(bf16[128,8,128]{0,2,1:T(8,128)(2,1)S(1)} %copy.145), channel_id=1, source_target_pairs={{0,2},{1,3},{2,4},{3,5},{4,6},{5,7},{6,8},{7,9},{8,10},{9,11},{10,... | collective-permute-start | bytes 786440 | tf_op jit(solution)/shard_map/ppermute | solution.py:16
  107.5 48.8 %collective-permute-start.2 = (bf16[128,8,128]{2,0,1:T(8,128)(2,1)S(1)}, bf16[128,8,128]{2,0,1:T(8,128)(2,1)S(1)}, u32[]{:S(2)}, u32[]{:S(2)}) collective-permute-start(bf16[128,8,128]{2,0,1:T(8,128)(2,1)S(1)} %copy.135), channel_id=1, source_target_pairs={{0,6},{1,7},{2,8},{3,9},{4,10},{5,11},{6,12},{7,13},{8,14},{9,15},... | collective-permute-start | bytes 786440 | tf_op jit(solution)/shard_map/ppermute | solution.py:16
  113.1 28.1 %collective-permute-start = (bf16[128,8,128]{2,0,1:T(8,128)(2,1)S(1)}, bf16[128,8,128]{2,0,1:T(8,128)(2,1)S(1)}, u32[]{:S(2)}, u32[]{:S(2)}) collective-permute-start(bf16[128,8,128]{2,0,1:T(8,128)(2,1)S(1)} %copy.135), channel_id=1, source_target_pairs={{0,8},{1,9},{2,10},{3,11},{4,12},{5,13},{6,14},{7,15},{16,24},{17,... | collective-permute-start | bytes 786440 | tf_op jit(solution)/shard_map/ppermute | solution.py:16
  114.5 35.2 %collective-permute-start.1 = (bf16[128,8,128]{2,0,1:T(8,128)(2,1)S(1)}, bf16[128,8,128]{2,0,1:T(8,128)(2,1)S(1)}, u32[]{:S(2)}, u32[]{:S(2)}) collective-permute-start(bf16[128,8,128]{2,0,1:T(8,128)(2,1)S(1)} %copy.135), channel_id=1, source_target_pairs={{0,7},{1,8},{2,9},{3,10},{4,11},{5,12},{6,13},{7,14},{8,15},{16,23... | collective-permute-start | bytes 786440 | tf_op jit(solution)/shard_map/ppermute | solution.py:16
  141.2 17.3 %collective-permute-start.3 = (bf16[128,8,128]{2,0,1:T(8,128)(2,1)S(1)}, bf16[128,8,128]{2,0,1:T(8,128)(2,1)S(1)}, u32[]{:S(2)}, u32[]{:S(2)}) collective-permute-start(bf16[128,8,128]{2,0,1:T(8,128)(2,1)S(1)} %copy.135), channel_id=1, source_target_pairs={{0,5},{1,6},{2,7},{3,8},{4,9},{5,10},{6,11},{7,12},{8,13},{9,14},{... | collective-permute-start | bytes 786440 | tf_op jit(solution)/shard_map/ppermute | solution.py:16
  149.7 13.4 %collective-permute-start.4 = (bf16[128,8,128]{2,0,1:T(8,128)(2,1)S(1)}, bf16[128,8,128]{2,0,1:T(8,128)(2,1)S(1)}, u32[]{:S(2)}, u32[]{:S(2)}) collective-permute-start(bf16[128,8,128]{2,0,1:T(8,128)(2,1)S(1)} %copy.135), channel_id=1, source_target_pairs={{0,4},{1,5},{2,6},{3,7},{4,8},{5,9},{6,10},{7,11},{8,12},{9,13},{1... | collective-permute-start | bytes 786440 | tf_op jit(solution)/shard_map/ppermute | solution.py:16
  156.4 12.3 %collective-permute-start.5 = (bf16[128,8,128]{2,0,1:T(8,128)(2,1)S(1)}, bf16[128,8,128]{2,0,1:T(8,128)(2,1)S(1)}, u32[]{:S(2)}, u32[]{:S(2)}) collective-permute-start(bf16[128,8,128]{2,0,1:T(8,128)(2,1)S(1)} %copy.135), channel_id=1, source_target_pairs={{0,3},{1,4},{2,5},{3,6},{4,7},{5,8},{6,9},{7,10},{8,11},{9,12},{10... | collective-permute-start | bytes 786440 | tf_op jit(solution)/shard_map/ppermute | solution.py:16
  207.0 21.0 %collective-permute-start.31 = (f32[128,8,128]{2,0,1:T(8,128)}, f32[128,8,128]{2,0,1:T(8,128)S(1)}, u32[]{:S(2)}, u32[]{:S(2)}) collective-permute-start(f32[128,8,128]{2,0,1:T(8,128)} %get-tuple-element.27), channel_id=1, source_target_pairs={{8,0},{9,1},{10,2},{11,3},{12,4},{13,5},{14,6},{15,7},{24,16},{25,... | collective-permute-start | bytes 1572872 | tf_op jit(solution)/shard_map/ppermute | solution.py:16
  208.3 36.1 %collective-permute-start.30 = (f32[128,8,128]{2,0,1:T(8,128)S(1)}, f32[128,8,128]{2,0,1:T(8,128)S(1)}, u32[]{:S(2)}, u32[]{:S(2)}) collective-permute-start(f32[128,8,128]{2,0,1:T(8,128)S(1)} %get-tuple-element.28), channel_id=1, source_target_pairs={{7,0},{8,1},{9,2},{10,3},{11,4},{12,5},{13,6},{14,7},{15,8},{23,16... | collective-permute-start | bytes 1572872 | tf_op jit(solution)/shard_map/ppermute | solution.py:16
  209.6 59.1 %collective-permute-start.29 = (f32[128,8,128]{2,0,1:T(8,128)S(1)}, f32[128,8,128]{2,0,1:T(8,128)S(1)}, u32[]{:S(2)}, u32[]{:S(2)}) collective-permute-start(f32[128,8,128]{2,0,1:T(8,128)S(1)} %get-tuple-element.29), channel_id=1, source_target_pairs={{6,0},{7,1},{8,2},{9,3},{10,4},{11,5},{12,6},{13,7},{14,8},{15,9},... | collective-permute-start | bytes 1572872 | tf_op jit(solution)/shard_map/ppermute | solution.py:16
  211.5 68.1 %collective-permute-start.28 = (f32[128,8,128]{2,0,1:T(8,128)}, f32[128,8,128]{2,0,1:T(8,128)S(1)}, u32[]{:S(2)}, u32[]{:S(2)}) collective-permute-start(f32[128,8,128]{2,0,1:T(8,128)} %get-tuple-element.30), channel_id=1, source_target_pairs={{5,0},{6,1},{7,2},{8,3},{9,4},{10,5},{11,6},{12,7},{13,8},{14,9},{... | collective-permute-start | bytes 1572872 | tf_op jit(solution)/shard_map/ppermute | solution.py:16
  213.9 83.5 %collective-permute-start.27 = (f32[128,8,128]{2,0,1:T(8,128)S(1)}, f32[128,8,128]{2,0,1:T(8,128)S(1)}, u32[]{:S(2)}, u32[]{:S(2)}) collective-permute-start(f32[128,8,128]{2,0,1:T(8,128)S(1)} %get-tuple-element.31), channel_id=1, source_target_pairs={{4,0},{5,1},{6,2},{7,3},{8,4},{9,5},{10,6},{11,7},{12,8},{13,9},{1... | collective-permute-start | bytes 1572872 | tf_op jit(solution)/shard_map/ppermute | solution.py:16
  227.9 119.5 %collective-permute-start.26 = (f32[128,8,128]{2,0,1:T(8,128)S(1)}, f32[128,8,128]{2,0,1:T(8,128)S(1)}, u32[]{:S(2)}, u32[]{:S(2)}) collective-permute-start(f32[128,8,128]{2,0,1:T(8,128)S(1)} %get-tuple-element.32), channel_id=1, source_target_pairs={{3,0},{4,1},{5,2},{6,3},{7,4},{8,5},{9,6},{10,7},{11,8},{12,9},{13... | collective-permute-start | bytes 1572872 | tf_op jit(solution)/shard_map/ppermute | solution.py:16
  244.3 133.3 %collective-permute-start.25 = (f32[128,8,128]{2,0,1:T(8,128)S(1)}, f32[128,8,128]{2,0,1:T(8,128)S(1)}, u32[]{:S(2)}, u32[]{:S(2)}) collective-permute-start(f32[128,8,128]{2,0,1:T(8,128)S(1)} %get-tuple-element.33), channel_id=1, source_target_pairs={{2,0},{3,1},{4,2},{5,3},{6,4},{7,5},{8,6},{9,7},{10,8},{11,9},{12,... | collective-permute-start | bytes 1572872 | tf_op jit(solution)/shard_map/ppermute | solution.py:16
  268.7 110.8 %collective-permute-start.32 = (f32[128,8,128]{0,2,1:T(8,128)S(1)}, f32[128,8,128]{0,2,1:T(8,128)S(1)}, u32[]{:S(2)}, u32[]{:S(2)}) collective-permute-start(f32[128,8,128]{0,2,1:T(8,128)S(1)} %get-tuple-element.18), channel_id=1, source_target_pairs={{1,0},{2,1},{3,2},{4,3},{5,4},{6,5},{7,6},{8,7},{9,8},{10,9},{11,1... | collective-permute-start | bytes 1572872 | tf_op jit(solution)/shard_map/ppermute | solution.py:16
  279.6 101.9 %collective-permute-start.39 = (f32[128,8,128]{0,2,1:T(8,128)S(1)}, f32[128,8,128]{0,2,1:T(8,128)S(1)}, u32[]{:S(2)}, u32[]{:S(2)}) collective-permute-start(f32[128,8,128]{0,2,1:T(8,128)S(1)} %get-tuple-element.19), channel_id=1, source_target_pairs={{8,0},{9,1},{10,2},{11,3},{12,4},{13,5},{14,6},{15,7},{24,16},{25,... | collective-permute-start | bytes 1572872 | tf_op jit(solution)/shard_map/ppermute | solution.py:16
  297.4 86.0 %collective-permute-start.38 = (f32[128,8,128]{0,2,1:T(8,128)S(1)}, f32[128,8,128]{0,2,1:T(8,128)S(1)}, u32[]{:S(2)}, u32[]{:S(2)}) collective-permute-start(f32[128,8,128]{0,2,1:T(8,128)S(1)} %get-tuple-element.20), channel_id=1, source_target_pairs={{7,0},{8,1},{9,2},{10,3},{11,4},{12,5},{13,6},{14,7},{15,8},{23,16... | collective-permute-start | bytes 1572872 | tf_op jit(solution)/shard_map/ppermute | solution.py:16
  347.4 48.0 %collective-permute-start.37 = (f32[128,8,128]{0,2,1:T(8,128)}, f32[128,8,128]{0,2,1:T(8,128)}, u32[]{:S(2)}, u32[]{:S(2)}) collective-permute-start(f32[128,8,128]{0,2,1:T(8,128)} %get-tuple-element.21), channel_id=1, source_target_pairs={{6,0},{7,1},{8,2},{9,3},{10,4},{11,5},{12,6},{13,7},{14,8},{15,9},... | collective-permute-start | bytes 1572872 | tf_op jit(solution)/shard_map/ppermute | solution.py:16
  377.6 17.9 %collective-permute-start.36 = (f32[128,8,128]{0,2,1:T(8,128)}, f32[128,8,128]{0,2,1:T(8,128)}, u32[]{:S(2)}, u32[]{:S(2)}) collective-permute-start(f32[128,8,128]{0,2,1:T(8,128)} %get-tuple-element.22), channel_id=1, source_target_pairs={{5,0},{6,1},{7,2},{8,3},{9,4},{10,5},{11,6},{12,7},{13,8},{14,9},{... | collective-permute-start | bytes 1572872 | tf_op jit(solution)/shard_map/ppermute | solution.py:16
  379.5 15.9 %collective-permute-start.35 = (f32[128,8,128]{0,2,1:T(8,128)}, f32[128,8,128]{0,2,1:T(8,128)}, u32[]{:S(2)}, u32[]{:S(2)}) collective-permute-start(f32[128,8,128]{0,2,1:T(8,128)} %get-tuple-element.23), channel_id=1, source_target_pairs={{4,0},{5,1},{6,2},{7,3},{8,4},{9,5},{10,6},{11,7},{12,8},{13,9},{1... | collective-permute-start | bytes 1572872 | tf_op jit(solution)/shard_map/ppermute | solution.py:16
  381.5 56.0 %collective-permute-start.34 = (f32[128,8,128]{0,2,1:T(8,128)}, f32[128,8,128]{0,2,1:T(8,128)}, u32[]{:S(2)}, u32[]{:S(2)}) collective-permute-start(f32[128,8,128]{0,2,1:T(8,128)} %get-tuple-element.24), channel_id=1, source_target_pairs={{3,0},{4,1},{5,2},{6,3},{7,4},{8,5},{9,6},{10,7},{11,8},{12,9},{13... | collective-permute-start | bytes 1572872 | tf_op jit(solution)/shard_map/ppermute | solution.py:16
  383.4 74.7 %collective-permute-start.33 = (f32[128,8,128]{0,2,1:T(8,128)S(1)}, f32[128,8,128]{0,2,1:T(8,128)}, u32[]{:S(2)}, u32[]{:S(2)}) collective-permute-start(f32[128,8,128]{0,2,1:T(8,128)S(1)} %get-tuple-element.25), channel_id=1, source_target_pairs={{2,0},{3,1},{4,2},{5,3},{6,4},{7,5},{8,6},{9,7},{10,8},{11,9},{12,... | collective-permute-start | bytes 1572872 | tf_op jit(solution)/shard_map/ppermute | solution.py:16
  (46 other events, 1210.4 us)
where the time goes:
time: 463 us; the launch traced here: 461 us
  waiting for transfers between devices  251 us (54%)
  starting transfers between devices  149 us (32%)
  matrix products  22 us (5%)
  local copies, waits for them, and re-layouts  20.4 us (4%)
  other arithmetic  16.7 us (4%)
    ppermute x40, waiting for transfers between devices, from_behind(): return lax.ppermute(block, axis, route)  251 us
    ppermute x40, starting transfers between devices, from_behind(): return lax.ppermute(block, axis, route)  149 us
  transfers between devices with their start and end apart: 40, of which 17 were waited for; matrix products, arithmetic and copies ran while one was open for 4% of the time, Pallas kernels for 0%

commit v1 on v0

v1 whole, which is shorter than its diff:
```python
import functools
import math

import jax
import jax.numpy as jnp
from jax import lax
from jax.experimental import pallas as pl
from jax.experimental.pallas import tpu as pltpu
from jax.sharding import PartitionSpec as P

WINDOW = 1024
SCALE = 168.0 ** (-0.5)
LOG2E = math.log2(math.e)
NEGATIVE = -1e30
BLOCK = 256
AUX = 8
NT = (((1,), (1,)), ((), ()))
NN = (((1,), (0,)), ((), ()))


def dot(a, b, dims):
    return lax.dot_general(a, b, dims, preferred_element_type=jnp.float32)


def forward_kernel(
    halo, index_ref, message_ref, own_ref, other_ref, seg_ref, readout_ref,
    prob_ref, out_ref, inverse_ref, reward_ref, low_ref,
    key_s, value_s, bound_s, score_s,
):
    heads, tokens = message_ref.shape[0], message_ref.shape[0] * 128
    key_blocks = own_ref.shape[0]
    shift = halo // BLOCK
    index = index_ref[0]
    head = lax.rem(index, heads)
    even = lax.rem(index, 2) == 0

    def place(keys, values):
        for s in range(key_blocks):
            key_s[s * 128 : (s + 1) * 128, :] = keys[s]
            value_s[:, s * 128 : (s + 1) * 128] = values[s].T

    @pl.when(even)
    def _():
        place(own_ref, other_ref)

    @pl.when(jnp.logical_not(even))
    def _():
        place(other_ref, own_ref)

    seg_all = seg_ref[...]
    seg = seg_all[key_blocks - heads :]
    row = lax.broadcasted_iota(jnp.int32, (heads, 128), 0)
    lane = lax.broadcasted_iota(jnp.int32, (heads, 128), 1)
    token = halo + row * 128 + lane
    low = token - (WINDOW - 1)
    begin = jnp.zeros((heads, 128), jnp.int32)
    for s in range(0, 4):
        count = jnp.sum(jnp.where(seg_all < s, 1, 0))
        begin = jnp.where(seg == s, count, begin)
    low = jnp.maximum(low, begin)
    bound_s[...] = low
    for i in range(tokens // BLOCK):
        low_ref[i] = lax.div(jnp.min(low[2 * i : 2 * i + 1]), BLOCK)

    weights = jnp.broadcast_to(readout_ref[pl.ds(head, 1), :], (128, 128)).T[:, :1]
    key_iota = lax.broadcasted_iota(jnp.int32, (BLOCK, BLOCK), 0)
    query_iota = lax.broadcasted_iota(jnp.int32, (BLOCK, BLOCK), 1)

    def query_block(i, _):
        query = message_ref[pl.ds(2 * i, 2), 0:128, :].reshape(BLOCK, 128)
        bound = jnp.concatenate(
            [bound_s[pl.ds(2 * i, 1), :], bound_s[pl.ds(2 * i + 1, 1), :]], axis=1
        )
        last = i + shift
        first = low_ref[i]

        def scores(kb):
            start = pl.multiple_of(kb * BLOCK, BLOCK)
            return dot(key_s[pl.ds(start, BLOCK), :], query, NT) * (SCALE * LOG2E)

        def tops(score):
            return jnp.max(score.reshape(BLOCK // 8, 8, BLOCK), axis=0)

        def score_step(kb, top):
            score = jnp.where(key_iota >= bound - kb * BLOCK, scores(kb), NEGATIVE)
            score_s[last - kb] = score
            return jnp.maximum(top, tops(score))

        score = jnp.where(
            (key_iota >= bound - last * BLOCK) & (key_iota <= query_iota), scores(last), NEGATIVE
        )
        score_s[0] = score
        top = lax.fori_loop(first, last, score_step, tops(score))
        top = jnp.max(top, axis=0, keepdims=True)

        def value_step(kb, carry):
            total, out = carry
            prob = jnp.exp2(score_s[last - kb] - top)
            total = total + jnp.sum(prob.reshape(BLOCK // 8, 8, BLOCK), axis=0)
            prob = prob.astype(jnp.bfloat16)
            prob_ref[i, last - kb] = prob
            start = pl.multiple_of(kb * BLOCK, BLOCK)
            return total, out + dot(value_s[:, pl.ds(start, BLOCK)], prob, NN)

        total, out = lax.fori_loop(
            first,
            last + 1,
            value_step,
            (jnp.zeros((8, BLOCK), jnp.float32), jnp.zeros((128, BLOCK), jnp.float32)),
        )
        inverse = 1.0 / jnp.sum(total, axis=0, keepdims=True)
        out = out * inverse
        out_ref[:, pl.ds(pl.multiple_of(i * BLOCK, BLOCK), BLOCK)] = out
        inverse_ref[pl.ds(i, 1), :] = inverse
        reward = jnp.sum(out * weights, axis=0, keepdims=True)
        reward_ref[pl.ds(2 * i, 1), :] = reward[:, :128]
        reward_ref[pl.ds(2 * i + 1, 1), :] = reward[:, 128:]
        return 0

    lax.fori_loop(0, tokens // BLOCK, query_block, 0)


def backward_kernel(
    halo, index_ref, low_ref, message_ref, own_ref, other_ref, grad_ref, readout_ref, reward_ref,
    flag_ref, prob_ref, out_ref, inverse_ref,
    query_ref, keep_ref, send_ref,
    key_s, value_s, grad_s, delta_s, query_s, key_grad_s, value_grad_s,
):
    heads, tokens = message_ref.shape[0], message_ref.shape[0] * 128
    key_blocks = own_ref.shape[0]
    shift = halo // BLOCK
    index = index_ref[0]
    head = lax.rem(index, heads)
    even = lax.rem(index, 2) == 0

    def place(keys, values):
        for s in range(key_blocks):
            key_s[:, s * 128 : (s + 1) * 128] = keys[s].T
            value_s[s * 128 : (s + 1) * 128, :] = values[s]

    @pl.when(even)
    def _():
        place(own_ref, other_ref)

    @pl.when(jnp.logical_not(even))
    def _():
        place(other_ref, own_ref)

    live = flag_ref[0]
    probe = live * (jax.nn.sigmoid(reward_ref[...]) - flag_ref[1])
    live_t, probe_t = live.T, probe.T
    weights = readout_ref[pl.ds(head, 1), :]
    for s in range(heads):
        grad = live_t[:, s : s + 1] * grad_ref[s].astype(jnp.float32)
        grad = (grad + probe_t[:, s : s + 1] * weights).astype(jnp.bfloat16)
        grad_s[s] = grad
        out = out_ref[:, s * 128 : (s + 1) * 128]
        delta_s[s // 2 : s // 2 + 1, (s % 2) * 128 : (s % 2 + 1) * 128] = jnp.sum(
            grad.astype(jnp.float32).T * out, axis=0, keepdims=True
        )

    key_grad_s[...] = jnp.zeros_like(key_grad_s)
    value_grad_s[...] = jnp.zeros_like(value_grad_s)

    def query_block(i, _):
        query = message_ref[pl.ds(2 * i, 2), 0:128, :].reshape(BLOCK, 128)
        grad = grad_s[pl.ds(2 * i, 2)].reshape(BLOCK, 128)
        inverse = inverse_ref[pl.ds(i, 1), :]
        delta = delta_s[pl.ds(i, 1), :]
        last = i + shift

        def step(kb, query_grad):
            rows = pl.ds(pl.multiple_of(kb * BLOCK, BLOCK), BLOCK)
            prob = prob_ref[i, last - kb].astype(jnp.float32) * inverse
            value_grad_s[rows, :] += dot(prob.astype(jnp.bfloat16), grad, NN)
            grad_prob = dot(value_s[rows, :], grad, NT)
            grad_score = (prob * (grad_prob - delta)).astype(jnp.bfloat16)
            key_grad_s[rows, :] += dot(grad_score, query, NN)
            return query_grad + dot(key_s[:, rows], grad_score, NN)

        query_grad = lax.fori_loop(
            low_ref[i], last + 1, step, jnp.zeros((128, BLOCK), jnp.float32)
        )
        query_grad = (query_grad * SCALE).T.astype(jnp.bfloat16)
        query_ref[pl.ds(2 * i, 2)] = query_grad.reshape(2, 128, 128)
        return 0

    lax.fori_loop(0, tokens // BLOCK, query_block, 0)
    shape = keep_ref.shape

    @pl.when(even)
    def _():
        keep_ref[...] = (key_grad_s[...] * SCALE).astype(jnp.bfloat16).reshape(shape)
        send_ref[...] = value_grad_s[...].astype(jnp.bfloat16).reshape(shape)

    @pl.when(jnp.logical_not(even))
    def _():
        keep_ref[...] = value_grad_s[...].astype(jnp.bfloat16).reshape(shape)
        send_ref[...] = (key_grad_s[...] * SCALE).astype(jnp.bfloat16).reshape(shape)


def local(queries, keys, values, grad_out, readout, segments, loss_mask, labels):
    rows, heads, depth = queries.shape
    devices = lax.axis_size("context")
    index = lax.axis_index("context")
    clusters = [list(range(s, s + heads)) for s in range(0, devices, heads)]
    many = len(clusters) > 1
    halo = WINDOW if many else 0
    tokens = rows * heads
    key_tokens = tokens + halo
    pairs = [(i, i ^ 1) for i in range(devices)]
    bf16, f32 = jnp.bfloat16, jnp.float32

    def exchange(array):
        return lax.all_to_all(
            array, "context", 0, 0, tiled=True, axis_index_groups=clusters if many else None
        )

    def swap(array):
        return lax.ppermute(array, "context", pairs)

    pair = jnp.stack([keys, values], axis=2).reshape(rows, heads, depth)
    flags = jnp.stack([segments, loss_mask, labels]).astype(bf16)
    flags = jnp.pad(flags, ((0, AUX - 3), (0, 0)))
    message = jnp.concatenate(
        [
            jnp.transpose(queries, (1, 0, 2)),
            jnp.transpose(pair, (1, 0, 2)),
            jnp.broadcast_to(flags[None], (heads, AUX, depth)),
        ],
        axis=1,
    )
    message = exchange(message)
    later, message = lax.optimization_barrier((jnp.transpose(grad_out, (1, 0, 2)), message))
    grad = exchange(later)
    own = message[:, rows : 2 * rows]
    other = swap(own)
    flags = message[:, 2 * rows :]
    seg = flags[:, 0].astype(jnp.int32)
    flag = jnp.stack([flags[:, 1], flags[:, 2]]).astype(f32)
    if many:
        ahead = [(i, i + heads) for i in range(devices - heads)]
        blocks = halo // rows
        far = lax.ppermute((own[-blocks:], other[-blocks:], flags[-blocks:, 0]), "context", ahead)
        own = jnp.concatenate([far[0], own], axis=0)
        other = jnp.concatenate([far[1], other], axis=0)
        far_seg = jnp.where(index < heads, -1, far[2].astype(jnp.int32))
        seg = jnp.concatenate([far_seg, seg], axis=0)

    vmem = pl.BlockSpec(memory_space=pltpu.VMEM)
    smem = pl.BlockSpec(memory_space=pltpu.SMEM)
    count = tokens // BLOCK
    reach = WINDOW // BLOCK + 1
    where = jnp.reshape(index, (1,)).astype(jnp.int32)
    prob, out, inverse, reward, low = pl.pallas_call(
        functools.partial(forward_kernel, halo),
        out_shape=(
            jax.ShapeDtypeStruct((count, reach, BLOCK, BLOCK), bf16),
            jax.ShapeDtypeStruct((depth, tokens), f32),
            jax.ShapeDtypeStruct((count, BLOCK), f32),
            jax.ShapeDtypeStruct((heads, rows), f32),
            jax.ShapeDtypeStruct((count,), jnp.int32),
        ),
        in_specs=[smem] + [vmem] * 5,
        out_specs=(vmem, vmem, vmem, vmem, smem),
        scratch_shapes=[
            pltpu.VMEM((key_tokens, depth), bf16),
            pltpu.VMEM((depth, key_tokens), bf16),
            pltpu.VMEM((heads, rows), jnp.int32),
            pltpu.VMEM((reach, BLOCK, BLOCK), f32),
        ],
        compiler_params=pltpu.CompilerParams(vmem_limit_bytes=40 << 20),
        cost_estimate=pl.CostEstimate(
            flops=4 * BLOCK * BLOCK * depth * count * reach,
            bytes_accessed=16 << 20,
            transcendentals=BLOCK * BLOCK * count * reach,
        ),
        name="attention_forward",
    )(where, message, own, other, seg, readout)

    for step in (1, 2, 4, 8):
        reward = reward + lax.ppermute(reward, "context", [(i, i ^ step) for i in range(devices)])

    query_grad, keep, send = pl.pallas_call(
        functools.partial(backward_kernel, halo),
        out_shape=(
            jax.ShapeDtypeStruct((heads, rows, depth), bf16),
            jax.ShapeDtypeStruct((key_tokens // rows, rows, depth), bf16),
            jax.ShapeDtypeStruct((key_tokens // rows, rows, depth), bf16),
        ),
        in_specs=[smem, smem] + [vmem] * 10,
        out_specs=(vmem, vmem, vmem),
        scratch_shapes=[
            pltpu.VMEM((depth, key_tokens), bf16),
            pltpu.VMEM((key_tokens, depth), bf16),
            pltpu.VMEM((heads, rows, depth), bf16),
            pltpu.VMEM((count, BLOCK), f32),
            pltpu.VMEM((depth, tokens), f32),
            pltpu.VMEM((key_tokens, depth), f32),
            pltpu.VMEM((key_tokens, depth), f32),
        ],
        compiler_params=pltpu.CompilerParams(vmem_limit_bytes=40 << 20),
        cost_estimate=pl.CostEstimate(
            flops=8 * BLOCK * BLOCK * depth * count * reach,
            bytes_accessed=16 << 20,
            transcendentals=0,
        ),
        name="attention_backward",
    )(where, low, message, own, other, grad, readout, reward, flag, prob, out, inverse)

    total = keep.astype(f32) + swap(send).astype(f32)
    if many:
        behind = [(i + heads, i) for i in range(devices - heads)]
        back = lax.ppermute(total[:blocks].astype(bf16), "context", behind)
        total = total[blocks:]
        total = total + jnp.pad(
            back.astype(f32), ((heads - blocks, 0), (0, 0), (0, 0))
        )
    home = exchange(jnp.concatenate([query_grad, total.astype(bf16)], axis=1))
    home = jnp.transpose(home, (1, 0, 2))
    return home[:rows], home[rows:, 0::2], home[rows:, 1::2]


def solution(mesh):
    sharded = P(("groups", "context"))
    return jax.shard_map(
        local,
        mesh=mesh,
        in_specs=(sharded,) * 4 + (P(),) + (sharded,) * 3,
        out_specs=(sharded,) * 3,
        check_vma=False,
    )
```

time: 463 us -> 122 us (0.26)
  the two profiles are of different devices: /device:TPU:12 before, /device:TPU:1 now
where the time goes in v1:
time: 122 us; the launch traced here: 123 us
  blocking collectives  31.3 us (26%)
  waiting for transfers between devices  30.4 us (25%)
  starting transfers between devices  23.3 us (19%)
  Pallas kernels  21.7 us (18%)
  local copies, waits for them, and re-layouts  12.4 us (10%)
  other arithmetic  3.1 us (3%)
    all_to_all x1, blocking collectives, exchange(): lax.all_to_all(array, 'context', 0, 0, tiled=True, axis_index_groups=clus...  31.3 us
    all_to_all x2, waiting for transfers between devices, exchange(): lax.all_to_all(array, 'context', 0, 0, tiled=True, axis_index_groups=clus...  22.8 us
    all_to_all x2, starting transfers between devices, exchange(): lax.all_to_all(array, 'context', 0, 0, tiled=True, axis_index_groups=clus...  14.2 us
    unnamed x21, local copies, waits for them, and re-layouts  12 us
    pallas_call x1, Pallas kernels, local(): pl.pallas_call(functools.partial(backward_kernel, halo), out_shape=(jax.S...  11.4 us
    pallas_call x1, Pallas kernels, local(): pl.pallas_call(functools.partial(forward_kernel, halo), out_shape=(jax.Sh...  10.3 us
    ppermute x4, starting transfers between devices, local(): lax.ppermute(reward, 'context', [(i, i ^ step) for i in range(devices)])  5.24 us
    ppermute x4, waiting for transfers between devices, local(): lax.ppermute(reward, 'context', [(i, i ^ step) for i in range(devices)])  4.33 us
  transfers between devices with their start and end apart: 8, of which 7 were waited for; matrix products, arithmetic and copies ran while one was open for 1% of the time, Pallas kernels for 8%

profile of v1, /device:TPU:1, one launch (start us, length us, event | category | flops | bytes accessed | tf_op | source)
XLA Modules:
  0.0 123.0 jit_solution(14153754439521729927)
XLA Ops:
  0.7 0.7 convert_bitcast_fusion.2
  1.3 1.2 copy.33
  2.5 1.1 pad_maximum_fusion.2
  3.8 1.1 pad_maximum_fusion
  4.8 7.3 %all-to-all-start = ((bf16[16,264,128]{2,1,0:T(8,128)(2,1)}), bf16[16,264,128]{2,1,0:T(8,128)(2,1)S(1)}, u32[]{:S(2)}, u32[]{:S(2)}) async-start(bf16[16,264,128]{2,1,0:T(8,128)(2,1)} %pad_maximum_fusion), calls=%async_computation | async-start | bytes 2162688 | tf_op jit(solution)/shard_map/all_to_all | solution.py:215
  12.2 0.9 copy.34
  13.1 22.8 %all-to-all-done.message_ref = bf16[16,264,128]{2,1,0:T(8,128)(2,1)S(1)} async-done(((bf16[16,264,128]{2,1,0:T(8,128)(2,1)}), bf16[16,264,128]{2,1,0:T(8,128)(2,1)S(1)}, u32[]{:S(2)}, u32[]{:S(2)}) %all-to-all-start) | async-done | bytes 1081376 | tf_op jit(solution)/shard_map/all_to_all | solution.py:215
  36.0 6.9 %all-to-all-start.1 = ((bf16[16,128,128]{2,1,0:T(8,128)(2,1)}), bf16[16,128,128]{2,1,0:T(8,128)(2,1)S(1)}, u32[]{:S(2)}, u32[]{:S(2)}) async-start(bf16[16,128,128]{2,1,0:T(8,128)(2,1)} %bitcast.27), calls=%async_computation.1 | async-start | bytes 1048576 | tf_op jit(solution)/shard_map/all_to_all | solution.py:215
  42.9 0.2 collective-permute-start
  43.1 0.1 copy.25
  43.2 1.7 %collective-permute-done.other_ref = bf16[16,128,128]{2,1,0:T(8,128)(2,1)S(1)} collective-permute-done((bf16[16,128,128]{2,1,0:T(8,128)(2,1)S(1)}, bf16[16,128,128]{2,1,0:T(8,128)(2,1)S(1)}, u32[]{:S(2)}, u32[]{:S(2)}) %collective-permute-start) | collective-permute-done | bytes 524320 | tf_op jit(solution)/shard_map/ppermute | solution.py:220
  44.9 10.3 %attention_forward.1 = (bf16[8,5,256,256]{3,2,1,0:T(8,128)(2,1)S(1)}, f32[128,2048]{1,0:T(8,128)S(1)}, f32[8,256]{1,0:T(8,128)S(1)}, f32[16,128]{1,0:T(8,128)S(1)}, s32[8]{0:T(128)S(1)}) custom-call(s32[1]{0:T(128)} %bitcast.index_ref, bf16[16,264,128]{2,1,0:T(8,128)(2,1)S(1)} %all-to-all-done.message_ref, bf16[16,128,128]{2,1,0:T(8,128)(2,1)S(1)} %slice.25.own_ref, ...), custom_call_target="tpu_custom_call" | custom-call | flops 1342177280 | bytes 16777216 | tf_op jit(solution)/shard_map/attention_forward/pallas_call | solution.py:255
  55.2 2.3 %copy-done.1 = bf16[8,5,256,256]{3,2,1,0:T(8,128)(2,1)} copy-done((bf16[8,5,256,256]{3,2,1,0:T(8,128)(2,1)}, bf16[8,5,256,256]{3,2,1,0:T(8,128)(2,1)S(1)}, u32[]{:S(2)}) %copy-start.1) | copy-done | bytes 5242904
  57.5 1.0 copy-done.3
  58.5 0.1 collective-permute-start.1
  58.6 1.0 collective-permute-done.1
  59.7 1.4 %collective-permute-start.2 = (f32[16,128]{1,0:T(8,128)S(1)}, f32[16,128]{1,0:T(8,128)S(1)}, u32[]{:S(2)}, u32[]{:S(2)}) collective-permute-start(f32[16,128]{1,0:T(8,128)S(1)} %add.17), channel_id=1, source_target_pairs={{0,2},{1,3},{2,0},{3,1},{4,6},{5,7},{6,4},{7,5},{8,10},{9,11},{10,... | collective-permute-start | bytes 24584 | tf_op jit(solution)/shard_map/ppermute | solution.py:282
  61.1 1.1 collective-permute-done.2
  62.2 1.4 %collective-permute-start.3 = (f32[16,128]{1,0:T(8,128)S(1)}, f32[16,128]{1,0:T(8,128)S(1)}, u32[]{:S(2)}, u32[]{:S(2)}) collective-permute-start(f32[16,128]{1,0:T(8,128)S(1)} %add.18), channel_id=1, source_target_pairs={{0,4},{1,5},{2,6},{3,7},{4,0},{5,1},{6,2},{7,3},{8,12},{9,13},{10,... | collective-permute-start | bytes 24584 | tf_op jit(solution)/shard_map/ppermute | solution.py:282
  63.6 1.1 collective-permute-done.3
  64.7 2.3 %collective-permute-start.4 = (f32[16,128]{1,0:T(8,128)S(1)}, f32[16,128]{1,0:T(8,128)S(1)}, u32[]{:S(2)}, u32[]{:S(2)}) collective-permute-start(f32[16,128]{1,0:T(8,128)S(1)} %add.19), channel_id=1, source_target_pairs={{0,8},{1,9},{2,10},{3,11},{4,12},{5,13},{6,14},{7,15},{8,0},{9,1},... | collective-permute-start | bytes 24584 | tf_op jit(solution)/shard_map/ppermute | solution.py:282
  67.0 1.1 collective-permute-done.4
  68.1 2.5 %copy-done.2 = bf16[8,5,256,256]{3,2,1,0:T(8,128)(2,1)S(1)} copy-done((bf16[8,5,256,256]{3,2,1,0:T(8,128)(2,1)S(1)}, bf16[8,5,256,256]{3,2,1,0:T(8,128)(2,1)}, u32[]{:S(2)}) %copy-start.2) | copy-done | bytes 5242904
  70.6 1.2 copy-done.4
  71.8 11.4 %attention_backward.1 = (bf16[16,128,128]{2,1,0:T(8,128)(2,1)S(1)}, bf16[16,128,128]{2,1,0:T(8,128)(2,1)S(1)}, bf16[16,128,128]{2,1,0:T(8,128)(2,1)S(1)}) custom-call(s32[1]{0:T(128)} %bitcast.index_ref, s32[8]{0:T(128)S(1)} %get-tuple-element.14.low_ref, bf16[16,264,128]{2,1,0:T(8,128)(2,1)S(1)} %all-to-all-done.message_ref, ...), custom_call_target="tpu_custom_call" | custom-call | flops 2684354560 | bytes 16777216 | tf_op jit(solution)/shard_map/attention_backward/pallas_call | solution.py:284
  83.2 3.7 %collective-permute-start.5 = (bf16[16,128,128]{2,1,0:T(8,128)(2,1)S(1)}, bf16[16,128,128]{2,1,0:T(8,128)(2,1)S(1)}, u32[]{:S(2)}, u32[]{:S(2)}) collective-permute-start(bf16[16,128,128]{2,1,0:T(8,128)(2,1)S(1)} %get-tuple-element.22), channel_id=1, source_target_pairs={{0,1},{1,0},{2,3},{3,2},{4,5},{5,4},{6,7},{7,6},{8,9},{9,8},{10,11... | collective-permute-start | bytes 1572872 | tf_op jit(solution)/shard_map/ppermute | solution.py:220
  86.9 1.5 %collective-permute-done.5 = bf16[16,128,128]{2,1,0:T(8,128)(2,1)S(1)} collective-permute-done((bf16[16,128,128]{2,1,0:T(8,128)(2,1)S(1)}, bf16[16,128,128]{2,1,0:T(8,128)(2,1)S(1)}, u32[]{:S(2)}, u32[]{:S(2)}) %collective-permute-start.5) | collective-permute-done | bytes 524320 | tf_op jit(solution)/shard_map/ppermute | solution.py:220
  88.5 0.1 add_convert_fusion
  88.7 31.3 %all_to_all.15 = bf16[16,256,128]{2,1,0:T(8,128)(2,1)S(1)} all-to-all(bf16[16,256,128]{2,1,0:T(8,128)(2,1)S(1)} %pad_maximum_fusion.1), channel_id=1, replica_groups=mesh['groups'=2,'context'=16] {'context'}, dimensions={0} | all-to-all | bytes 2097152 | tf_op jit(solution)/shard_map/all_to_all | solution.py:215
  120.1 0.9 copy.30
  121.0 1.1 copy.28
  122.1 0.9 copy.29
  (27 shorter events, 0.4 us)
Async XLA Ops:
  0.6 3.1 %copy-start.6 = (s32[128]{0:T(128)S(1)}, s32[128]{0:T(128)}, u32[]{:S(2)}) copy-start(s32[128]{0:T(128)} %param.15) | copy-start | bytes 1540
  0.6 3.1 %copy-start.7 = (s32[128]{0:T(128)S(1)}, s32[128]{0:T(128)}, u32[]{:S(2)}) copy-start(s32[128]{0:T(128)} %param.14) | copy-start | bytes 1540
  3.8 8.4 %copy-start.5 = (bf16[128,16,128]{2,1,0:T(8,128)(2,1)S(1)}, bf16[128,16,128]{2,1,0:T(8,128)(2,1)}, u32[]{:S(2)}) copy-start(bf16[128,16,128]{2,1,0:T(8,128)(2,1)} %param.11) | copy-start | bytes 1572868
  4.8 31.1 %all-to-all-start = ((bf16[16,264,128]{2,1,0:T(8,128)(2,1)}), bf16[16,264,128]{2,1,0:T(8,128)(2,1)S(1)}, u32[]{:S(2)}, u32[]{:S(2)}) async-start(bf16[16,264,128]{2,1,0:T(8,128)(2,1)} %pad_maximum_fusion), calls=%async_computation | async-start | bytes 2162688 | tf_op jit(solution)/shard_map/all_to_all | solution.py:215
  36.0 8.9 %copy-start = (f32[16,128]{1,0:T(8,128)S(1)}, f32[16,128]{1,0:T(8,128)}, u32[]{:S(2)}) copy-start(f32[16,128]{1,0:T(8,128)} %readout_ref.3) | copy-start | bytes 24580
  36.0 32.1 %all-to-all-start.1 = ((bf16[16,128,128]{2,1,0:T(8,128)(2,1)}), bf16[16,128,128]{2,1,0:T(8,128)(2,1)S(1)}, u32[]{:S(2)}, u32[]{:S(2)}) async-start(bf16[16,128,128]{2,1,0:T(8,128)(2,1)} %bitcast.27), calls=%async_computation.1 | async-start | bytes 1048576 | tf_op jit(solution)/shard_map/all_to_all | solution.py:215
  42.9 2.0 %collective-permute-start = (bf16[16,128,128]{2,1,0:T(8,128)(2,1)S(1)}, bf16[16,128,128]{2,1,0:T(8,128)(2,1)S(1)}, u32[]{:S(2)}, u32[]{:S(2)}) collective-permute-start(bf16[16,128,128]{2,1,0:T(8,128)(2,1)S(1)} %slice.25.own_ref), channel_id=1, source_target_pairs={{0,1},{1,0},{2,3},{3,2},{4,5},{5,4},{6,7},{7,6},{8,9},{9,8},{10,11... | collective-permute-start | bytes 1572872 | tf_op jit(solution)/shard_map/ppermute | solution.py:220
  55.2 2.3 %copy-start.1 = (bf16[8,5,256,256]{3,2,1,0:T(8,128)(2,1)}, bf16[8,5,256,256]{3,2,1,0:T(8,128)(2,1)S(1)}, u32[]{:S(2)}) copy-start(bf16[8,5,256,256]{3,2,1,0:T(8,128)(2,1)S(1)} %get-tuple-element.17.prob_ref) | copy-start | bytes 15728644
  57.5 1.0 copy-start.3
  58.5 1.2 collective-permute-start.1
  59.7 2.5 %collective-permute-start.2 = (f32[16,128]{1,0:T(8,128)S(1)}, f32[16,128]{1,0:T(8,128)S(1)}, u32[]{:S(2)}, u32[]{:S(2)}) collective-permute-start(f32[16,128]{1,0:T(8,128)S(1)} %add.17), channel_id=1, source_target_pairs={{0,2},{1,3},{2,0},{3,1},{4,6},{5,7},{6,4},{7,5},{8,10},{9,11},{10,... | collective-permute-start | bytes 24584 | tf_op jit(solution)/shard_map/ppermute | solution.py:282
  62.2 2.5 %collective-permute-start.3 = (f32[16,128]{1,0:T(8,128)S(1)}, f32[16,128]{1,0:T(8,128)S(1)}, u32[]{:S(2)}, u32[]{:S(2)}) collective-permute-start(f32[16,128]{1,0:T(8,128)S(1)} %add.18), channel_id=1, source_target_pairs={{0,4},{1,5},{2,6},{3,7},{4,0},{5,1},{6,2},{7,3},{8,12},{9,13},{10,... | collective-permute-start | bytes 24584 | tf_op jit(solution)/shard_map/ppermute | solution.py:282
  64.7 3.4 %collective-permute-start.4 = (f32[16,128]{1,0:T(8,128)S(1)}, f32[16,128]{1,0:T(8,128)S(1)}, u32[]{:S(2)}, u32[]{:S(2)}) collective-permute-start(f32[16,128]{1,0:T(8,128)S(1)} %add.19), channel_id=1, source_target_pairs={{0,8},{1,9},{2,10},{3,11},{4,12},{5,13},{6,14},{7,15},{8,0},{9,1},... | collective-permute-start | bytes 24584 | tf_op jit(solution)/shard_map/ppermute | solution.py:282
  68.1 2.5 %copy-start.2 = (bf16[8,5,256,256]{3,2,1,0:T(8,128)(2,1)S(1)}, bf16[8,5,256,256]{3,2,1,0:T(8,128)(2,1)}, u32[]{:S(2)}) copy-start(bf16[8,5,256,256]{3,2,1,0:T(8,128)(2,1)} %copy-done.1) | copy-start | bytes 15728644
  70.6 1.2 copy-start.4
  83.2 5.2 %collective-permute-start.5 = (bf16[16,128,128]{2,1,0:T(8,128)(2,1)S(1)}, bf16[16,128,128]{2,1,0:T(8,128)(2,1)S(1)}, u32[]{:S(2)}, u32[]{:S(2)}) collective-permute-start(bf16[16,128,128]{2,1,0:T(8,128)(2,1)S(1)} %get-tuple-element.22), channel_id=1, source_target_pairs={{0,1},{1,0},{2,3},{3,2},{4,5},{5,4},{6,7},{7,6},{8,9},{9,8},{10,11... | collective-permute-start | bytes 1572872 | tf_op jit(solution)/shard_map/ppermute | solution.py:220

commit v2 on v1

v2 whole, which is shorter than its diff:
```python
import functools
import math

import jax
import jax.numpy as jnp
from jax import lax
from jax.experimental import pallas as pl
from jax.experimental.pallas import tpu as pltpu
from jax.sharding import PartitionSpec as P

WINDOW = 1024
SCALE = 168.0 ** (-0.5)
LOG2E = math.log2(math.e)
NEGATIVE = -1e30
BLOCK = 256
AUX = 8
REACH = WINDOW // BLOCK + 1
VMEM = pl.BlockSpec(memory_space=pltpu.VMEM)
SMEM = pl.BlockSpec(memory_space=pltpu.SMEM)
HBM = pl.BlockSpec(memory_space=pltpu.HBM)
NT = (((1,), (1,)), ((), ()))
NN = (((1,), (0,)), ((), ()))


def dot(a, b, dims):
    return lax.dot_general(a, b, dims, preferred_element_type=jnp.float32)


def starts_of(seg_all, halo):
    return [jnp.sum(jnp.where(seg_all < s, 1, 0)) for s in range(0 if halo else 1, 4)]


def begin_of(starts, token):
    begin = jnp.zeros_like(token)
    for start in starts:
        begin = jnp.maximum(begin, jnp.where(start <= token, start, 0))
    return jnp.maximum(begin, token - (WINDOW - 1))


def by_reach(count, body):
    for n in range(1, REACH + 1):
        pl.when(count == n)(functools.partial(body, n))


def chunk(n):
    return pl.ds(n * BLOCK, BLOCK)


def forward_kernel(
    halo, index_ref, message_ref, own_ref, other_ref, seg_ref, readout_ref,
    prob_ref, inverse_ref, reward_ref, low_ref,
    key_s, side_s, bound_s, prob_s, sems,
):
    heads, tokens = message_ref.shape[0], message_ref.shape[0] * 128
    key_blocks = own_ref.shape[0]
    shift = halo // BLOCK
    index = index_ref[0]
    head = lax.rem(index, heads)
    even = lax.rem(index, 2) == 0
    low_bits = jnp.bfloat16

    weights = jnp.broadcast_to(readout_ref[pl.ds(head, 1), :], (8, 128))
    part = lax.broadcasted_iota(jnp.int32, (8, 128), 0)
    high = weights.astype(low_bits).astype(jnp.float32)
    middle = (weights - high).astype(low_bits).astype(jnp.float32)
    rest = weights - high - middle
    split = jnp.where(part == 0, high, jnp.where(part == 1, middle, rest))
    split = jnp.where(part < 3, split, 0.0).astype(low_bits)
    side = lax.broadcasted_iota(jnp.int32, (8, 128), 0)

    def place(keys, values):
        for s in range(key_blocks):
            key_s[s * 128 : (s + 1) * 128, :] = keys[s]
            worth = jnp.sum(dot(split, values[s], NT), axis=0, keepdims=True)
            worth_high = worth.astype(low_bits).astype(jnp.float32)
            lines = jnp.where(side == 0, worth_high, jnp.where(side == 1, worth - worth_high, 0.0))
            side_s[:, s * 128 : (s + 1) * 128] = jnp.where(side == 2, 1.0, lines).astype(low_bits)

    @pl.when(even)
    def _():
        place(own_ref, other_ref)

    @pl.when(jnp.logical_not(even))
    def _():
        place(other_ref, own_ref)

    starts = starts_of(seg_ref[...], halo)
    token = halo + lax.broadcasted_iota(jnp.int32, (tokens // BLOCK, BLOCK), 0) * BLOCK
    token = token + lax.broadcasted_iota(jnp.int32, (tokens // BLOCK, BLOCK), 1)
    bound_s[...] = begin_of(starts, token)
    key_iota = lax.broadcasted_iota(jnp.int32, (BLOCK, BLOCK), 0)
    query_iota = lax.broadcasted_iota(jnp.int32, (BLOCK, BLOCK), 1)

    def copy(i):
        return pltpu.make_async_copy(prob_s.at[i], prob_ref.at[i], sems.at[i])

    def query_block(i, _):
        first = lax.div(begin_of(starts, halo + i * BLOCK), BLOCK)
        low_ref[i] = first

        def body(n):
            query = message_ref[pl.ds(2 * i, 2), 0:128, :].reshape(BLOCK, 128)
            bound = bound_s[pl.ds(i, 1), :] - first * BLOCK
            scores, tops = [], []
            for j in range(n):
                rows = pl.ds(pl.multiple_of((first + j) * BLOCK, BLOCK), BLOCK)
                valid = key_iota >= bound - j * BLOCK
                if j == n - 1:
                    valid = valid & (key_iota <= query_iota)
                score = jnp.where(valid, dot(key_s[rows, :], query, NT), NEGATIVE)
                scores.append(score)
                tops.append(jnp.max(score.reshape(BLOCK // 8, 8, BLOCK), axis=0))
            top = jnp.max(functools.reduce(jnp.maximum, tops), axis=0, keepdims=True)
            sums = jnp.zeros((8, BLOCK), jnp.float32)
            for j in range(n):
                prob = jnp.exp2((scores[j] - top) * (SCALE * LOG2E)).astype(low_bits)
                prob_s[i, chunk(j), :] = prob
                columns = pl.ds(pl.multiple_of((first + j) * BLOCK, BLOCK), BLOCK)
                sums = sums + dot(side_s[:, columns], prob, NN)
            inverse = 1.0 / sums[2:3]
            reward = (sums[0:1] + sums[1:2]) * inverse
            for half in range(2):
                lanes = slice(half * 128, (half + 1) * 128)
                inverse_ref[pl.ds(2 * i + half, 1), :] = inverse[:, lanes]
                reward_ref[pl.ds(2 * i + half, 1), :] = reward[:, lanes]

        by_reach(i + shift + 1 - first, body)
        copy(i).start()
        return 0

    lax.fori_loop(0, tokens // BLOCK, query_block, 0)

    def finish(i, _):
        copy(i).wait()
        return 0

    lax.fori_loop(0, tokens // BLOCK, finish, 0)


def backward_kernel(
    halo, index_ref, low_ref, message_ref, own_ref, other_ref, grad_ref, readout_ref, reward_ref,
    flag_ref, inverse_ref, prob_ref,
    query_ref, keep_ref, send_ref,
    key_s, value_s, grad_s, scaled_s, query_s, prob_s, key_grad_s, value_grad_s, sems,
):
    heads, tokens = message_ref.shape[0], message_ref.shape[0] * 128
    key_blocks = own_ref.shape[0]
    shift = halo // BLOCK
    index = index_ref[0]
    head = lax.rem(index, heads)
    even = lax.rem(index, 2) == 0

    def copy(i):
        return pltpu.make_async_copy(prob_ref.at[i], prob_s.at[i], sems.at[i])

    for i in range(tokens // BLOCK):
        copy(i).start()

    def place(keys, values):
        for s in range(key_blocks):
            key_s[:, s * 128 : (s + 1) * 128] = keys[s].T
            value_s[s * 128 : (s + 1) * 128, :] = values[s]

    @pl.when(even)
    def _():
        place(own_ref, other_ref)

    @pl.when(jnp.logical_not(even))
    def _():
        place(other_ref, own_ref)

    live = flag_ref[0]
    probe = live * (jax.nn.sigmoid(reward_ref[...]) - flag_ref[1])
    live_t, probe_t, inverse_t = live.T, probe.T, inverse_ref[...].T
    weights = readout_ref[pl.ds(head, 1), :]
    for s in range(heads):
        grad = live_t[:, s : s + 1] * grad_ref[s].astype(jnp.float32)
        grad = (grad + probe_t[:, s : s + 1] * weights).astype(jnp.bfloat16)
        inverse = inverse_t[:, s : s + 1]
        grad_s[s] = grad
        scaled_s[s] = (grad.astype(jnp.float32) * inverse).astype(jnp.bfloat16)
        query_s[s] = (message_ref[s, 0:128, :].astype(jnp.float32) * inverse).astype(jnp.bfloat16)

    key_grad_s[...] = jnp.zeros_like(key_grad_s)
    value_grad_s[...] = jnp.zeros_like(value_grad_s)

    def query_block(i, _):
        first = low_ref[i]
        copy(i).wait()

        def body(n):
            grad = grad_s[pl.ds(2 * i, 2)].reshape(BLOCK, 128)
            scaled = scaled_s[pl.ds(2 * i, 2)].reshape(BLOCK, 128)
            query = query_s[pl.ds(2 * i, 2)].reshape(BLOCK, 128)
            inverse = jnp.concatenate(
                [inverse_ref[pl.ds(2 * i, 1), :], inverse_ref[pl.ds(2 * i + 1, 1), :]], axis=1
            )
            rows = [pl.ds(pl.multiple_of((first + j) * BLOCK, BLOCK), BLOCK) for j in range(n)]
            grad_probs = []
            delta = jnp.zeros((8, BLOCK), jnp.float32)
            for j in range(n):
                grad_prob = dot(value_s[rows[j], :], grad, NT)
                grad_probs.append(grad_prob)
                prob = prob_s[i, chunk(j), :].astype(jnp.float32)
                delta = delta + jnp.sum((prob * grad_prob).reshape(BLOCK // 8, 8, BLOCK), axis=0)
                value_grad_s[rows[j], :] += dot(prob_s[i, chunk(j), :], scaled, NN)
            delta = jnp.sum(delta, axis=0, keepdims=True) * inverse
            query_grad = jnp.zeros((128, BLOCK), jnp.float32)
            for j in range(n):
                prob = prob_s[i, chunk(j), :].astype(jnp.float32)
                grad_score = (prob * (grad_probs[j] - delta)).astype(jnp.bfloat16)
                key_grad_s[rows[j], :] += dot(grad_score, query, NN)
                query_grad = query_grad + dot(key_s[:, rows[j]], grad_score, NN)
            query_grad = (query_grad * (inverse * SCALE)).T.astype(jnp.bfloat16)
            query_ref[pl.ds(2 * i, 2)] = query_grad.reshape(2, 128, 128)

        by_reach(i + shift + 1 - first, body)
        return 0

    lax.fori_loop(0, tokens // BLOCK, query_block, 0)
    shape = keep_ref.shape

    @pl.when(even)
    def _():
        keep_ref[...] = (key_grad_s[...] * SCALE).astype(jnp.bfloat16).reshape(shape)
        send_ref[...] = value_grad_s[...].astype(jnp.bfloat16).reshape(shape)

    @pl.when(jnp.logical_not(even))
    def _():
        keep_ref[...] = value_grad_s[...].astype(jnp.bfloat16).reshape(shape)
        send_ref[...] = (key_grad_s[...] * SCALE).astype(jnp.bfloat16).reshape(shape)


def attention_forward(halo, where, message, own, other, seg, readout):
    heads, depth = message.shape[0], message.shape[2]
    key_tokens = own.shape[0] * own.shape[1]
    count = heads * own.shape[1] // BLOCK
    return pl.pallas_call(
        functools.partial(forward_kernel, halo),
        out_shape=(
            jax.ShapeDtypeStruct((count, REACH * BLOCK, BLOCK), jnp.bfloat16),
            jax.ShapeDtypeStruct((heads, own.shape[1]), jnp.float32),
            jax.ShapeDtypeStruct((heads, own.shape[1]), jnp.float32),
            jax.ShapeDtypeStruct((count,), jnp.int32),
        ),
        in_specs=[SMEM] + [VMEM] * 5,
        out_specs=(HBM, VMEM, VMEM, SMEM),
        scratch_shapes=[
            pltpu.VMEM((key_tokens, depth), jnp.bfloat16),
            pltpu.VMEM((8, key_tokens), jnp.bfloat16),
            pltpu.VMEM((count, BLOCK), jnp.int32),
            pltpu.VMEM((count, REACH * BLOCK, BLOCK), jnp.bfloat16),
            pltpu.SemaphoreType.DMA((count,)),
        ],
        compiler_params=pltpu.CompilerParams(vmem_limit_bytes=24 << 20),
        cost_estimate=pl.CostEstimate(
            flops=4 * BLOCK * BLOCK * depth * count * REACH,
            bytes_accessed=16 << 20,
            transcendentals=BLOCK * BLOCK * count * REACH,
        ),
        name="attention_forward",
    )(where, message, own, other, seg, readout)


def attention_backward(halo, where, low, message, own, other, grad, readout, reward, flag, inverse, prob):
    heads, depth = message.shape[0], message.shape[2]
    key_tokens = own.shape[0] * own.shape[1]
    count = heads * own.shape[1] // BLOCK
    return pl.pallas_call(
        functools.partial(backward_kernel, halo),
        out_shape=(
            jax.ShapeDtypeStruct(grad.shape, jnp.bfloat16),
            jax.ShapeDtypeStruct(own.shape, jnp.bfloat16),
            jax.ShapeDtypeStruct(own.shape, jnp.bfloat16),
        ),
        in_specs=[SMEM, SMEM] + [VMEM] * 8 + [HBM],
        out_specs=(VMEM, VMEM, VMEM),
        scratch_shapes=[
            pltpu.VMEM((depth, key_tokens), jnp.bfloat16),
            pltpu.VMEM((key_tokens, depth), jnp.bfloat16),
            pltpu.VMEM(grad.shape, jnp.bfloat16),
            pltpu.VMEM(grad.shape, jnp.bfloat16),
            pltpu.VMEM(grad.shape, jnp.bfloat16),
            pltpu.VMEM((count, REACH * BLOCK, BLOCK), jnp.bfloat16),
            pltpu.VMEM((key_tokens, depth), jnp.float32),
            pltpu.VMEM((key_tokens, depth), jnp.float32),
            pltpu.SemaphoreType.DMA((count,)),
        ],
        compiler_params=pltpu.CompilerParams(vmem_limit_bytes=24 << 20),
        cost_estimate=pl.CostEstimate(
            flops=8 * BLOCK * BLOCK * depth * count * REACH,
            bytes_accessed=16 << 20,
            transcendentals=0,
        ),
        name="attention_backward",
    )(where, low, message, own, other, grad, readout, reward, flag, inverse, prob)


def local(queries, keys, values, grad_out, readout, segments, loss_mask, labels):
    rows, heads, depth = queries.shape
    devices = lax.axis_size("context")
    index = lax.axis_index("context")
    clusters = [list(range(s, s + heads)) for s in range(0, devices, heads)]
    many = len(clusters) > 1
    halo = WINDOW if many else 0
    pairs = [(i, i ^ 1) for i in range(devices)]
    bf16, f32 = jnp.bfloat16, jnp.float32

    def exchange(array):
        return lax.all_to_all(
            array, "context", 0, 0, tiled=True, axis_index_groups=clusters if many else None
        )

    def swap(array):
        return lax.ppermute(array, "context", pairs)

    pair = jnp.stack([keys, values], axis=2).reshape(rows, heads, depth)
    flags = jnp.stack([segments, loss_mask, labels]).astype(bf16)
    flags = jnp.pad(flags, ((0, AUX - 3), (0, 0)))
    message = jnp.concatenate(
        [
            jnp.transpose(queries, (1, 0, 2)),
            jnp.transpose(pair, (1, 0, 2)),
            jnp.broadcast_to(flags[None], (heads, AUX, depth)),
        ],
        axis=1,
    )
    message = exchange(message)
    later, message = lax.optimization_barrier((jnp.transpose(grad_out, (1, 0, 2)), message))
    grad = exchange(later)
    own = message[:, rows : 2 * rows]
    other = swap(own)
    flags = message[:, 2 * rows :]
    seg = flags[:, 0].astype(jnp.int32)
    flag = jnp.stack([flags[:, 1], flags[:, 2]]).astype(f32)
    if many:
        ahead = [(i, i + heads) for i in range(devices - heads)]
        blocks = halo // rows
        far = lax.ppermute((own[-blocks:], other[-blocks:], flags[-blocks:, 0]), "context", ahead)
        own = jnp.concatenate([far[0], own], axis=0)
        other = jnp.concatenate([far[1], other], axis=0)
        far_seg = jnp.where(index < heads, -1, far[2].astype(jnp.int32))
        seg = jnp.concatenate([far_seg, seg], axis=0)

    where = jnp.reshape(index, (1,)).astype(jnp.int32)
    prob, inverse, reward, low = attention_forward(halo, where, message, own, other, seg, readout)

    for step in (1, 2, 4, 8):
        reward = reward + lax.ppermute(reward, "context", [(i, i ^ step) for i in range(devices)])

    query_grad, keep, send = attention_backward(
        halo, where, low, message, own, other, grad, readout, reward, flag, inverse, prob
    )
    total = keep.astype(f32) + swap(send).astype(f32)
    if many:
        behind = [(i + heads, i) for i in range(devices - heads)]
        back = lax.ppermute(total[:blocks].astype(bf16), "context", behind)
        total = total[blocks:]
        total = total + jnp.pad(
            back.astype(f32), ((heads - blocks, 0), (0, 0), (0, 0))
        )
    home = exchange(jnp.concatenate([query_grad, total.astype(bf16)], axis=1))
    home = jnp.transpose(home, (1, 0, 2))
    return home[:rows], home[rows:, 0::2], home[rows:, 1::2]


def solution(mesh):
    sharded = P(("groups", "context"))
    return jax.shard_map(
        local,
        mesh=mesh,
        in_specs=(sharded,) * 4 + (P(),) + (sharded,) * 3,
        out_specs=(sharded,) * 3,
        check_vma=False,
    )
```

time: 122 us -> 117 us (0.959); the launches traced: 123 us -> 116 us
  Pallas kernels: 21.7 us -> 16.9 us
  local copies, waits for them, and re-layouts: 12.4 us -> 10.2 us
    pallas_call x2, Pallas kernels: 21.7 us -> 16.9 us  [the longest x1 9.64 us: attention_backward(): pl.pallas_call(functools.partial(backward_kernel, halo), out_shape=(jax.S...]
    unnamed x21 -> x17, local copies, waits for them, and re-layouts: 12 us -> 9.81 us
  transfers between devices with their start and end apart: 8 -> 8, of which waited for: 7 -> 7; matrix products, arithmetic and copies ran while one was open for 1% -> 1% of each run, Pallas kernels for 8% -> 6%
where the time goes in v2:
time: 117 us; the launch traced here: 116 us
  blocking collectives  31.3 us (27%)
  waiting for transfers between devices  30.4 us (26%)
  starting transfers between devices  23.3 us (20%)
  Pallas kernels  16.9 us (14%)
  local copies, waits for them, and re-layouts  10.2 us (9%)
  other arithmetic  3.11 us (3%)
    all_to_all x1, blocking collectives, exchange(): lax.all_to_all(array, 'context', 0, 0, tiled=True, axis_index_groups=clus...  31.3 us
    all_to_all x2, waiting for transfers between devices, exchange(): lax.all_to_all(array, 'context', 0, 0, tiled=True, axis_index_groups=clus...  22.8 us
    all_to_all x2, starting transfers between devices, exchange(): lax.all_to_all(array, 'context', 0, 0, tiled=True, axis_index_groups=clus...  14.2 us
    unnamed x17, local copies, waits for them, and re-layouts  9.81 us
    pallas_call x1, Pallas kernels, attention_backward(): pl.pallas_call(functools.partial(backward_kernel, halo), out_shape=(jax.S...  9.64 us
    pallas_call x1, Pallas kernels, attention_forward(): pl.pallas_call(functools.partial(forward_kernel, halo), out_shape=(jax.Sh...  7.27 us
    ppermute x4, starting transfers between devices, local(): lax.ppermute(reward, 'context', [(i, i ^ step) for i in range(devices)])  5.23 us
    ppermute x4, waiting for transfers between devices, local(): lax.ppermute(reward, 'context', [(i, i ^ step) for i in range(devices)])  4.34 us
  transfers between devices with their start and end apart: 8, of which 7 were waited for; matrix products, arithmetic and copies ran while one was open for 1% of the time, Pallas kernels for 6%

profile of v2, /device:TPU:1, one launch (start us, length us, event | category | flops | bytes accessed | tf_op | source)
XLA Modules:
  0.0 116.0 jit_solution(16804683770532786107)
XLA Ops:
  0.7 0.7 convert_bitcast_fusion.2
  1.3 1.2 %copy.33 = bf16[128,16,128]{2,0,1:T(8,128)(2,1)S(1)} copy(bf16[128,16,128]{2,1,0:T(8,128)(2,1)} %param.8) | data formatting | bytes 1048576 | tf_op args[0]
  2.5 1.1 pad_maximum_fusion.2
  3.6 0.1 copy.24
  3.8 1.1 pad_maximum_fusion
  4.9 7.3 %all-to-all-start = ((bf16[16,264,128]{2,1,0:T(8,128)(2,1)}), bf16[16,264,128]{2,1,0:T(8,128)(2,1)S(1)}, u32[]{:S(2)}, u32[]{:S(2)}) async-start(bf16[16,264,128]{2,1,0:T(8,128)(2,1)} %pad_maximum_fusion), calls=%async_computation | async-start | bytes 2162688 | tf_op jit(solution)/shard_map/all_to_all | solution.py:310
  12.2 0.9 copy.34
  13.1 22.8 %all-to-all-done.message_ref = bf16[16,264,128]{2,1,0:T(8,128)(2,1)S(1)} async-done(((bf16[16,264,128]{2,1,0:T(8,128)(2,1)}), bf16[16,264,128]{2,1,0:T(8,128)(2,1)S(1)}, u32[]{:S(2)}, u32[]{:S(2)}) %all-to-all-start) | async-done | bytes 1081376 | tf_op jit(solution)/shard_map/all_to_all | solution.py:310
  36.0 6.9 %all-to-all-start.1 = ((bf16[16,128,128]{2,1,0:T(8,128)(2,1)}), bf16[16,128,128]{2,1,0:T(8,128)(2,1)S(1)}, u32[]{:S(2)}, u32[]{:S(2)}) async-start(bf16[16,128,128]{2,1,0:T(8,128)(2,1)} %bitcast.27), calls=%async_computation.1 | async-start | bytes 1048576 | tf_op jit(solution)/shard_map/all_to_all | solution.py:310
  42.9 0.2 collective-permute-start
  43.1 0.1 copy.25
  43.2 1.7 %collective-permute-done.other_ref = bf16[16,128,128]{2,1,0:T(8,128)(2,1)S(1)} collective-permute-done((bf16[16,128,128]{2,1,0:T(8,128)(2,1)S(1)}, bf16[16,128,128]{2,1,0:T(8,128)(2,1)S(1)}, u32[]{:S(2)}, u32[]{:S(2)}) %collective-permute-start) | collective-permute-done | bytes 524320 | tf_op jit(solution)/shard_map/ppermute | solution.py:315
  44.9 7.3 %attention_forward.1 = (bf16[8,1280,256]{2,1,0:T(8,128)(2,1)S(1)}, f32[16,128]{1,0:T(8,128)S(1)}, f32[16,128]{1,0:T(8,128)S(1)}, s32[8]{0:T(128)S(1)}) custom-call(s32[1]{0:T(128)} %bitcast.index_ref, bf16[16,264,128]{2,1,0:T(8,128)(2,1)S(1)} %all-to-all-done.message_ref, bf16[16,128,128]{2,1,0:T(8,128)(2,1)S(1)} %slice.25.own_ref, ...), custom_call_target="tpu_custom_call" | custom-call | flops 1342177280 | bytes 16777216 | tf_op jit(solution)/shard_map/attention_forward/pallas_call | solution.py:238
  52.2 2.3 %copy-done.1 = bf16[8,1280,256]{2,1,0:T(8,128)(2,1)} copy-done((bf16[8,1280,256]{2,1,0:T(8,128)(2,1)}, bf16[8,1280,256]{2,1,0:T(8,128)(2,1)S(1)}, u32[]{:S(2)}) %copy-start.1) | copy-done | bytes 5242904
  54.5 0.1 collective-permute-start.1
  54.6 1.0 collective-permute-done.1
  55.7 1.4 %collective-permute-start.2 = (f32[16,128]{1,0:T(8,128)S(1)}, f32[16,128]{1,0:T(8,128)S(1)}, u32[]{:S(2)}, u32[]{:S(2)}) collective-permute-start(f32[16,128]{1,0:T(8,128)S(1)} %add.17), channel_id=1, source_target_pairs={{0,2},{1,3},{2,0},{3,1},{4,6},{5,7},{6,4},{7,5},{8,10},{9,11},{10,... | collective-permute-start | bytes 24584 | tf_op jit(solution)/shard_map/ppermute | solution.py:349
  57.1 1.1 collective-permute-done.2
  58.2 1.4 %collective-permute-start.3 = (f32[16,128]{1,0:T(8,128)S(1)}, f32[16,128]{1,0:T(8,128)S(1)}, u32[]{:S(2)}, u32[]{:S(2)}) collective-permute-start(f32[16,128]{1,0:T(8,128)S(1)} %add.18), channel_id=1, source_target_pairs={{0,4},{1,5},{2,6},{3,7},{4,0},{5,1},{6,2},{7,3},{8,12},{9,13},{10,... | collective-permute-start | bytes 24584 | tf_op jit(solution)/shard_map/ppermute | solution.py:349
  59.6 1.1 collective-permute-done.3
  60.7 2.3 %collective-permute-start.4 = (f32[16,128]{1,0:T(8,128)S(1)}, f32[16,128]{1,0:T(8,128)S(1)}, u32[]{:S(2)}, u32[]{:S(2)}) collective-permute-start(f32[16,128]{1,0:T(8,128)S(1)} %add.19), channel_id=1, source_target_pairs={{0,8},{1,9},{2,10},{3,11},{4,12},{5,13},{6,14},{7,15},{8,0},{9,1},... | collective-permute-start | bytes 24584 | tf_op jit(solution)/shard_map/ppermute | solution.py:349
  63.0 1.1 collective-permute-done.4
  64.1 2.5 %copy-done.2 = bf16[8,1280,256]{2,1,0:T(8,128)(2,1)S(1)} copy-done((bf16[8,1280,256]{2,1,0:T(8,128)(2,1)S(1)}, bf16[8,1280,256]{2,1,0:T(8,128)(2,1)}, u32[]{:S(2)}) %copy-start.2) | copy-done | bytes 5242904
  66.6 9.6 %attention_backward.1 = (bf16[16,128,128]{2,1,0:T(8,128)(2,1)S(1)}, bf16[16,128,128]{2,1,0:T(8,128)(2,1)S(1)}, bf16[16,128,128]{2,1,0:T(8,128)(2,1)S(1)}) custom-call(s32[1]{0:T(128)} %bitcast.index_ref, s32[8]{0:T(128)S(1)} %get-tuple-element.13.low_ref, bf16[16,264,128]{2,1,0:T(8,128)(2,1)S(1)} %all-to-all-done.message_ref, ...), custom_call_target="tpu_custom_call" | custom-call | flops 2684354560 | bytes 16777216 | tf_op jit(solution)/shard_map/attention_backward/pallas_call | solution.py:269
  76.2 3.7 %collective-permute-start.5 = (bf16[16,128,128]{2,1,0:T(8,128)(2,1)S(1)}, bf16[16,128,128]{2,1,0:T(8,128)(2,1)S(1)}, u32[]{:S(2)}, u32[]{:S(2)}) collective-permute-start(bf16[16,128,128]{2,1,0:T(8,128)(2,1)S(1)} %get-tuple-element.20), channel_id=1, source_target_pairs={{0,1},{1,0},{2,3},{3,2},{4,5},{5,4},{6,7},{7,6},{8,9},{9,8},{10,11... | collective-permute-start | bytes 1572872 | tf_op jit(solution)/shard_map/ppermute | solution.py:315
  79.9 1.5 %collective-permute-done.5 = bf16[16,128,128]{2,1,0:T(8,128)(2,1)S(1)} collective-permute-done((bf16[16,128,128]{2,1,0:T(8,128)(2,1)S(1)}, bf16[16,128,128]{2,1,0:T(8,128)(2,1)S(1)}, u32[]{:S(2)}, u32[]{:S(2)}) %collective-permute-start.5) | collective-permute-done | bytes 524320 | tf_op jit(solution)/shard_map/ppermute | solution.py:315
  81.4 0.1 add_convert_fusion
  81.6 0.1 pad_maximum_fusion.1
  81.7 31.3 %all_to_all.15 = bf16[16,256,128]{2,1,0:T(8,128)(2,1)S(1)} all-to-all(bf16[16,256,128]{2,1,0:T(8,128)(2,1)S(1)} %pad_maximum_fusion.1), channel_id=1, replica_groups=mesh['groups'=2,'context'=16] {'context'}, dimensions={0} | all-to-all | bytes 2097152 | tf_op jit(solution)/shard_map/all_to_all | solution.py:310
  113.1 0.9 copy.30
  114.0 1.1 copy.28
  115.1 0.9 copy.29
  (23 shorter events, 0.2 us)
Async XLA Ops:
  0.6 3.1 %copy-start.4 = (s32[128]{0:T(128)S(1)}, s32[128]{0:T(128)}, u32[]{:S(2)}) copy-start(s32[128]{0:T(128)} %param.15) | copy-start | bytes 1540
  0.6 3.1 %copy-start.5 = (s32[128]{0:T(128)S(1)}, s32[128]{0:T(128)}, u32[]{:S(2)}) copy-start(s32[128]{0:T(128)} %param.14) | copy-start | bytes 1540
  3.8 8.5 %copy-start.3 = (bf16[128,16,128]{2,1,0:T(8,128)(2,1)S(1)}, bf16[128,16,128]{2,1,0:T(8,128)(2,1)}, u32[]{:S(2)}) copy-start(bf16[128,16,128]{2,1,0:T(8,128)(2,1)} %param.11) | copy-start | bytes 1572868
  4.9 31.1 %all-to-all-start = ((bf16[16,264,128]{2,1,0:T(8,128)(2,1)}), bf16[16,264,128]{2,1,0:T(8,128)(2,1)S(1)}, u32[]{:S(2)}, u32[]{:S(2)}) async-start(bf16[16,264,128]{2,1,0:T(8,128)(2,1)} %pad_maximum_fusion), calls=%async_computation | async-start | bytes 2162688 | tf_op jit(solution)/shard_map/all_to_all | solution.py:310
  36.0 8.9 %copy-start = (f32[16,128]{1,0:T(8,128)S(1)}, f32[16,128]{1,0:T(8,128)}, u32[]{:S(2)}) copy-start(f32[16,128]{1,0:T(8,128)} %readout_ref.3) | copy-start | bytes 24580
  36.0 28.1 %all-to-all-start.1 = ((bf16[16,128,128]{2,1,0:T(8,128)(2,1)}), bf16[16,128,128]{2,1,0:T(8,128)(2,1)S(1)}, u32[]{:S(2)}, u32[]{:S(2)}) async-start(bf16[16,128,128]{2,1,0:T(8,128)(2,1)} %bitcast.27), calls=%async_computation.1 | async-start | bytes 1048576 | tf_op jit(solution)/shard_map/all_to_all | solution.py:310
  42.9 2.0 %collective-permute-start = (bf16[16,128,128]{2,1,0:T(8,128)(2,1)S(1)}, bf16[16,128,128]{2,1,0:T(8,128)(2,1)S(1)}, u32[]{:S(2)}, u32[]{:S(2)}) collective-permute-start(bf16[16,128,128]{2,1,0:T(8,128)(2,1)S(1)} %slice.25.own_ref), channel_id=1, source_target_pairs={{0,1},{1,0},{2,3},{3,2},{4,5},{5,4},{6,7},{7,6},{8,9},{9,8},{10,11... | collective-permute-start | bytes 1572872 | tf_op jit(solution)/shard_map/ppermute | solution.py:315
  52.2 2.3 %copy-start.1 = (bf16[8,1280,256]{2,1,0:T(8,128)(2,1)}, bf16[8,1280,256]{2,1,0:T(8,128)(2,1)S(1)}, u32[]{:S(2)}) copy-start(bf16[8,1280,256]{2,1,0:T(8,128)(2,1)S(1)} %get-tuple-element.17.prob_ref) | copy-start | bytes 15728644
  54.5 1.2 %collective-permute-start.1 = (f32[16,128]{1,0:T(8,128)S(1)}, f32[16,128]{1,0:T(8,128)S(1)}, u32[]{:S(2)}, u32[]{:S(2)}) collective-permute-start(f32[16,128]{1,0:T(8,128)S(1)} %get-tuple-element.15), channel_id=1, source_target_pairs={{0,1},{1,0},{2,3},{3,2},{4,5},{5,4},{6,7},{7,6},{8,9},{9,8},{10,11... | collective-permute-start | bytes 24584 | tf_op jit(solution)/shard_map/ppermute | solution.py:349
  55.7 2.5 %collective-permute-start.2 = (f32[16,128]{1,0:T(8,128)S(1)}, f32[16,128]{1,0:T(8,128)S(1)}, u32[]{:S(2)}, u32[]{:S(2)}) collective-permute-start(f32[16,128]{1,0:T(8,128)S(1)} %add.17), channel_id=1, source_target_pairs={{0,2},{1,3},{2,0},{3,1},{4,6},{5,7},{6,4},{7,5},{8,10},{9,11},{10,... | collective-permute-start | bytes 24584 | tf_op jit(solution)/shard_map/ppermute | solution.py:349
  58.2 2.5 %collective-permute-start.3 = (f32[16,128]{1,0:T(8,128)S(1)}, f32[16,128]{1,0:T(8,128)S(1)}, u32[]{:S(2)}, u32[]{:S(2)}) collective-permute-start(f32[16,128]{1,0:T(8,128)S(1)} %add.18), channel_id=1, source_target_pairs={{0,4},{1,5},{2,6},{3,7},{4,0},{5,1},{6,2},{7,3},{8,12},{9,13},{10,... | collective-permute-start | bytes 24584 | tf_op jit(solution)/shard_map/ppermute | solution.py:349
  60.7 3.4 %collective-permute-start.4 = (f32[16,128]{1,0:T(8,128)S(1)}, f32[16,128]{1,0:T(8,128)S(1)}, u32[]{:S(2)}, u32[]{:S(2)}) collective-permute-start(f32[16,128]{1,0:T(8,128)S(1)} %add.19), channel_id=1, source_target_pairs={{0,8},{1,9},{2,10},{3,11},{4,12},{5,13},{6,14},{7,15},{8,0},{9,1},... | collective-permute-start | bytes 24584 | tf_op jit(solution)/shard_map/ppermute | solution.py:349
  64.1 2.5 %copy-start.2 = (bf16[8,1280,256]{2,1,0:T(8,128)(2,1)S(1)}, bf16[8,1280,256]{2,1,0:T(8,128)(2,1)}, u32[]{:S(2)}) copy-start(bf16[8,1280,256]{2,1,0:T(8,128)(2,1)} %copy-done.1) | copy-start | bytes 15728644
  76.2 5.2 %collective-permute-start.5 = (bf16[16,128,128]{2,1,0:T(8,128)(2,1)S(1)}, bf16[16,128,128]{2,1,0:T(8,128)(2,1)S(1)}, u32[]{:S(2)}, u32[]{:S(2)}) collective-permute-start(bf16[16,128,128]{2,1,0:T(8,128)(2,1)S(1)} %get-tuple-element.20), channel_id=1, source_target_pairs={{0,1},{1,0},{2,3},{3,2},{4,5},{5,4},{6,7},{7,6},{8,9},{9,8},{10,11... | collective-permute-start | bytes 1572872 | tf_op jit(solution)/shard_map/ppermute | solution.py:315

commit v3 on v2

--- a/solution.py
+++ b/solution.py
@@ -17,7 +17,6 @@
 REACH = WINDOW // BLOCK + 1
 VMEM = pl.BlockSpec(memory_space=pltpu.VMEM)
 SMEM = pl.BlockSpec(memory_space=pltpu.SMEM)
-HBM = pl.BlockSpec(memory_space=pltpu.HBM)
 NT = (((1,), (1,)), ((), ()))
 NN = (((1,), (0,)), ((), ()))
 
@@ -26,15 +25,25 @@
     return lax.dot_general(a, b, dims, preferred_element_type=jnp.float32)
 
 
-def starts_of(seg_all, halo):
-    return [jnp.sum(jnp.where(seg_all < s, 1, 0)) for s in range(0 if halo else 1, 4)]
+def starts_of(seg_all):
+    return [jnp.sum(jnp.where(seg_all < s, 1, 0)) for s in range(4)]
 
 
 def begin_of(starts, token):
-    begin = jnp.zeros_like(token)
+    begin = token - (WINDOW - 1)
     for start in starts:
         begin = jnp.maximum(begin, jnp.where(start <= token, start, 0))
-    return jnp.maximum(begin, token - (WINDOW - 1))
+    return begin
+
+
+def tokens_of(tokens, halo):
+    shape = (tokens // BLOCK, BLOCK)
+    row = lax.broadcasted_iota(jnp.int32, shape, 0)
+    return halo + row * BLOCK + lax.broadcasted_iota(jnp.int32, shape, 1)
+
+
+def rows_of(block):
+    return pl.ds(pl.multiple_of(block * BLOCK, BLOCK), BLOCK)
 
 
 def by_reach(count, body):
@@ -42,14 +51,10 @@
         pl.when(count == n)(functools.partial(body, n))
 
 
-def chunk(n):
-    return pl.ds(n * BLOCK, BLOCK)
-
-
 def forward_kernel(
     halo, index_ref, message_ref, own_ref, other_ref, seg_ref, readout_ref,
-    prob_ref, inverse_ref, reward_ref, low_ref,
-    key_s, side_s, bound_s, prob_s, sems,
+    total_ref, reward_ref, starts_ref,
+    key_s, side_s, bound_s,
 ):
     heads, tokens = message_ref.shape[0], message_ref.shape[0] * 128
     key_blocks = own_ref.shape[0]
@@ -84,64 +89,49 @@
     def _():
         place(other_ref, own_ref)
 
-    starts = starts_of(seg_ref[...], halo)
-    token = halo + lax.broadcasted_iota(jnp.int32, (tokens // BLOCK, BLOCK), 0) * BLOCK
-    token = token + lax.broadcasted_iota(jnp.int32, (tokens // BLOCK, BLOCK), 1)
-    bound_s[...] = begin_of(starts, token)
+    starts = starts_of(seg_ref[...])
+    for n, start in enumerate(starts):
+        starts_ref[n] = start
+    bound_s[...] = begin_of(starts, tokens_of(tokens, halo))
     key_iota = lax.broadcasted_iota(jnp.int32, (BLOCK, BLOCK), 0)
     query_iota = lax.broadcasted_iota(jnp.int32, (BLOCK, BLOCK), 1)
 
-    def copy(i):
-        return pltpu.make_async_copy(prob_s.at[i], prob_ref.at[i], sems.at[i])
-
     def query_block(i, _):
         first = lax.div(begin_of(starts, halo + i * BLOCK), BLOCK)
-        low_ref[i] = first
 
         def body(n):
             query = message_ref[pl.ds(2 * i, 2), 0:128, :].reshape(BLOCK, 128)
             bound = bound_s[pl.ds(i, 1), :] - first * BLOCK
             scores, tops = [], []
             for j in range(n):
-                rows = pl.ds(pl.multiple_of((first + j) * BLOCK, BLOCK), BLOCK)
+                score = dot(key_s[rows_of(first + j), :], query, NT)
                 valid = key_iota >= bound - j * BLOCK
                 if j == n - 1:
                     valid = valid & (key_iota <= query_iota)
-                score = jnp.where(valid, dot(key_s[rows, :], query, NT), NEGATIVE)
+                score = jnp.where(valid, score, NEGATIVE)
                 scores.append(score)
                 tops.append(jnp.max(score.reshape(BLOCK // 8, 8, BLOCK), axis=0))
             top = jnp.max(functools.reduce(jnp.maximum, tops), axis=0, keepdims=True)
             sums = jnp.zeros((8, BLOCK), jnp.float32)
             for j in range(n):
                 prob = jnp.exp2((scores[j] - top) * (SCALE * LOG2E)).astype(low_bits)
-                prob_s[i, chunk(j), :] = prob
-                columns = pl.ds(pl.multiple_of((first + j) * BLOCK, BLOCK), BLOCK)
-                sums = sums + dot(side_s[:, columns], prob, NN)
-            inverse = 1.0 / sums[2:3]
-            reward = (sums[0:1] + sums[1:2]) * inverse
-            for half in range(2):
-                lanes = slice(half * 128, (half + 1) * 128)
-                inverse_ref[pl.ds(2 * i + half, 1), :] = inverse[:, lanes]
-                reward_ref[pl.ds(2 * i + half, 1), :] = reward[:, lanes]
+                sums = sums + dot(side_s[:, rows_of(first + j)], prob, NN)
+            reward = (sums[0:1] + sums[1:2]) / sums[2:3]
+            total_ref[pl.ds(i, 1), :] = top * (SCALE * LOG2E) + jnp.log2(sums[2:3])
+            reward_ref[pl.ds(2 * i, 1), :] = reward[:, :128]
+            reward_ref[pl.ds(2 * i + 1, 1), :] = reward[:, 128:]
 
         by_reach(i + shift + 1 - first, body)
-        copy(i).start()
         return 0
 
     lax.fori_loop(0, tokens // BLOCK, query_block, 0)
 
-    def finish(i, _):
-        copy(i).wait()
-        return 0
-
-    lax.fori_loop(0, tokens // BLOCK, finish, 0)
-
 
 def backward_kernel(
-    halo, index_ref, low_ref, message_ref, own_ref, other_ref, grad_ref, readout_ref, reward_ref,
-    flag_ref, inverse_ref, prob_ref,
+    halo, index_ref, starts_ref, message_ref, own_ref, other_ref, grad_ref, readout_ref, reward_ref,
+    flag_ref, total_ref,
     query_ref, keep_ref, send_ref,
-    key_s, value_s, grad_s, scaled_s, query_s, prob_s, key_grad_s, value_grad_s, sems,
+    key_s, turned_s, value_s, grad_s, bound_s, key_grad_s, value_grad_s,
 ):
     heads, tokens = message_ref.shape[0], message_ref.shape[0] * 128
     key_blocks = own_ref.shape[0]
@@ -150,15 +140,10 @@
     head = lax.rem(index, heads)
     even = lax.rem(index, 2) == 0
 
-    def copy(i):
-        return pltpu.make_async_copy(prob_ref.at[i], prob_s.at[i], sems.at[i])
-
-    for i in range(tokens // BLOCK):
-        copy(i).start()
-
     def place(keys, values):
         for s in range(key_blocks):
-            key_s[:, s * 128 : (s + 1) * 128] = keys[s].T
+            key_s[s * 128 : (s + 1) * 128, :] = keys[s]
+            turned_s[:, s * 128 : (s + 1) * 128] = keys[s].T
             value_s[s * 128 : (s + 1) * 128, :] = values[s]
 
     @pl.when(even)
@@ -171,47 +156,58 @@
 
     live = flag_ref[0]
     probe = live * (jax.nn.sigmoid(reward_ref[...]) - flag_ref[1])
-    live_t, probe_t, inverse_t = live.T, probe.T, inverse_ref[...].T
+    live_t, probe_t = live.T, probe.T
     weights = readout_ref[pl.ds(head, 1), :]
     for s in range(heads):
         grad = live_t[:, s : s + 1] * grad_ref[s].astype(jnp.float32)
-        grad = (grad + probe_t[:, s : s + 1] * weights).astype(jnp.bfloat16)
-        inverse = inverse_t[:, s : s + 1]
-        grad_s[s] = grad
-        scaled_s[s] = (grad.astype(jnp.float32) * inverse).astype(jnp.bfloat16)
-        query_s[s] = (message_ref[s, 0:128, :].astype(jnp.float32) * inverse).astype(jnp.bfloat16)
-
-    key_grad_s[...] = jnp.zeros_like(key_grad_s)
-    value_grad_s[...] = jnp.zeros_like(value_grad_s)
+        grad_s[s] = (grad + probe_t[:, s : s + 1] * weights).astype(jnp.bfloat16)
+
+    starts = [starts_ref[n] for n in range(4)]
+    bound_s[...] = begin_of(starts, tokens_of(tokens, halo))
+    key_iota = lax.broadcasted_iota(jnp.int32, (BLOCK, BLOCK), 0)
+    query_iota = lax.broadcasted_iota(jnp.int32, (BLOCK, BLOCK), 1)
+    if halo:
+        key_grad_s[:halo, :] = jnp.zeros((halo, 128), jnp.float32)
+        value_grad_s[:halo, :] = jnp.zeros((halo, 128), jnp.float32)
 
     def query_block(i, _):
-        first = low_ref[i]
-        copy(i).wait()
+        first = lax.div(begin_of(starts, halo + i * BLOCK), BLOCK)
 
         def body(n):
             grad = grad_s[pl.ds(2 * i, 2)].reshape(BLOCK, 128)
-            scaled = scaled_s[pl.ds(2 * i, 2)].reshape(BLOCK, 128)
-            query = query_s[pl.ds(2 * i, 2)].reshape(BLOCK, 128)
-            inverse = jnp.concatenate(
-                [inverse_ref[pl.ds(2 * i, 1), :], inverse_ref[pl.ds(2 * i + 1, 1), :]], axis=1
-            )
-            rows = [pl.ds(pl.multiple_of((first + j) * BLOCK, BLOCK), BLOCK) for j in range(n)]
-            grad_probs = []
+            query = message_ref[pl.ds(2 * i, 2), 0:128, :].reshape(BLOCK, 128)
+            bound = bound_s[pl.ds(i, 1), :] - first * BLOCK
+            total = total_ref[pl.ds(i, 1), :]
+            probs, grad_probs = [], []
             delta = jnp.zeros((8, BLOCK), jnp.float32)
             for j in range(n):
-                grad_prob = dot(value_s[rows[j], :], grad, NT)
+                rows = rows_of(first + j)
+                score = dot(key_s[rows, :], query, NT) * (SCALE * LOG2E) - total
+                valid = key_iota >= bound - j * BLOCK
+                if j == n - 1:
+                    valid = valid & (key_iota <= query_iota)
+                prob = jnp.exp2(jnp.where(valid, score, NEGATIVE))
+                grad_prob = dot(value_s[rows, :], grad, NT)
+                delta = delta + jnp.sum((prob * grad_prob).reshape(BLOCK // 8, 8, BLOCK), axis=0)
+                value_grad = dot(prob.astype(jnp.bfloat16), grad, NN)
+                if j == n - 1:
+                    value_grad_s[rows, :] = value_grad
+                else:
+                    value_grad_s[rows, :] += value_grad
+                probs.append(prob)
                 grad_probs.append(grad_prob)
-                prob = prob_s[i, chunk(j), :].astype(jnp.float32)
-                delta = delta + jnp.sum((prob * grad_prob).reshape(BLOCK // 8, 8, BLOCK), axis=0)
-                value_grad_s[rows[j], :] += dot(prob_s[i, chunk(j), :], scaled, NN)
-            delta = jnp.sum(delta, axis=0, keepdims=True) * inverse
+            delta = jnp.sum(delta, axis=0, keepdims=True)
             query_grad = jnp.zeros((128, BLOCK), jnp.float32)
             for j in range(n):
-                prob = prob_s[i, chunk(j), :].astype(jnp.float32)
-                grad_score = (prob * (grad_probs[j] - delta)).astype(jnp.bfloat16)
-                key_grad_s[rows[j], :] += dot(grad_score, query, NN)
-                query_grad = query_grad + dot(key_s[:, rows[j]], grad_score, NN)
-            query_grad = (query_grad * (inverse * SCALE)).T.astype(jnp.bfloat16)
+                rows = rows_of(first + j)
+                grad_score = (probs[j] * (grad_probs[j] - delta)).astype(jnp.bfloat16)
+                key_grad = dot(grad_score, query, NN)
+                if j == n - 1:
+                    key_grad_s[rows, :] = key_grad
+                else:
+                    key_grad_s[rows, :] += key_grad
+                query_grad = query_grad + dot(turned_s[:, rows], grad_score, NN)
+            query_grad = (query_grad * SCALE).T.astype(jnp.bfloat16)
             query_ref[pl.ds(2 * i, 2)] = query_grad.reshape(2, 128, 128)
 
         by_reach(i + shift + 1 - first, body)
@@ -238,19 +234,16 @@
     return pl.pallas_call(
         functools.partial(forward_kernel, halo),
         out_shape=(
-            jax.ShapeDtypeStruct((count, REACH * BLOCK, BLOCK), jnp.bfloat16),
+            jax.ShapeDtypeStruct((count, BLOCK), jnp.float32),
             jax.ShapeDtypeStruct((heads, own.shape[1]), jnp.float32),
-            jax.ShapeDtypeStruct((heads, own.shape[1]), jnp.float32),
-            jax.ShapeDtypeStruct((count,), jnp.int32),
+            jax.ShapeDtypeStruct((4,), jnp.int32),
         ),
         in_specs=[SMEM] + [VMEM] * 5,
-        out_specs=(HBM, VMEM, VMEM, SMEM),
+        out_specs=(VMEM, VMEM, SMEM),
         scratch_shapes=[
             pltpu.VMEM((key_tokens, depth), jnp.bfloat16),
             pltpu.VMEM((8, key_tokens), jnp.bfloat16),
             pltpu.VMEM((count, BLOCK), jnp.int32),
-            pltpu.VMEM((count, REACH * BLOCK, BLOCK), jnp.bfloat16),
-            pltpu.SemaphoreType.DMA((count,)),
         ],
         compiler_params=pltpu.CompilerParams(vmem_limit_bytes=24 << 20),
         cost_estimate=pl.CostEstimate(
@@ -262,7 +255,7 @@
     )(where, message, own, other, seg, readout)
 
 
-def attention_backward(halo, where, low, message, own, other, grad, readout, reward, flag, inverse, prob):
+def attention_backward(halo, where, starts, message, own, other, grad, readout, reward, flag, total):
     heads, depth = message.shape[0], message.shape[2]
     key_tokens = own.shape[0] * own.shape[1]
     count = heads * own.shape[1] // BLOCK
@@ -273,18 +266,16 @@
             jax.ShapeDtypeStruct(own.shape, jnp.bfloat16),
             jax.ShapeDtypeStruct(own.shape, jnp.bfloat16),
         ),
-        in_specs=[SMEM, SMEM] + [VMEM] * 8 + [HBM],
+        in_specs=[SMEM, SMEM] + [VMEM] * 8,
         out_specs=(VMEM, VMEM, VMEM),
         scratch_shapes=[
+            pltpu.VMEM((key_tokens, depth), jnp.bfloat16),
             pltpu.VMEM((depth, key_tokens), jnp.bfloat16),
             pltpu.VMEM((key_tokens, depth), jnp.bfloat16),
             pltpu.VMEM(grad.shape, jnp.bfloat16),
-            pltpu.VMEM(grad.shape, jnp.bfloat16),
-            pltpu.VMEM(grad.shape, jnp.bfloat16),
-            pltpu.VMEM((count, REACH * BLOCK, BLOCK), jnp.bfloat16),
+            pltpu.VMEM((count, BLOCK), jnp.int32),
             pltpu.VMEM((key_tokens, depth), jnp.float32),
             pltpu.VMEM((key_tokens, depth), jnp.float32),
-            pltpu.SemaphoreType.DMA((count,)),
         ],
         compiler_params=pltpu.CompilerParams(vmem_limit_bytes=24 << 20),
         cost_estimate=pl.CostEstimate(
@@ -293,7 +284,7 @@
             transcendentals=0,
         ),
         name="attention_backward",
-    )(where, low, message, own, other, grad, readout, reward, flag, inverse, prob)
+    )(where, starts, message, own, other, grad, readout, reward, flag, total)
 
 
 def local(queries, keys, values, grad_out, readout, segments, loss_mask, labels):
@@ -343,13 +334,13 @@
         seg = jnp.concatenate([far_seg, seg], axis=0)
 
     where = jnp.reshape(index, (1,)).astype(jnp.int32)
-    prob, inverse, reward, low = attention_forward(halo, where, message, own, other, seg, readout)
+    total, reward, starts = attention_forward(halo, where, message, own, other, seg, readout)
 
     for step in (1, 2, 4, 8):
         reward = reward + lax.ppermute(reward, "context", [(i, i ^ step) for i in range(devices)])
 
     query_grad, keep, send = attention_backward(
-        halo, where, low, message, own, other, grad, readout, reward, flag, inverse, prob
+        halo, where, starts, message, own, other, grad, readout, reward, flag, total
     )
     total = keep.astype(f32) + swap(send).astype(f32)
     if many:

time: 117 us -> 109 us (0.932)
  local copies, waits for them, and re-layouts: 10.2 us -> 5.86 us
  Pallas kernels: 16.9 us -> 15.2 us
    unnamed x17, local copies, waits for them, and re-layouts: 9.81 us -> 5.49 us
    pallas_call x1, Pallas kernels: 7.27 us -> 5.66 us  [attention_forward(): pl.pallas_call(functools.partial(forward_kernel, halo), out_shape=(jax.Sh...]
  transfers between devices with their start and end apart: 8 -> 8, of which waited for: 7 -> 7; matrix products, arithmetic and copies ran while one was open for 1% -> 1% of each run, Pallas kernels for 6% -> 5%
where the time goes in v3:
time: 109 us
  blocking collectives  31.3 us (29%)
  waiting for transfers between devices  31.2 us (29%)
  starting transfers between devices  22.5 us (21%)
  Pallas kernels  15.2 us (14%)
  local copies, waits for them, and re-layouts  5.86 us (5%)
  other arithmetic  2.13 us (2%)
    all_to_all x1, blocking collectives, exchange(): lax.all_to_all(array, 'context', 0, 0, tiled=True, axis_index_groups=clus...  31.3 us
    all_to_all x2, waiting for transfers between devices, exchange(): lax.all_to_all(array, 'context', 0, 0, tiled=True, axis_index_groups=clus...  22.8 us
    all_to_all x2, starting transfers between devices, exchange(): lax.all_to_all(array, 'context', 0, 0, tiled=True, axis_index_groups=clus...  14.2 us
    pallas_call x1, Pallas kernels, attention_backward(): pl.pallas_call(functools.partial(backward_kernel, halo), out_shape=(jax.S...  9.5 us
    pallas_call x1, Pallas kernels, attention_forward(): pl.pallas_call(functools.partial(forward_kernel, halo), out_shape=(jax.Sh...  5.66 us
    unnamed x17, local copies, waits for them, and re-layouts  5.49 us
    ppermute x4, waiting for transfers between devices, local(): lax.ppermute(reward, 'context', [(i, i ^ step) for i in range(devices)])  5.2 us
    ppermute x4, starting transfers between devices, local(): lax.ppermute(reward, 'context', [(i, i ^ step) for i in range(devices)])  4.75 us
  transfers between devices with their start and end apart: 8, of which 7 were waited for; matrix products, arithmetic and copies ran while one was open for 1% of the time, Pallas kernels for 5%

profile of v3, /device:TPU:1, one launch (start us, length us, event | category | flops | bytes accessed | tf_op | source)
XLA Modules:
  0.0 109.0 jit_solution(589700930855530970)
XLA Ops:
  0.7 0.7 convert_bitcast_fusion.2
  1.4 1.2 %copy.33 = bf16[128,16,128]{2,0,1:T(8,128)(2,1)S(1)} copy(bf16[128,16,128]{2,1,0:T(8,128)(2,1)} %param.8) | data formatting | bytes 1048576 | tf_op args[0]
  2.6 0.1 pad_maximum_fusion.2
  2.6 0.1 copy.24
  2.8 0.5 copy-done.4
  3.2 0.0 copy-done.5
  3.3 1.1 pad_maximum_fusion
  4.3 7.5 %all-to-all-start = ((bf16[16,264,128]{2,1,0:T(8,128)(2,1)}), bf16[16,264,128]{2,1,0:T(8,128)(2,1)S(1)}, u32[]{:S(2)}, u32[]{:S(2)}) async-start(bf16[16,264,128]{2,1,0:T(8,128)(2,1)} %pad_maximum_fusion), calls=%async_computation | async-start | bytes 2162688 | tf_op jit(solution)/shard_map/all_to_all | solution.py:301
  11.8 0.9 copy.34
  12.8 22.8 %all-to-all-done.message_ref = bf16[16,264,128]{2,1,0:T(8,128)(2,1)S(1)} async-done(((bf16[16,264,128]{2,1,0:T(8,128)(2,1)}), bf16[16,264,128]{2,1,0:T(8,128)(2,1)S(1)}, u32[]{:S(2)}, u32[]{:S(2)}) %all-to-all-start) | async-done | bytes 1081376 | tf_op jit(solution)/shard_map/all_to_all | solution.py:301
  35.6 6.7 %all-to-all-start.1 = ((bf16[16,128,128]{2,1,0:T(8,128)(2,1)}), bf16[16,128,128]{2,1,0:T(8,128)(2,1)S(1)}, u32[]{:S(2)}, u32[]{:S(2)}) async-start(bf16[16,128,128]{2,1,0:T(8,128)(2,1)} %bitcast.27), calls=%async_computation.1 | async-start | bytes 1048576 | tf_op jit(solution)/shard_map/all_to_all | solution.py:301
  42.4 0.2 collective-permute-start
  42.6 0.1 copy.25
  42.7 1.6 %collective-permute-done.other_ref = bf16[16,128,128]{2,1,0:T(8,128)(2,1)S(1)} collective-permute-done((bf16[16,128,128]{2,1,0:T(8,128)(2,1)S(1)}, bf16[16,128,128]{2,1,0:T(8,128)(2,1)S(1)}, u32[]{:S(2)}, u32[]{:S(2)}) %collective-permute-start) | collective-permute-done | bytes 524320 | tf_op jit(solution)/shard_map/ppermute | solution.py:306
  44.4 5.7 %attention_forward.1 = (f32[8,256]{1,0:T(8,128)S(1)}, f32[16,128]{1,0:T(8,128)S(1)}, s32[4]{0:T(128)S(1)}) custom-call(s32[1]{0:T(128)} %bitcast.index_ref, bf16[16,264,128]{2,1,0:T(8,128)(2,1)S(1)} %all-to-all-done.message_ref, bf16[16,128,128]{2,1,0:T(8,128)(2,1)S(1)} %slice.25.own_ref, bf16[16,128,128]{2,1,0:T(8,128)(2,1)S(1)} %collective-permute-done.other_ref, ...), custom_call_target="tpu_custom_call" | custom-call | flops 1342177280 | bytes 16777216 | tf_op jit(solution)/shard_map/attention_forward/pallas_call | solution.py:234
  50.0 0.2 collective-permute-start.1
  50.2 1.0 collective-permute-done.1
  51.3 1.4 %collective-permute-start.2 = (f32[16,128]{1,0:T(8,128)S(1)}, f32[16,128]{1,0:T(8,128)S(1)}, u32[]{:S(2)}, u32[]{:S(2)}) collective-permute-start(f32[16,128]{1,0:T(8,128)S(1)} %add.17), channel_id=1, source_target_pairs={{0,2},{1,3},{2,0},{3,1},{4,6},{5,7},{6,4},{7,5},{8,10},{9,11},{10,... | collective-permute-start | bytes 24584 | tf_op jit(solution)/shard_map/ppermute | solution.py:340
  52.7 1.4 %collective-permute-done.2 = f32[16,128]{1,0:T(8,128)S(1)} collective-permute-done((f32[16,128]{1,0:T(8,128)S(1)}, f32[16,128]{1,0:T(8,128)S(1)}, u32[]{:S(2)}, u32[]{:S(2)}) %collective-permute-start.2) | collective-permute-done | bytes 8224 | tf_op jit(solution)/shard_map/ppermute | solution.py:340
  54.1 1.1 collective-permute-start.3
  55.2 1.4 %collective-permute-done.3 = f32[16,128]{1,0:T(8,128)S(1)} collective-permute-done((f32[16,128]{1,0:T(8,128)S(1)}, f32[16,128]{1,0:T(8,128)S(1)}, u32[]{:S(2)}, u32[]{:S(2)}) %collective-permute-start.3) | collective-permute-done | bytes 8224 | tf_op jit(solution)/shard_map/ppermute | solution.py:340
  56.6 2.1 %collective-permute-start.4 = (f32[16,128]{1,0:T(8,128)S(1)}, f32[16,128]{1,0:T(8,128)S(1)}, u32[]{:S(2)}, u32[]{:S(2)}) collective-permute-start(f32[16,128]{1,0:T(8,128)S(1)} %add.19), channel_id=1, source_target_pairs={{0,8},{1,9},{2,10},{3,11},{4,12},{5,13},{6,14},{7,15},{8,0},{9,1},... | collective-permute-start | bytes 24584 | tf_op jit(solution)/shard_map/ppermute | solution.py:340
  58.7 1.3 %collective-permute-done.4 = f32[16,128]{1,0:T(8,128)S(1)} collective-permute-done((f32[16,128]{1,0:T(8,128)S(1)}, f32[16,128]{1,0:T(8,128)S(1)}, u32[]{:S(2)}, u32[]{:S(2)}) %collective-permute-start.4) | collective-permute-done | bytes 8224 | tf_op jit(solution)/shard_map/ppermute | solution.py:340
  60.0 9.5 %attention_backward.1 = (bf16[16,128,128]{2,1,0:T(8,128)(2,1)S(1)}, bf16[16,128,128]{2,1,0:T(8,128)(2,1)S(1)}, bf16[16,128,128]{2,1,0:T(8,128)(2,1)S(1)}) custom-call(s32[1]{0:T(128)} %bitcast.index_ref, s32[4]{0:T(128)S(1)} %get-tuple-element.12.starts_ref, bf16[16,264,128]{2,1,0:T(8,128)(2,1)S(1)} %all-to-all-done.message_ref, ...), custom_call_target="tpu_custom_call" | custom-call | flops 2684354560 | bytes 16777216 | tf_op jit(solution)/shard_map/attention_backward/pallas_call | solution.py:262
  69.5 3.4 %collective-permute-start.5 = (bf16[16,128,128]{2,1,0:T(8,128)(2,1)S(1)}, bf16[16,128,128]{2,1,0:T(8,128)(2,1)S(1)}, u32[]{:S(2)}, u32[]{:S(2)}) collective-permute-start(bf16[16,128,128]{2,1,0:T(8,128)(2,1)S(1)} %get-tuple-element.18), channel_id=1, source_target_pairs={{0,1},{1,0},{2,3},{3,2},{4,5},{5,4},{6,7},{7,6},{8,9},{9,8},{10,11... | collective-permute-start | bytes 1572872 | tf_op jit(solution)/shard_map/ppermute | solution.py:306
  72.9 1.5 %collective-permute-done.5 = bf16[16,128,128]{2,1,0:T(8,128)(2,1)S(1)} collective-permute-done((bf16[16,128,128]{2,1,0:T(8,128)(2,1)S(1)}, bf16[16,128,128]{2,1,0:T(8,128)(2,1)S(1)}, u32[]{:S(2)}, u32[]{:S(2)}) %collective-permute-start.5) | collective-permute-done | bytes 524320 | tf_op jit(solution)/shard_map/ppermute | solution.py:306
  74.5 0.1 add_convert_fusion
  74.6 0.1 pad_maximum_fusion.1
  74.7 31.3 %all_to_all.15 = bf16[16,256,128]{2,1,0:T(8,128)(2,1)S(1)} all-to-all(bf16[16,256,128]{2,1,0:T(8,128)(2,1)S(1)} %pad_maximum_fusion.1), channel_id=1, replica_groups=mesh['groups'=2,'context'=16] {'context'}, dimensions={0} | all-to-all | bytes 2097152 | tf_op jit(solution)/shard_map/all_to_all | solution.py:301
  106.1 0.9 copy.30
  106.9 1.1 %copy.28 = bf16[128,16,128]{2,1,0:T(8,128)(2,1)} copy(bf16[128,16,128]{2,0,1:T(8,128)(2,1)S(1)} %slice.35) | data formatting | bytes 1048576
  108.1 0.9 copy.29
  (23 shorter events, 0.2 us)
Async XLA Ops:
  0.6 1.9 %copy-start.2 = (bf16[128,8,128]{2,1,0:T(8,128)(2,1)S(1)}, bf16[128,8,128]{2,1,0:T(8,128)(2,1)}, u32[]{:S(2)}) copy-start(bf16[128,8,128]{2,1,0:T(8,128)(2,1)} %param.10) | copy-start | bytes 786436
  0.6 1.9 %copy-start.3 = (bf16[128,8,128]{2,1,0:T(8,128)(2,1)S(1)}, bf16[128,8,128]{2,1,0:T(8,128)(2,1)}, u32[]{:S(2)}) copy-start(bf16[128,8,128]{2,1,0:T(8,128)(2,1)} %param.9) | copy-start | bytes 786436
  2.5 0.7 copy-start.4
  2.6 0.7 copy-start.5
  4.3 7.5 %copy-start.1 = (bf16[128,16,128]{2,1,0:T(8,128)(2,1)S(1)}, bf16[128,16,128]{2,1,0:T(8,128)(2,1)}, u32[]{:S(2)}) copy-start(bf16[128,16,128]{2,1,0:T(8,128)(2,1)} %param.11) | copy-start | bytes 1572868
  4.3 31.3 %all-to-all-start = ((bf16[16,264,128]{2,1,0:T(8,128)(2,1)}), bf16[16,264,128]{2,1,0:T(8,128)(2,1)S(1)}, u32[]{:S(2)}, u32[]{:S(2)}) async-start(bf16[16,264,128]{2,1,0:T(8,128)(2,1)} %pad_maximum_fusion), calls=%async_computation | async-start | bytes 2162688 | tf_op jit(solution)/shard_map/all_to_all | solution.py:301
  35.6 24.4 %all-to-all-start.1 = ((bf16[16,128,128]{2,1,0:T(8,128)(2,1)}), bf16[16,128,128]{2,1,0:T(8,128)(2,1)S(1)}, u32[]{:S(2)}, u32[]{:S(2)}) async-start(bf16[16,128,128]{2,1,0:T(8,128)(2,1)} %bitcast.27), calls=%async_computation.1 | async-start | bytes 1048576 | tf_op jit(solution)/shard_map/all_to_all | solution.py:301
  42.4 2.0 %collective-permute-start = (bf16[16,128,128]{2,1,0:T(8,128)(2,1)S(1)}, bf16[16,128,128]{2,1,0:T(8,128)(2,1)S(1)}, u32[]{:S(2)}, u32[]{:S(2)}) collective-permute-start(bf16[16,128,128]{2,1,0:T(8,128)(2,1)S(1)} %slice.25.own_ref), channel_id=1, source_target_pairs={{0,1},{1,0},{2,3},{3,2},{4,5},{5,4},{6,7},{7,6},{8,9},{9,8},{10,11... | collective-permute-start | bytes 1572872 | tf_op jit(solution)/shard_map/ppermute | solution.py:306
  42.6 1.8 %copy-start = (f32[16,128]{1,0:T(8,128)S(1)}, f32[16,128]{1,0:T(8,128)}, u32[]{:S(2)}) copy-start(f32[16,128]{1,0:T(8,128)} %readout_ref.3) | copy-start | bytes 24580
  50.0 1.2 %collective-permute-start.1 = (f32[16,128]{1,0:T(8,128)S(1)}, f32[16,128]{1,0:T(8,128)S(1)}, u32[]{:S(2)}, u32[]{:S(2)}) collective-permute-start(f32[16,128]{1,0:T(8,128)S(1)} %get-tuple-element.14), channel_id=1, source_target_pairs={{0,1},{1,0},{2,3},{3,2},{4,5},{5,4},{6,7},{7,6},{8,9},{9,8},{10,11... | collective-permute-start | bytes 24584 | tf_op jit(solution)/shard_map/ppermute | solution.py:340
  51.3 2.8 %collective-permute-start.2 = (f32[16,128]{1,0:T(8,128)S(1)}, f32[16,128]{1,0:T(8,128)S(1)}, u32[]{:S(2)}, u32[]{:S(2)}) collective-permute-start(f32[16,128]{1,0:T(8,128)S(1)} %add.17), channel_id=1, source_target_pairs={{0,2},{1,3},{2,0},{3,1},{4,6},{5,7},{6,4},{7,5},{8,10},{9,11},{10,... | collective-permute-start | bytes 24584 | tf_op jit(solution)/shard_map/ppermute | solution.py:340
  54.1 2.5 %collective-permute-start.3 = (f32[16,128]{1,0:T(8,128)S(1)}, f32[16,128]{1,0:T(8,128)S(1)}, u32[]{:S(2)}, u32[]{:S(2)}) collective-permute-start(f32[16,128]{1,0:T(8,128)S(1)} %add.18), channel_id=1, source_target_pairs={{0,4},{1,5},{2,6},{3,7},{4,0},{5,1},{6,2},{7,3},{8,12},{9,13},{10,... | collective-permute-start | bytes 24584 | tf_op jit(solution)/shard_map/ppermute | solution.py:340
  56.6 3.4 %collective-permute-start.4 = (f32[16,128]{1,0:T(8,128)S(1)}, f32[16,128]{1,0:T(8,128)S(1)}, u32[]{:S(2)}, u32[]{:S(2)}) collective-permute-start(f32[16,128]{1,0:T(8,128)S(1)} %add.19), channel_id=1, source_target_pairs={{0,8},{1,9},{2,10},{3,11},{4,12},{5,13},{6,14},{7,15},{8,0},{9,1},... | collective-permute-start | bytes 24584 | tf_op jit(solution)/shard_map/ppermute | solution.py:340
  69.5 4.9 %collective-permute-start.5 = (bf16[16,128,128]{2,1,0:T(8,128)(2,1)S(1)}, bf16[16,128,128]{2,1,0:T(8,128)(2,1)S(1)}, u32[]{:S(2)}, u32[]{:S(2)}) collective-permute-start(bf16[16,128,128]{2,1,0:T(8,128)(2,1)S(1)} %get-tuple-element.18), channel_id=1, source_target_pairs={{0,1},{1,0},{2,3},{3,2},{4,5},{5,4},{6,7},{7,6},{8,9},{9,8},{10,11... | collective-permute-start | bytes 1572872 | tf_op jit(solution)/shard_map/ppermute | solution.py:306

commit v4 on v3

--- a/solution.py
+++ b/solution.py
@@ -14,7 +14,8 @@
 NEGATIVE = -1e30
 BLOCK = 256
 AUX = 8
-REACH = WINDOW // BLOCK + 1
+QUERIES = 2 * BLOCK
+REACH = (WINDOW + QUERIES) // BLOCK
 VMEM = pl.BlockSpec(memory_space=pltpu.VMEM)
 SMEM = pl.BlockSpec(memory_space=pltpu.SMEM)
 NT = (((1,), (1,)), ((), ()))
@@ -37,9 +38,9 @@
 
 
 def tokens_of(tokens, halo):
-    shape = (tokens // BLOCK, BLOCK)
+    shape = (tokens // QUERIES, QUERIES)
     row = lax.broadcasted_iota(jnp.int32, shape, 0)
-    return halo + row * BLOCK + lax.broadcasted_iota(jnp.int32, shape, 1)
+    return halo + row * QUERIES + lax.broadcasted_iota(jnp.int32, shape, 1)
 
 
 def rows_of(block):
@@ -47,8 +48,27 @@
 
 
 def by_reach(count, body):
-    for n in range(1, REACH + 1):
+    for n in range(2, REACH + 1):
         pl.when(count == n)(functools.partial(body, n))
+
+
+def late(j, n):
+    return slice(BLOCK, QUERIES) if j == n - 1 else slice(0, QUERIES)
+
+
+def valid_of(key_iota, causal, bound, j, n):
+    span = late(j, n)
+    valid = key_iota[:, span] >= bound[:, span] - j * BLOCK
+    if j == n - 1:
+        return valid & causal[:, :BLOCK]
+    return valid & causal if j == n - 2 else valid
+
+
+def fold(parts, combine, reduce):
+    if reduce is not None:
+        parts = [reduce(p.reshape(p.shape[0] // 8, 8, p.shape[1]), axis=0) for p in parts]
+    whole = functools.reduce(combine, parts[:-1])
+    return jnp.concatenate([whole[:, :BLOCK], combine(whole[:, BLOCK:], parts[-1])], axis=1)
 
 
 def forward_kernel(
@@ -93,38 +113,36 @@
     for n, start in enumerate(starts):
         starts_ref[n] = start
     bound_s[...] = begin_of(starts, tokens_of(tokens, halo))
-    key_iota = lax.broadcasted_iota(jnp.int32, (BLOCK, BLOCK), 0)
-    query_iota = lax.broadcasted_iota(jnp.int32, (BLOCK, BLOCK), 1)
+    key_iota = lax.broadcasted_iota(jnp.int32, (BLOCK, QUERIES), 0)
+    query_iota = lax.broadcasted_iota(jnp.int32, (BLOCK, QUERIES), 1)
+    causal = key_iota <= query_iota
 
     def query_block(i, _):
-        first = lax.div(begin_of(starts, halo + i * BLOCK), BLOCK)
+        first = lax.div(begin_of(starts, halo + i * QUERIES), BLOCK)
 
         def body(n):
-            query = message_ref[pl.ds(2 * i, 2), 0:128, :].reshape(BLOCK, 128)
+            query = message_ref[pl.ds(4 * i, 4), 0:128, :].reshape(QUERIES, 128)
             bound = bound_s[pl.ds(i, 1), :] - first * BLOCK
-            scores, tops = [], []
+            scores = []
             for j in range(n):
-                score = dot(key_s[rows_of(first + j), :], query, NT)
-                valid = key_iota >= bound - j * BLOCK
-                if j == n - 1:
-                    valid = valid & (key_iota <= query_iota)
-                score = jnp.where(valid, score, NEGATIVE)
-                scores.append(score)
-                tops.append(jnp.max(score.reshape(BLOCK // 8, 8, BLOCK), axis=0))
-            top = jnp.max(functools.reduce(jnp.maximum, tops), axis=0, keepdims=True)
-            sums = jnp.zeros((8, BLOCK), jnp.float32)
+                span = late(j, n)
+                score = dot(key_s[rows_of(first + j), :], query[span], NT)
+                scores.append(jnp.where(valid_of(key_iota, causal, bound, j, n), score, NEGATIVE))
+            top = jnp.max(fold(scores, jnp.maximum, jnp.max), axis=0, keepdims=True)
+            sums = []
             for j in range(n):
-                prob = jnp.exp2((scores[j] - top) * (SCALE * LOG2E)).astype(low_bits)
-                sums = sums + dot(side_s[:, rows_of(first + j)], prob, NN)
+                prob = jnp.exp2((scores[j] - top[:, late(j, n)]) * (SCALE * LOG2E))
+                sums.append(dot(side_s[:, rows_of(first + j)], prob.astype(low_bits), NN))
+            sums = fold(sums, jnp.add, None)
             reward = (sums[0:1] + sums[1:2]) / sums[2:3]
             total_ref[pl.ds(i, 1), :] = top * (SCALE * LOG2E) + jnp.log2(sums[2:3])
-            reward_ref[pl.ds(2 * i, 1), :] = reward[:, :128]
-            reward_ref[pl.ds(2 * i + 1, 1), :] = reward[:, 128:]
-
-        by_reach(i + shift + 1 - first, body)
+            for part in range(4):
+                reward_ref[pl.ds(4 * i + part, 1), :] = reward[:, part * 128 : (part + 1) * 128]
+
+        by_reach(2 * i + 2 + shift - first, body)
         return 0
 
-    lax.fori_loop(0, tokens // BLOCK, query_block, 0)
+    lax.fori_loop(0, tokens // QUERIES, query_block, 0)
 
 
 def backward_kernel(
@@ -164,56 +182,54 @@
 
     starts = [starts_ref[n] for n in range(4)]
     bound_s[...] = begin_of(starts, tokens_of(tokens, halo))
-    key_iota = lax.broadcasted_iota(jnp.int32, (BLOCK, BLOCK), 0)
-    query_iota = lax.broadcasted_iota(jnp.int32, (BLOCK, BLOCK), 1)
+    key_iota = lax.broadcasted_iota(jnp.int32, (BLOCK, QUERIES), 0)
+    query_iota = lax.broadcasted_iota(jnp.int32, (BLOCK, QUERIES), 1)
+    causal = key_iota <= query_iota
     if halo:
         key_grad_s[:halo, :] = jnp.zeros((halo, 128), jnp.float32)
         value_grad_s[:halo, :] = jnp.zeros((halo, 128), jnp.float32)
 
     def query_block(i, _):
-        first = lax.div(begin_of(starts, halo + i * BLOCK), BLOCK)
+        first = lax.div(begin_of(starts, halo + i * QUERIES), BLOCK)
 
         def body(n):
-            grad = grad_s[pl.ds(2 * i, 2)].reshape(BLOCK, 128)
-            query = message_ref[pl.ds(2 * i, 2), 0:128, :].reshape(BLOCK, 128)
+            grad = grad_s[pl.ds(4 * i, 4)].reshape(QUERIES, 128)
+            query = message_ref[pl.ds(4 * i, 4), 0:128, :].reshape(QUERIES, 128)
             bound = bound_s[pl.ds(i, 1), :] - first * BLOCK
             total = total_ref[pl.ds(i, 1), :]
-            probs, grad_probs = [], []
-            delta = jnp.zeros((8, BLOCK), jnp.float32)
+            probs, grad_probs, deltas = [], [], []
             for j in range(n):
-                rows = rows_of(first + j)
-                score = dot(key_s[rows, :], query, NT) * (SCALE * LOG2E) - total
-                valid = key_iota >= bound - j * BLOCK
-                if j == n - 1:
-                    valid = valid & (key_iota <= query_iota)
+                rows, span = rows_of(first + j), late(j, n)
+                score = dot(key_s[rows, :], query[span], NT) * (SCALE * LOG2E) - total[:, span]
+                valid = valid_of(key_iota, causal, bound, j, n)
                 prob = jnp.exp2(jnp.where(valid, score, NEGATIVE))
-                grad_prob = dot(value_s[rows, :], grad, NT)
-                delta = delta + jnp.sum((prob * grad_prob).reshape(BLOCK // 8, 8, BLOCK), axis=0)
-                value_grad = dot(prob.astype(jnp.bfloat16), grad, NN)
-                if j == n - 1:
+                grad_prob = dot(value_s[rows, :], grad[span], NT)
+                deltas.append(prob * grad_prob)
+                value_grad = dot(prob.astype(jnp.bfloat16), grad[span], NN)
+                if j >= n - 2:
                     value_grad_s[rows, :] = value_grad
                 else:
                     value_grad_s[rows, :] += value_grad
                 probs.append(prob)
                 grad_probs.append(grad_prob)
-            delta = jnp.sum(delta, axis=0, keepdims=True)
-            query_grad = jnp.zeros((128, BLOCK), jnp.float32)
+            delta = jnp.sum(fold(deltas, jnp.add, jnp.sum), axis=0, keepdims=True)
+            query_grads = []
             for j in range(n):
-                rows = rows_of(first + j)
-                grad_score = (probs[j] * (grad_probs[j] - delta)).astype(jnp.bfloat16)
-                key_grad = dot(grad_score, query, NN)
-                if j == n - 1:
+                rows, span = rows_of(first + j), late(j, n)
+                grad_score = (probs[j] * (grad_probs[j] - delta[:, span])).astype(jnp.bfloat16)
+                key_grad = dot(grad_score, query[span], NN)
+                if j >= n - 2:
                     key_grad_s[rows, :] = key_grad
                 else:
                     key_grad_s[rows, :] += key_grad
-                query_grad = query_grad + dot(turned_s[:, rows], grad_score, NN)
-            query_grad = (query_grad * SCALE).T.astype(jnp.bfloat16)
-            query_ref[pl.ds(2 * i, 2)] = query_grad.reshape(2, 128, 128)
-
-        by_reach(i + shift + 1 - first, body)
+                query_grads.append(dot(turned_s[:, rows], grad_score, NN))
+            query_grad = (fold(query_grads, jnp.add, None) * SCALE).T.astype(jnp.bfloat16)
+            query_ref[pl.ds(4 * i, 4)] = query_grad.reshape(4, 128, 128)
+
+        by_reach(2 * i + 2 + shift - first, body)
         return 0
 
-    lax.fori_loop(0, tokens // BLOCK, query_block, 0)
+    lax.fori_loop(0, tokens // QUERIES, query_block, 0)
     shape = keep_ref.shape
 
     @pl.when(even)
@@ -230,11 +246,11 @@
 def attention_forward(halo, where, message, own, other, seg, readout):
     heads, depth = message.shape[0], message.shape[2]
     key_tokens = own.shape[0] * own.shape[1]
-    count = heads * own.shape[1] // BLOCK
+    count = message.shape[0] * 128 // QUERIES
     return pl.pallas_call(
         functools.partial(forward_kernel, halo),
         out_shape=(
-            jax.ShapeDtypeStruct((count, BLOCK), jnp.float32),
+            jax.ShapeDtypeStruct((count, QUERIES), jnp.float32),
             jax.ShapeDtypeStruct((heads, own.shape[1]), jnp.float32),
             jax.ShapeDtypeStruct((4,), jnp.int32),
         ),
@@ -243,13 +259,13 @@
         scratch_shapes=[
             pltpu.VMEM((key_tokens, depth), jnp.bfloat16),
             pltpu.VMEM((8, key_tokens), jnp.bfloat16),
-            pltpu.VMEM((count, BLOCK), jnp.int32),
+            pltpu.VMEM((count, QUERIES), jnp.int32),
         ],
         compiler_params=pltpu.CompilerParams(vmem_limit_bytes=24 << 20),
         cost_estimate=pl.CostEstimate(
-            flops=4 * BLOCK * BLOCK * depth * count * REACH,
+            flops=4 * BLOCK * QUERIES * depth * count * REACH,
             bytes_accessed=16 << 20,
-            transcendentals=BLOCK * BLOCK * count * REACH,
+            transcendentals=BLOCK * QUERIES * count * REACH,
         ),
         name="attention_forward",
     )(where, message, own, other, seg, readout)
@@ -258,7 +274,7 @@
 def attention_backward(halo, where, starts, message, own, other, grad, readout, reward, flag, total):
     heads, depth = message.shape[0], message.shape[2]
     key_tokens = own.shape[0] * own.shape[1]
-    count = heads * own.shape[1] // BLOCK
+    count = message.shape[0] * 128 // QUERIES
     return pl.pallas_call(
         functools.partial(backward_kernel, halo),
         out_shape=(
@@ -273,13 +289,13 @@
             pltpu.VMEM((depth, key_tokens), jnp.bfloat16),
             pltpu.VMEM((key_tokens, depth), jnp.bfloat16),
             pltpu.VMEM(grad.shape, jnp.bfloat16),
-            pltpu.VMEM((count, BLOCK), jnp.int32),
+            pltpu.VMEM((count, QUERIES), jnp.int32),
             pltpu.VMEM((key_tokens, depth), jnp.float32),
             pltpu.VMEM((key_tokens, depth), jnp.float32),
         ],
         compiler_params=pltpu.CompilerParams(vmem_limit_bytes=24 << 20),
         cost_estimate=pl.CostEstimate(
-            flops=8 * BLOCK * BLOCK * depth * count * REACH,
+            flops=10 * BLOCK * QUERIES * depth * count * REACH,
             bytes_accessed=16 << 20,
             transcendentals=0,
         ),

time: 109 us -> 107 us (0.982); the launches traced: 109 us -> 105 us
  Pallas kernels: 15.2 us -> 11.2 us
  waiting for transfers between devices: 31.2 us -> 32.3 us
    pallas_call x1, Pallas kernels: 9.5 us -> 6.97 us  [attention_backward(): pl.pallas_call(functools.partial(backward_kernel, halo), out_shape=(jax.S...]
    pallas_call x1, Pallas kernels: 5.66 us -> 4.2 us  [attention_forward(): pl.pallas_call(functools.partial(forward_kernel, halo), out_shape=(jax.Sh...]
    ppermute x2, starting transfers between devices: 3.55 us -> 2.4 us  [swap(): return lax.ppermute(array, 'context', pairs)]
  transfers between devices with their start and end apart: 8 -> 8, of which waited for: 7 -> 7; matrix products, arithmetic and copies ran while one was open for 1% -> 1% of each run, Pallas kernels for 5% -> 4%
where the time goes in v4:
time: 107 us; the launch traced here: 105 us
  waiting for transfers between devices  32.3 us (30%)
  blocking collectives  31.2 us (29%)
  starting transfers between devices  21.5 us (20%)
  Pallas kernels  11.2 us (10%)
  local copies, waits for them, and re-layouts  5.86 us (5%)
  other arithmetic  2.13 us (2%)
    all_to_all x1, blocking collectives, exchange(): lax.all_to_all(array, 'context', 0, 0, tiled=True, axis_index_groups=clus...  31.2 us
    all_to_all x2, waiting for transfers between devices, exchange(): lax.all_to_all(array, 'context', 0, 0, tiled=True, axis_index_groups=clus...  22.8 us
    all_to_all x2, starting transfers between devices, exchange(): lax.all_to_all(array, 'context', 0, 0, tiled=True, axis_index_groups=clus...  14.2 us
    pallas_call x1, Pallas kernels, attention_backward(): pl.pallas_call(functools.partial(backward_kernel, halo), out_shape=(jax.S...  6.97 us
    ppermute x4, waiting for transfers between devices, local(): lax.ppermute(reward, 'context', [(i, i ^ step) for i in range(devices)])  6.23 us
    unnamed x17, local copies, waits for them, and re-layouts  5.49 us
    ppermute x4, starting transfers between devices, local(): lax.ppermute(reward, 'context', [(i, i ^ step) for i in range(devices)])  4.9 us
    pallas_call x1, Pallas kernels, attention_forward(): pl.pallas_call(functools.partial(forward_kernel, halo), out_shape=(jax.Sh...  4.2 us
  transfers between devices with their start and end apart: 8, of which 7 were waited for; matrix products, arithmetic and copies ran while one was open for 1% of the time, Pallas kernels for 4%

profile of v4, /device:TPU:1, one launch (start us, length us, event | category | flops | bytes accessed | tf_op | source)
XLA Modules:
  0.0 104.9 jit_solution(11611873635361050243)
XLA Ops:
  0.7 0.7 convert_bitcast_fusion.2
  1.4 1.2 %copy.33 = bf16[128,16,128]{2,0,1:T(8,128)(2,1)S(1)} copy(bf16[128,16,128]{2,1,0:T(8,128)(2,1)} %param.8) | data formatting | bytes 1048576 | tf_op args[0]
  2.6 0.1 pad_maximum_fusion.2
  2.6 0.1 copy.24
  2.8 0.5 copy-done.4
  3.2 0.0 copy-done.5
  3.3 1.1 %pad_maximum_fusion = bf16[16,264,128]{2,1,0:T(8,128)(2,1)} fusion(bf16[16,8,128]{2,1,0:T(8,128)(2,1)S(1)} %broadcast_in_dim.2, bf16[16,128,128]{2,1,0:T(8,128)(2,1)S(1)} %bitcast.31, bf16[16,128,128]{2,1,0:T(8,128)(2,1)S(1)} %bitcast.30), kind=kLoop, calls=%fused_computation | loop fusion | flops 3244032 | bytes 2162688 | tf_op jit(solution)/shard_map/concatenate | solution.py:327
  4.3 7.5 %all-to-all-start = ((bf16[16,264,128]{2,1,0:T(8,128)(2,1)}), bf16[16,264,128]{2,1,0:T(8,128)(2,1)S(1)}, u32[]{:S(2)}, u32[]{:S(2)}) async-start(bf16[16,264,128]{2,1,0:T(8,128)(2,1)} %pad_maximum_fusion), calls=%async_computation | async-start | bytes 2162688 | tf_op jit(solution)/shard_map/all_to_all | solution.py:317
  11.8 0.9 copy.34
  12.8 22.8 %all-to-all-done.message_ref = bf16[16,264,128]{2,1,0:T(8,128)(2,1)S(1)} async-done(((bf16[16,264,128]{2,1,0:T(8,128)(2,1)}), bf16[16,264,128]{2,1,0:T(8,128)(2,1)S(1)}, u32[]{:S(2)}, u32[]{:S(2)}) %all-to-all-start) | async-done | bytes 1081376 | tf_op jit(solution)/shard_map/all_to_all | solution.py:317
  35.6 6.7 %all-to-all-start.1 = ((bf16[16,128,128]{2,1,0:T(8,128)(2,1)}), bf16[16,128,128]{2,1,0:T(8,128)(2,1)S(1)}, u32[]{:S(2)}, u32[]{:S(2)}) async-start(bf16[16,128,128]{2,1,0:T(8,128)(2,1)} %bitcast.27), calls=%async_computation.1 | async-start | bytes 1048576 | tf_op jit(solution)/shard_map/all_to_all | solution.py:317
  42.4 0.2 collective-permute-start
  42.6 0.1 copy.25
  42.7 1.6 %collective-permute-done.other_ref = bf16[16,128,128]{2,1,0:T(8,128)(2,1)S(1)} collective-permute-done((bf16[16,128,128]{2,1,0:T(8,128)(2,1)S(1)}, bf16[16,128,128]{2,1,0:T(8,128)(2,1)S(1)}, u32[]{:S(2)}, u32[]{:S(2)}) %collective-permute-start) | collective-permute-done | bytes 524320 | tf_op jit(solution)/shard_map/ppermute | solution.py:322
  44.4 4.2 %attention_forward.1 = (f32[4,512]{1,0:T(4,128)S(1)}, f32[16,128]{1,0:T(8,128)S(1)}, s32[4]{0:T(128)S(1)}) custom-call(s32[1]{0:T(128)} %bitcast.index_ref, bf16[16,264,128]{2,1,0:T(8,128)(2,1)S(1)} %all-to-all-done.message_ref, bf16[16,128,128]{2,1,0:T(8,128)(2,1)S(1)} %slice.25.own_ref, bf16[16,128,128]{2,1,0:T(8,128)(2,1)S(1)} %collective-permute-done.other_ref, ...), custom_call_target="tpu_custom_call" | custom-call | flops 1610612736 | bytes 16777216 | tf_op jit(solution)/shard_map/attention_forward/pallas_call | solution.py:250
  48.6 0.2 collective-permute-start.1
  48.8 1.0 collective-permute-done.1
  49.8 1.4 %collective-permute-start.2 = (f32[16,128]{1,0:T(8,128)S(1)}, f32[16,128]{1,0:T(8,128)S(1)}, u32[]{:S(2)}, u32[]{:S(2)}) collective-permute-start(f32[16,128]{1,0:T(8,128)S(1)} %add.17), channel_id=1, source_target_pairs={{0,2},{1,3},{2,0},{3,1},{4,6},{5,7},{6,4},{7,5},{8,10},{9,11},{10,... | collective-permute-start | bytes 24584 | tf_op jit(solution)/shard_map/ppermute | solution.py:356
  51.2 1.5 %collective-permute-done.2 = f32[16,128]{1,0:T(8,128)S(1)} collective-permute-done((f32[16,128]{1,0:T(8,128)S(1)}, f32[16,128]{1,0:T(8,128)S(1)}, u32[]{:S(2)}, u32[]{:S(2)}) %collective-permute-start.2) | collective-permute-done | bytes 8224 | tf_op jit(solution)/shard_map/ppermute | solution.py:356
  52.7 2.2 %collective-permute-start.3 = (f32[16,128]{1,0:T(8,128)S(1)}, f32[16,128]{1,0:T(8,128)S(1)}, u32[]{:S(2)}, u32[]{:S(2)}) collective-permute-start(f32[16,128]{1,0:T(8,128)S(1)} %add.18), channel_id=1, source_target_pairs={{0,4},{1,5},{2,6},{3,7},{4,0},{5,1},{6,2},{7,3},{8,12},{9,13},{10,... | collective-permute-start | bytes 24584 | tf_op jit(solution)/shard_map/ppermute | solution.py:356
  54.9 1.4 %collective-permute-done.3 = f32[16,128]{1,0:T(8,128)S(1)} collective-permute-done((f32[16,128]{1,0:T(8,128)S(1)}, f32[16,128]{1,0:T(8,128)S(1)}, u32[]{:S(2)}, u32[]{:S(2)}) %collective-permute-start.3) | collective-permute-done | bytes 8224 | tf_op jit(solution)/shard_map/ppermute | solution.py:356
  56.3 1.1 %collective-permute-start.4 = (f32[16,128]{1,0:T(8,128)S(1)}, f32[16,128]{1,0:T(8,128)S(1)}, u32[]{:S(2)}, u32[]{:S(2)}) collective-permute-start(f32[16,128]{1,0:T(8,128)S(1)} %add.19), channel_id=1, source_target_pairs={{0,8},{1,9},{2,10},{3,11},{4,12},{5,13},{6,14},{7,15},{8,0},{9,1},... | collective-permute-start | bytes 24584 | tf_op jit(solution)/shard_map/ppermute | solution.py:356
  57.5 2.3 %collective-permute-done.4 = f32[16,128]{1,0:T(8,128)S(1)} collective-permute-done((f32[16,128]{1,0:T(8,128)S(1)}, f32[16,128]{1,0:T(8,128)S(1)}, u32[]{:S(2)}, u32[]{:S(2)}) %collective-permute-start.4) | collective-permute-done | bytes 8224 | tf_op jit(solution)/shard_map/ppermute | solution.py:356
  59.7 7.0 %attention_backward.1 = (bf16[16,128,128]{2,1,0:T(8,128)(2,1)S(1)}, bf16[16,128,128]{2,1,0:T(8,128)(2,1)S(1)}, bf16[16,128,128]{2,1,0:T(8,128)(2,1)S(1)}) custom-call(s32[1]{0:T(128)} %bitcast.index_ref, s32[4]{0:T(128)S(1)} %get-tuple-element.12.starts_ref, bf16[16,264,128]{2,1,0:T(8,128)(2,1)S(1)} %all-to-all-done.message_ref, ...), custom_call_target="tpu_custom_call" | custom-call | flops 4026531840 | bytes 16777216 | tf_op jit(solution)/shard_map/attention_backward/pallas_call | solution.py:278
  66.7 2.2 %collective-permute-start.5 = (bf16[16,128,128]{2,1,0:T(8,128)(2,1)S(1)}, bf16[16,128,128]{2,1,0:T(8,128)(2,1)S(1)}, u32[]{:S(2)}, u32[]{:S(2)}) collective-permute-start(bf16[16,128,128]{2,1,0:T(8,128)(2,1)S(1)} %get-tuple-element.18), channel_id=1, source_target_pairs={{0,1},{1,0},{2,3},{3,2},{4,5},{5,4},{6,7},{7,6},{8,9},{9,8},{10,11... | collective-permute-start | bytes 1572872 | tf_op jit(solution)/shard_map/ppermute | solution.py:322
  69.0 1.5 %collective-permute-done.5 = bf16[16,128,128]{2,1,0:T(8,128)(2,1)S(1)} collective-permute-done((bf16[16,128,128]{2,1,0:T(8,128)(2,1)S(1)}, bf16[16,128,128]{2,1,0:T(8,128)(2,1)S(1)}, u32[]{:S(2)}, u32[]{:S(2)}) %collective-permute-start.5) | collective-permute-done | bytes 524320 | tf_op jit(solution)/shard_map/ppermute | solution.py:322
  70.5 0.1 add_convert_fusion
  70.6 0.1 pad_maximum_fusion.1
  70.7 31.2 %all_to_all.15 = bf16[16,256,128]{2,1,0:T(8,128)(2,1)S(1)} all-to-all(bf16[16,256,128]{2,1,0:T(8,128)(2,1)S(1)} %pad_maximum_fusion.1), channel_id=1, replica_groups=mesh['groups'=2,'context'=16] {'context'}, dimensions={0} | all-to-all | bytes 2097152 | tf_op jit(solution)/shard_map/all_to_all | solution.py:317
  102.0 0.9 copy.30
  102.9 1.1 %copy.28 = bf16[128,16,128]{2,1,0:T(8,128)(2,1)} copy(bf16[128,16,128]{2,0,1:T(8,128)(2,1)S(1)} %slice.35) | data formatting | bytes 1048576
  104.0 0.9 copy.29
  (23 shorter events, 0.2 us)
Async XLA Ops:
  0.6 1.9 %copy-start.2 = (bf16[128,8,128]{2,1,0:T(8,128)(2,1)S(1)}, bf16[128,8,128]{2,1,0:T(8,128)(2,1)}, u32[]{:S(2)}) copy-start(bf16[128,8,128]{2,1,0:T(8,128)(2,1)} %param.10) | copy-start | bytes 786436
  0.6 1.9 %copy-start.3 = (bf16[128,8,128]{2,1,0:T(8,128)(2,1)S(1)}, bf16[128,8,128]{2,1,0:T(8,128)(2,1)}, u32[]{:S(2)}) copy-start(bf16[128,8,128]{2,1,0:T(8,128)(2,1)} %param.9) | copy-start | bytes 786436
  2.5 0.7 copy-start.4
  2.6 0.7 copy-start.5
  4.3 7.5 %copy-start.1 = (bf16[128,16,128]{2,1,0:T(8,128)(2,1)S(1)}, bf16[128,16,128]{2,1,0:T(8,128)(2,1)}, u32[]{:S(2)}) copy-start(bf16[128,16,128]{2,1,0:T(8,128)(2,1)} %param.11) | copy-start | bytes 1572868
  4.3 31.3 %all-to-all-start = ((bf16[16,264,128]{2,1,0:T(8,128)(2,1)}), bf16[16,264,128]{2,1,0:T(8,128)(2,1)S(1)}, u32[]{:S(2)}, u32[]{:S(2)}) async-start(bf16[16,264,128]{2,1,0:T(8,128)(2,1)} %pad_maximum_fusion), calls=%async_computation | async-start | bytes 2162688 | tf_op jit(solution)/shard_map/all_to_all | solution.py:317
  35.6 24.1 %all-to-all-start.1 = ((bf16[16,128,128]{2,1,0:T(8,128)(2,1)}), bf16[16,128,128]{2,1,0:T(8,128)(2,1)S(1)}, u32[]{:S(2)}, u32[]{:S(2)}) async-start(bf16[16,128,128]{2,1,0:T(8,128)(2,1)} %bitcast.27), calls=%async_computation.1 | async-start | bytes 1048576 | tf_op jit(solution)/shard_map/all_to_all | solution.py:317
  42.4 2.0 %collective-permute-start = (bf16[16,128,128]{2,1,0:T(8,128)(2,1)S(1)}, bf16[16,128,128]{2,1,0:T(8,128)(2,1)S(1)}, u32[]{:S(2)}, u32[]{:S(2)}) collective-permute-start(bf16[16,128,128]{2,1,0:T(8,128)(2,1)S(1)} %slice.25.own_ref), channel_id=1, source_target_pairs={{0,1},{1,0},{2,3},{3,2},{4,5},{5,4},{6,7},{7,6},{8,9},{9,8},{10,11... | collective-permute-start | bytes 1572872 | tf_op jit(solution)/shard_map/ppermute | solution.py:322
  42.6 1.8 %copy-start = (f32[16,128]{1,0:T(8,128)S(1)}, f32[16,128]{1,0:T(8,128)}, u32[]{:S(2)}) copy-start(f32[16,128]{1,0:T(8,128)} %readout_ref.3) | copy-start | bytes 24580
  48.6 1.2 %collective-permute-start.1 = (f32[16,128]{1,0:T(8,128)S(1)}, f32[16,128]{1,0:T(8,128)S(1)}, u32[]{:S(2)}, u32[]{:S(2)}) collective-permute-start(f32[16,128]{1,0:T(8,128)S(1)} %get-tuple-element.14), channel_id=1, source_target_pairs={{0,1},{1,0},{2,3},{3,2},{4,5},{5,4},{6,7},{7,6},{8,9},{9,8},{10,11... | collective-permute-start | bytes 24584 | tf_op jit(solution)/shard_map/ppermute | solution.py:356
  49.8 2.9 %collective-permute-start.2 = (f32[16,128]{1,0:T(8,128)S(1)}, f32[16,128]{1,0:T(8,128)S(1)}, u32[]{:S(2)}, u32[]{:S(2)}) collective-permute-start(f32[16,128]{1,0:T(8,128)S(1)} %add.17), channel_id=1, source_target_pairs={{0,2},{1,3},{2,0},{3,1},{4,6},{5,7},{6,4},{7,5},{8,10},{9,11},{10,... | collective-permute-start | bytes 24584 | tf_op jit(solution)/shard_map/ppermute | solution.py:356
  52.7 3.6 %collective-permute-start.3 = (f32[16,128]{1,0:T(8,128)S(1)}, f32[16,128]{1,0:T(8,128)S(1)}, u32[]{:S(2)}, u32[]{:S(2)}) collective-permute-start(f32[16,128]{1,0:T(8,128)S(1)} %add.18), channel_id=1, source_target_pairs={{0,4},{1,5},{2,6},{3,7},{4,0},{5,1},{6,2},{7,3},{8,12},{9,13},{10,... | collective-permute-start | bytes 24584 | tf_op jit(solution)/shard_map/ppermute | solution.py:356
  56.3 3.4 %collective-permute-start.4 = (f32[16,128]{1,0:T(8,128)S(1)}, f32[16,128]{1,0:T(8,128)S(1)}, u32[]{:S(2)}, u32[]{:S(2)}) collective-permute-start(f32[16,128]{1,0:T(8,128)S(1)} %add.19), channel_id=1, source_target_pairs={{0,8},{1,9},{2,10},{3,11},{4,12},{5,13},{6,14},{7,15},{8,0},{9,1},... | collective-permute-start | bytes 24584 | tf_op jit(solution)/shard_map/ppermute | solution.py:356
  66.7 3.8 %collective-permute-start.5 = (bf16[16,128,128]{2,1,0:T(8,128)(2,1)S(1)}, bf16[16,128,128]{2,1,0:T(8,128)(2,1)S(1)}, u32[]{:S(2)}, u32[]{:S(2)}) collective-permute-start(bf16[16,128,128]{2,1,0:T(8,128)(2,1)S(1)} %get-tuple-element.18), channel_id=1, source_target_pairs={{0,1},{1,0},{2,3},{3,2},{4,5},{5,4},{6,7},{7,6},{8,9},{9,8},{10,11... | collective-permute-start | bytes 1572872 | tf_op jit(solution)/shard_map/ppermute | solution.py:322

commit v5 on v4

--- a/solution.py
+++ b/solution.py
@@ -17,6 +17,7 @@
 QUERIES = 2 * BLOCK
 REACH = (WINDOW + QUERIES) // BLOCK
 VMEM = pl.BlockSpec(memory_space=pltpu.VMEM)
+ANY = pl.BlockSpec(memory_space=pl.ANY)
 SMEM = pl.BlockSpec(memory_space=pltpu.SMEM)
 NT = (((1,), (1,)), ((), ()))
 NN = (((1,), (0,)), ((), ()))
@@ -303,6 +304,88 @@
     )(where, starts, message, own, other, grad, readout, reward, flag, total)
 
 
+def pack_kernel(
+    segments_ref, mask_ref, labels_ref, queries_ref, keys_ref, values_ref,
+    message_ref, query_s, key_s, value_s, message_s, in_sems, out_sems,
+):
+    rows, kv_heads = keys_ref.shape[:2]
+    copies = [
+        pltpu.make_async_copy(source, target, in_sems.at[n])
+        for n, (source, target) in enumerate(
+            [(queries_ref, query_s), (keys_ref, key_s), (values_ref, value_s)]
+        )
+    ]
+    for copy in copies:
+        copy.start()
+    line = lax.broadcasted_iota(jnp.int32, (AUX, rows), 0)
+    flags = jnp.where(line == 1, mask_ref[...].reshape(1, rows), labels_ref[...].reshape(1, rows))
+    flags = jnp.where(line == 0, segments_ref[...].reshape(1, rows), flags)
+    flags = flags.astype(jnp.float32).astype(jnp.bfloat16)
+    for h in range(2 * kv_heads):
+        message_s[h, 2 * rows :, :] = flags
+
+    def send(n, first, last):
+        part = (slice(None), slice(first, last))
+        return pltpu.make_async_copy(message_s.at[part], message_ref.at[part], out_sems.at[n])
+
+    copies[0].wait()
+    message_s[:, :rows, :] = jnp.swapaxes(query_s[...], 0, 1)
+    first = send(0, 0, rows)
+    first.start()
+    copies[1].wait()
+    keys = jnp.swapaxes(key_s[...], 0, 1)
+    copies[2].wait()
+    values = jnp.swapaxes(value_s[...], 0, 1)
+    for h in range(kv_heads):
+        message_s[2 * h, rows : 2 * rows, :] = keys[h]
+        message_s[2 * h + 1, rows : 2 * rows, :] = values[h]
+    second = send(1, rows, 2 * rows + AUX)
+    second.start()
+    first.wait()
+    second.wait()
+
+
+def pack(segments, loss_mask, labels, queries, keys, values):
+    rows, heads, depth = queries.shape
+    shape = (heads, 2 * rows + AUX, depth)
+    return pl.pallas_call(
+        pack_kernel,
+        out_shape=jax.ShapeDtypeStruct(shape, jnp.bfloat16),
+        in_specs=[VMEM] * 3 + [ANY] * 3,
+        out_specs=ANY,
+        scratch_shapes=[
+            pltpu.VMEM(queries.shape, jnp.bfloat16),
+            pltpu.VMEM(keys.shape, jnp.bfloat16),
+            pltpu.VMEM(values.shape, jnp.bfloat16),
+            pltpu.VMEM(shape, jnp.bfloat16),
+            pltpu.SemaphoreType.DMA((3,)),
+            pltpu.SemaphoreType.DMA((2,)),
+        ],
+        compiler_params=pltpu.CompilerParams(vmem_limit_bytes=60 << 20),
+        name="pack",
+    )(segments, loss_mask, labels, queries, keys, values)
+
+
+def unpack_kernel(home_ref, query_ref, key_ref, value_ref):
+    rows = query_ref.shape[0]
+    heads = home_ref.shape[0]
+    query_ref[...] = jnp.swapaxes(home_ref[:, :rows, :], 0, 1)
+    for parity, target in enumerate((key_ref, value_ref)):
+        parts = [home_ref[h : h + 1, rows:, :] for h in range(parity, heads, 2)]
+        target[...] = jnp.swapaxes(jnp.concatenate(parts, axis=0), 0, 1)
+
+
+def unpack(home, queries, keys, values):
+    return pl.pallas_call(
+        unpack_kernel,
+        out_shape=tuple(jax.ShapeDtypeStruct(a.shape, a.dtype) for a in (queries, keys, values)),
+        in_specs=[VMEM],
+        out_specs=(VMEM,) * 3,
+        compiler_params=pltpu.CompilerParams(vmem_limit_bytes=24 << 20),
+        name="unpack",
+    )(home)
+
+
 def local(queries, keys, values, grad_out, readout, segments, loss_mask, labels):
     rows, heads, depth = queries.shape
     devices = lax.axis_size("context")
@@ -321,17 +404,7 @@
     def swap(array):
         return lax.ppermute(array, "context", pairs)
 
-    pair = jnp.stack([keys, values], axis=2).reshape(rows, heads, depth)
-    flags = jnp.stack([segments, loss_mask, labels]).astype(bf16)
-    flags = jnp.pad(flags, ((0, AUX - 3), (0, 0)))
-    message = jnp.concatenate(
-        [
-            jnp.transpose(queries, (1, 0, 2)),
-            jnp.transpose(pair, (1, 0, 2)),
-            jnp.broadcast_to(flags[None], (heads, AUX, depth)),
-        ],
-        axis=1,
-    )
+    message = pack(segments, loss_mask, labels, queries, keys, values)
     message = exchange(message)
     later, message = lax.optimization_barrier((jnp.transpose(grad_out, (1, 0, 2)), message))
     grad = exchange(later)
@@ -367,8 +440,7 @@
             back.astype(f32), ((heads - blocks, 0), (0, 0), (0, 0))
         )
     home = exchange(jnp.concatenate([query_grad, total.astype(bf16)], axis=1))
-    home = jnp.transpose(home, (1, 0, 2))
-    return home[:rows], home[rows:, 0::2], home[rows:, 1::2]
+    return unpack(home, queries, keys, values)
 
 
 def solution(mesh):

time: 107 us -> 104 us (0.972)
  local copies, waits for them, and re-layouts: 5.86 us -> 1.13 us
  Pallas kernels: 11.2 us -> 15.2 us
  other arithmetic: 2.13 us -> 0.26 us
    unnamed x17 -> x5, local copies, waits for them, and re-layouts: 5.49 us -> 0.94 us
    pallas_call x0 -> x2, Pallas kernels: none -> 4 us  [the longest x1 2.95 us: pack(): pl.pallas_call(pack_kernel, out_shape=jax.ShapeDtypeStruct(shape, jnp.bfl...]
    concatenate x1 -> x0, other arithmetic: 1.09 us -> none  [local(): jnp.concatenate([jnp.transpose(queries, (1, 0, 2)), jnp.transpose(pair, (...]
where the time goes in v5:
time: 104 us; the launch traced here: 102 us
  waiting for transfers between devices  32.3 us (31%)
  blocking collectives  31.2 us (30%)
  starting transfers between devices  21.5 us (21%)
  Pallas kernels  15.2 us (15%)
  local copies, waits for them, and re-layouts  1.13 us (1%)
    all_to_all x1, blocking collectives, exchange(): lax.all_to_all(array, 'context', 0, 0, tiled=True, axis_index_groups=clus...  31.2 us
    all_to_all x2, waiting for transfers between devices, exchange(): lax.all_to_all(array, 'context', 0, 0, tiled=True, axis_index_groups=clus...  22.8 us
    all_to_all x2, starting transfers between devices, exchange(): lax.all_to_all(array, 'context', 0, 0, tiled=True, axis_index_groups=clus...  14.2 us
    pallas_call x1, Pallas kernels, attention_backward(): pl.pallas_call(functools.partial(backward_kernel, halo), out_shape=(jax.S...  6.96 us
    ppermute x4, waiting for transfers between devices, local(): lax.ppermute(reward, 'context', [(i, i ^ step) for i in range(devices)])  6.25 us
    ppermute x4, starting transfers between devices, local(): lax.ppermute(reward, 'context', [(i, i ^ step) for i in range(devices)])  4.88 us
    pallas_call x1, Pallas kernels, attention_forward(): pl.pallas_call(functools.partial(forward_kernel, halo), out_shape=(jax.Sh...  4.2 us
    ppermute x2, waiting for transfers between devices, swap(): return lax.ppermute(array, 'context', pairs)  3.19 us
  transfers between devices with their start and end apart: 8, of which 7 were waited for; matrix products, arithmetic and copies ran while one was open for 1% of the time, Pallas kernels for 4%

profile of v5, /device:TPU:1, one launch (start us, length us, event | category | flops | bytes accessed | tf_op | source)
XLA Modules:
  0.0 102.2 jit_solution(10026263064176219665)
XLA Ops:
  0.6 3.0 %pack.1 = bf16[16,264,128]{2,1,0:T(8,128)(2,1)} custom-call(s32[128]{0:T(128)} %segments_ref.1, s32[128]{0:T(128)} %mask_ref.1, s32[128]{0:T(128)} %labels_ref.1, bf16[128,16,128]{2,1,0:T(8,128)(2,1)} %queries_ref.1, bf16[128,8,128]{2,1,0:T(8,128)(2,1)} %keys_ref.1, bf16[128,8,128]{2,1,0:T(8,128)(2,1)} %values_ref.1), custom_call_target="tpu_custom_call" | custom-call | tf_op jit(solution)/shard_map/pack/pallas_call | solution.py:351
  3.6 0.0 copy-start.1
  3.6 7.5 %all-to-all-start = ((bf16[16,264,128]{2,1,0:T(8,128)(2,1)}), bf16[16,264,128]{2,1,0:T(8,128)(2,1)S(1)}, u32[]{:S(2)}, u32[]{:S(2)}) async-start(bf16[16,264,128]{2,1,0:T(8,128)(2,1)} %pack.1), calls=%async_computation | async-start | bytes 2162688 | tf_op jit(solution)/shard_map/all_to_all | solution.py:400
  11.1 0.0 copy-done.1
  11.1 0.9 copy.24
  12.0 22.8 %all-to-all-done.message_ref = bf16[16,264,128]{2,1,0:T(8,128)(2,1)S(1)} async-done(((bf16[16,264,128]{2,1,0:T(8,128)(2,1)}), bf16[16,264,128]{2,1,0:T(8,128)(2,1)S(1)}, u32[]{:S(2)}, u32[]{:S(2)}) %all-to-all-start) | async-done | bytes 1081376 | tf_op jit(solution)/shard_map/all_to_all | solution.py:400
  34.9 6.7 %all-to-all-start.1 = ((bf16[16,128,128]{2,1,0:T(8,128)(2,1)}), bf16[16,128,128]{2,1,0:T(8,128)(2,1)S(1)}, u32[]{:S(2)}, u32[]{:S(2)}) async-start(bf16[16,128,128]{2,1,0:T(8,128)(2,1)} %bitcast.12), calls=%async_computation.1 | async-start | bytes 1048576 | tf_op jit(solution)/shard_map/all_to_all | solution.py:400
  41.7 0.2 collective-permute-start
  41.8 0.0 copy-start
  41.8 0.1 copy.20
  42.0 1.6 %collective-permute-done.other_ref = bf16[16,128,128]{2,1,0:T(8,128)(2,1)S(1)} collective-permute-done((bf16[16,128,128]{2,1,0:T(8,128)(2,1)S(1)}, bf16[16,128,128]{2,1,0:T(8,128)(2,1)S(1)}, u32[]{:S(2)}, u32[]{:S(2)}) %collective-permute-start) | collective-permute-done | bytes 524320 | tf_op jit(solution)/shard_map/ppermute | solution.py:405
  43.6 0.0 copy-done
  43.6 4.2 %attention_forward.1 = (f32[4,512]{1,0:T(4,128)S(1)}, f32[16,128]{1,0:T(8,128)S(1)}, s32[4]{0:T(128)S(1)}) custom-call(s32[1]{0:T(128)} %bitcast.index_ref, bf16[16,264,128]{2,1,0:T(8,128)(2,1)S(1)} %all-to-all-done.message_ref, bf16[16,128,128]{2,1,0:T(8,128)(2,1)S(1)} %slice.16.own_ref, bf16[16,128,128]{2,1,0:T(8,128)(2,1)S(1)} %collective-permute-done.other_ref, ...), custom_call_target="tpu_custom_call" | custom-call | flops 1610612736 | bytes 16777216 | tf_op jit(solution)/shard_map/attention_forward/pallas_call | solution.py:251
  47.9 0.2 collective-permute-start.1
  48.0 1.1 %collective-permute-done.1 = f32[16,128]{1,0:T(8,128)S(1)} collective-permute-done((f32[16,128]{1,0:T(8,128)S(1)}, f32[16,128]{1,0:T(8,128)S(1)}, u32[]{:S(2)}, u32[]{:S(2)}) %collective-permute-start.1) | collective-permute-done | bytes 8224 | tf_op jit(solution)/shard_map/ppermute | solution.py:429
  49.1 1.4 %collective-permute-start.2 = (f32[16,128]{1,0:T(8,128)S(1)}, f32[16,128]{1,0:T(8,128)S(1)}, u32[]{:S(2)}, u32[]{:S(2)}) collective-permute-start(f32[16,128]{1,0:T(8,128)S(1)} %add.15), channel_id=1, source_target_pairs={{0,2},{1,3},{2,0},{3,1},{4,6},{5,7},{6,4},{7,5},{8,10},{9,11},{10,... | collective-permute-start | bytes 24584 | tf_op jit(solution)/shard_map/ppermute | solution.py:429
  50.5 1.5 %collective-permute-done.2 = f32[16,128]{1,0:T(8,128)S(1)} collective-permute-done((f32[16,128]{1,0:T(8,128)S(1)}, f32[16,128]{1,0:T(8,128)S(1)}, u32[]{:S(2)}, u32[]{:S(2)}) %collective-permute-start.2) | collective-permute-done | bytes 8224 | tf_op jit(solution)/shard_map/ppermute | solution.py:429
  52.0 2.2 %collective-permute-start.3 = (f32[16,128]{1,0:T(8,128)S(1)}, f32[16,128]{1,0:T(8,128)S(1)}, u32[]{:S(2)}, u32[]{:S(2)}) collective-permute-start(f32[16,128]{1,0:T(8,128)S(1)} %add.16), channel_id=1, source_target_pairs={{0,4},{1,5},{2,6},{3,7},{4,0},{5,1},{6,2},{7,3},{8,12},{9,13},{10,... | collective-permute-start | bytes 24584 | tf_op jit(solution)/shard_map/ppermute | solution.py:429
  54.2 1.4 %collective-permute-done.3 = f32[16,128]{1,0:T(8,128)S(1)} collective-permute-done((f32[16,128]{1,0:T(8,128)S(1)}, f32[16,128]{1,0:T(8,128)S(1)}, u32[]{:S(2)}, u32[]{:S(2)}) %collective-permute-start.3) | collective-permute-done | bytes 8224 | tf_op jit(solution)/shard_map/ppermute | solution.py:429
  55.6 1.1 %collective-permute-start.4 = (f32[16,128]{1,0:T(8,128)S(1)}, f32[16,128]{1,0:T(8,128)S(1)}, u32[]{:S(2)}, u32[]{:S(2)}) collective-permute-start(f32[16,128]{1,0:T(8,128)S(1)} %add.17), channel_id=1, source_target_pairs={{0,8},{1,9},{2,10},{3,11},{4,12},{5,13},{6,14},{7,15},{8,0},{9,1},... | collective-permute-start | bytes 24584 | tf_op jit(solution)/shard_map/ppermute | solution.py:429
  56.7 2.3 %collective-permute-done.4 = f32[16,128]{1,0:T(8,128)S(1)} collective-permute-done((f32[16,128]{1,0:T(8,128)S(1)}, f32[16,128]{1,0:T(8,128)S(1)}, u32[]{:S(2)}, u32[]{:S(2)}) %collective-permute-start.4) | collective-permute-done | bytes 8224 | tf_op jit(solution)/shard_map/ppermute | solution.py:429
  59.0 0.0 all-to-all-done.1.grad_ref
  59.0 7.0 %attention_backward.1 = (bf16[16,128,128]{2,1,0:T(8,128)(2,1)S(1)}, bf16[16,128,128]{2,1,0:T(8,128)(2,1)S(1)}, bf16[16,128,128]{2,1,0:T(8,128)(2,1)S(1)}) custom-call(s32[1]{0:T(128)} %bitcast.index_ref, s32[4]{0:T(128)S(1)} %get-tuple-element.12.starts_ref, bf16[16,264,128]{2,1,0:T(8,128)(2,1)S(1)} %all-to-all-done.message_ref, ...), custom_call_target="tpu_custom_call" | custom-call | flops 4026531840 | bytes 16777216 | tf_op jit(solution)/shard_map/attention_backward/pallas_call | solution.py:279
  66.0 2.2 %collective-permute-start.5 = (bf16[16,128,128]{2,1,0:T(8,128)(2,1)S(1)}, bf16[16,128,128]{2,1,0:T(8,128)(2,1)S(1)}, u32[]{:S(2)}, u32[]{:S(2)}) collective-permute-start(bf16[16,128,128]{2,1,0:T(8,128)(2,1)S(1)} %get-tuple-element.18), channel_id=1, source_target_pairs={{0,1},{1,0},{2,3},{3,2},{4,5},{5,4},{6,7},{7,6},{8,9},{9,8},{10,11... | collective-permute-start | bytes 1572872 | tf_op jit(solution)/shard_map/ppermute | solution.py:405
  68.2 1.5 %collective-permute-done.5 = bf16[16,128,128]{2,1,0:T(8,128)(2,1)S(1)} collective-permute-done((bf16[16,128,128]{2,1,0:T(8,128)(2,1)S(1)}, bf16[16,128,128]{2,1,0:T(8,128)(2,1)S(1)}, u32[]{:S(2)}, u32[]{:S(2)}) %collective-permute-start.5) | collective-permute-done | bytes 524320 | tf_op jit(solution)/shard_map/ppermute | solution.py:405
  69.7 0.1 add_convert_fusion
  69.9 0.1 pad_maximum_fusion
  70.0 31.2 %all_to_all.15.home_ref = bf16[16,256,128]{2,1,0:T(8,128)(2,1)S(1)} all-to-all(bf16[16,256,128]{2,1,0:T(8,128)(2,1)S(1)} %pad_maximum_fusion), channel_id=1, replica_groups=mesh['groups'=2,'context'=16] {'context'}, dimensions={0} | all-to-all | bytes 2097152 | tf_op jit(solution)/shard_map/all_to_all | solution.py:400
  101.1 1.0 %unpack.1 = (bf16[128,16,128]{2,1,0:T(8,128)(2,1)}, bf16[128,8,128]{2,1,0:T(8,128)(2,1)}, bf16[128,8,128]{2,1,0:T(8,128)(2,1)}) custom-call(bf16[16,256,128]{2,1,0:T(8,128)(2,1)S(1)} %all_to_all.15.home_ref), custom_call_target="tpu_custom_call" | custom-call | tf_op jit(solution)/shard_map/unpack/pallas_call | solution.py:379
  (7 shorter events, 0.1 us)
Async XLA Ops:
  3.6 7.5 %copy-start.1 = (bf16[128,16,128]{2,1,0:T(8,128)(2,1)S(1)}, bf16[128,16,128]{2,1,0:T(8,128)(2,1)}, u32[]{:S(2)}) copy-start(bf16[128,16,128]{2,1,0:T(8,128)(2,1)} %param.11) | copy-start | bytes 1572868
  3.6 31.3 %all-to-all-start = ((bf16[16,264,128]{2,1,0:T(8,128)(2,1)}), bf16[16,264,128]{2,1,0:T(8,128)(2,1)S(1)}, u32[]{:S(2)}, u32[]{:S(2)}) async-start(bf16[16,264,128]{2,1,0:T(8,128)(2,1)} %pack.1), calls=%async_computation | async-start | bytes 2162688 | tf_op jit(solution)/shard_map/all_to_all | solution.py:400
  34.9 24.1 %all-to-all-start.1 = ((bf16[16,128,128]{2,1,0:T(8,128)(2,1)}), bf16[16,128,128]{2,1,0:T(8,128)(2,1)S(1)}, u32[]{:S(2)}, u32[]{:S(2)}) async-start(bf16[16,128,128]{2,1,0:T(8,128)(2,1)} %bitcast.12), calls=%async_computation.1 | async-start | bytes 1048576 | tf_op jit(solution)/shard_map/all_to_all | solution.py:400
  41.7 2.0 %collective-permute-start = (bf16[16,128,128]{2,1,0:T(8,128)(2,1)S(1)}, bf16[16,128,128]{2,1,0:T(8,128)(2,1)S(1)}, u32[]{:S(2)}, u32[]{:S(2)}) collective-permute-start(bf16[16,128,128]{2,1,0:T(8,128)(2,1)S(1)} %slice.16.own_ref), channel_id=1, source_target_pairs={{0,1},{1,0},{2,3},{3,2},{4,5},{5,4},{6,7},{7,6},{8,9},{9,8},{10,11... | collective-permute-start | bytes 1572872 | tf_op jit(solution)/shard_map/ppermute | solution.py:405
  41.8 1.8 %copy-start = (f32[16,128]{1,0:T(8,128)S(1)}, f32[16,128]{1,0:T(8,128)}, u32[]{:S(2)}) copy-start(f32[16,128]{1,0:T(8,128)} %readout_ref.3) | copy-start | bytes 24580
  47.9 1.2 %collective-permute-start.1 = (f32[16,128]{1,0:T(8,128)S(1)}, f32[16,128]{1,0:T(8,128)S(1)}, u32[]{:S(2)}, u32[]{:S(2)}) collective-permute-start(f32[16,128]{1,0:T(8,128)S(1)} %get-tuple-element.14), channel_id=1, source_target_pairs={{0,1},{1,0},{2,3},{3,2},{4,5},{5,4},{6,7},{7,6},{8,9},{9,8},{10,11... | collective-permute-start | bytes 24584 | tf_op jit(solution)/shard_map/ppermute | solution.py:429
  49.1 2.9 %collective-permute-start.2 = (f32[16,128]{1,0:T(8,128)S(1)}, f32[16,128]{1,0:T(8,128)S(1)}, u32[]{:S(2)}, u32[]{:S(2)}) collective-permute-start(f32[16,128]{1,0:T(8,128)S(1)} %add.15), channel_id=1, source_target_pairs={{0,2},{1,3},{2,0},{3,1},{4,6},{5,7},{6,4},{7,5},{8,10},{9,11},{10,... | collective-permute-start | bytes 24584 | tf_op jit(solution)/shard_map/ppermute | solution.py:429
  52.0 3.6 %collective-permute-start.3 = (f32[16,128]{1,0:T(8,128)S(1)}, f32[16,128]{1,0:T(8,128)S(1)}, u32[]{:S(2)}, u32[]{:S(2)}) collective-permute-start(f32[16,128]{1,0:T(8,128)S(1)} %add.16), channel_id=1, source_target_pairs={{0,4},{1,5},{2,6},{3,7},{4,0},{5,1},{6,2},{7,3},{8,12},{9,13},{10,... | collective-permute-start | bytes 24584 | tf_op jit(solution)/shard_map/ppermute | solution.py:429
  55.6 3.4 %collective-permute-start.4 = (f32[16,128]{1,0:T(8,128)S(1)}, f32[16,128]{1,0:T(8,128)S(1)}, u32[]{:S(2)}, u32[]{:S(2)}) collective-permute-start(f32[16,128]{1,0:T(8,128)S(1)} %add.17), channel_id=1, source_target_pairs={{0,8},{1,9},{2,10},{3,11},{4,12},{5,13},{6,14},{7,15},{8,0},{9,1},... | collective-permute-start | bytes 24584 | tf_op jit(solution)/shard_map/ppermute | solution.py:429
  66.0 3.8 %collective-permute-start.5 = (bf16[16,128,128]{2,1,0:T(8,128)(2,1)S(1)}, bf16[16,128,128]{2,1,0:T(8,128)(2,1)S(1)}, u32[]{:S(2)}, u32[]{:S(2)}) collective-permute-start(bf16[16,128,128]{2,1,0:T(8,128)(2,1)S(1)} %get-tuple-element.18), channel_id=1, source_target_pairs={{0,1},{1,0},{2,3},{3,2},{4,5},{5,4},{6,7},{7,6},{8,9},{9,8},{10,11... | collective-permute-start | bytes 1572872 | tf_op jit(solution)/shard_map/ppermute | solution.py:405

commit v6 on v5

--- a/solution.py
+++ b/solution.py
@@ -14,6 +14,7 @@
 NEGATIVE = -1e30
 BLOCK = 256
 AUX = 8
+SEGMENT, MASK, LABEL = 3, 4, 5
 QUERIES = 2 * BLOCK
 REACH = (WINDOW + QUERIES) // BLOCK
 VMEM = pl.BlockSpec(memory_space=pltpu.VMEM)
@@ -72,44 +73,31 @@
     return jnp.concatenate([whole[:, :BLOCK], combine(whole[:, BLOCK:], parts[-1])], axis=1)
 
 
+def place(even, own_ref, other_ref, put):
+    def both(first, second):
+        for n in range(first.shape[0]):
+            put(n, jnp.concatenate([first[n], second[n]], axis=0))
+
+    pl.when(even)(lambda: both(own_ref, other_ref))
+    pl.when(jnp.logical_not(even))(lambda: both(other_ref, own_ref))
+
+
 def forward_kernel(
-    halo, index_ref, message_ref, own_ref, other_ref, seg_ref, readout_ref,
+    halo, index_ref, message_ref, own_ref, other_ref, seg_ref, lines_ref,
     total_ref, reward_ref, starts_ref,
     key_s, side_s, bound_s,
 ):
-    heads, tokens = message_ref.shape[0], message_ref.shape[0] * 128
-    key_blocks = own_ref.shape[0]
+    tokens = message_ref.shape[0] * 128
     shift = halo // BLOCK
-    index = index_ref[0]
-    head = lax.rem(index, heads)
-    even = lax.rem(index, 2) == 0
+    even = lax.rem(index_ref[0], 2) == 0
     low_bits = jnp.bfloat16
-
-    weights = jnp.broadcast_to(readout_ref[pl.ds(head, 1), :], (8, 128))
-    part = lax.broadcasted_iota(jnp.int32, (8, 128), 0)
-    high = weights.astype(low_bits).astype(jnp.float32)
-    middle = (weights - high).astype(low_bits).astype(jnp.float32)
-    rest = weights - high - middle
-    split = jnp.where(part == 0, high, jnp.where(part == 1, middle, rest))
-    split = jnp.where(part < 3, split, 0.0).astype(low_bits)
-    side = lax.broadcasted_iota(jnp.int32, (8, 128), 0)
-
-    def place(keys, values):
-        for s in range(key_blocks):
-            key_s[s * 128 : (s + 1) * 128, :] = keys[s]
-            worth = jnp.sum(dot(split, values[s], NT), axis=0, keepdims=True)
-            worth_high = worth.astype(low_bits).astype(jnp.float32)
-            lines = jnp.where(side == 0, worth_high, jnp.where(side == 1, worth - worth_high, 0.0))
-            side_s[:, s * 128 : (s + 1) * 128] = jnp.where(side == 2, 1.0, lines).astype(low_bits)
-
-    @pl.when(even)
-    def _():
-        place(own_ref, other_ref)
-
-    @pl.when(jnp.logical_not(even))
-    def _():
-        place(other_ref, own_ref)
-
+    for n in range(lines_ref.shape[0]):
+        side_s[:, n * 128 : (n + 1) * 128] = lines_ref[n]
+
+    def put(n, keys):
+        key_s[n * 128 : (n + 1) * 128, :] = keys
+
+    place(even, own_ref, other_ref, put)
     starts = starts_of(seg_ref[...])
     for n, start in enumerate(starts):
         starts_ref[n] = start
@@ -147,38 +135,33 @@
 
 
 def backward_kernel(
-    halo, index_ref, starts_ref, message_ref, own_ref, other_ref, grad_ref, readout_ref, reward_ref,
-    flag_ref, total_ref,
+    halo, index_ref, starts_ref, message_ref, own_ref, other_ref, later_ref, own_value_ref,
+    other_value_ref, readout_ref, reward_ref, flag_ref, total_ref,
     query_ref, keep_ref, send_ref,
     key_s, turned_s, value_s, grad_s, bound_s, key_grad_s, value_grad_s,
 ):
     heads, tokens = message_ref.shape[0], message_ref.shape[0] * 128
-    key_blocks = own_ref.shape[0]
     shift = halo // BLOCK
     index = index_ref[0]
     head = lax.rem(index, heads)
     even = lax.rem(index, 2) == 0
 
-    def place(keys, values):
-        for s in range(key_blocks):
-            key_s[s * 128 : (s + 1) * 128, :] = keys[s]
-            turned_s[:, s * 128 : (s + 1) * 128] = keys[s].T
-            value_s[s * 128 : (s + 1) * 128, :] = values[s]
-
-    @pl.when(even)
-    def _():
-        place(own_ref, other_ref)
-
-    @pl.when(jnp.logical_not(even))
-    def _():
-        place(other_ref, own_ref)
+    def put_key(n, keys):
+        key_s[n * 128 : (n + 1) * 128, :] = keys
+        turned_s[:, n * 128 : (n + 1) * 128] = keys.T
+
+    def put_value(n, values):
+        value_s[n * 128 : (n + 1) * 128, :] = values
+
+    place(even, own_ref, other_ref, put_key)
+    place(even, own_value_ref, other_value_ref, put_value)
 
     live = flag_ref[0]
     probe = live * (jax.nn.sigmoid(reward_ref[...]) - flag_ref[1])
     live_t, probe_t = live.T, probe.T
     weights = readout_ref[pl.ds(head, 1), :]
     for s in range(heads):
-        grad = live_t[:, s : s + 1] * grad_ref[s].astype(jnp.float32)
+        grad = live_t[:, s : s + 1] * later_ref[s, 0:128, :].astype(jnp.float32)
         grad_s[s] = (grad + probe_t[:, s : s + 1] * weights).astype(jnp.bfloat16)
 
     starts = [starts_ref[n] for n in range(4)]
@@ -244,15 +227,15 @@
         send_ref[...] = (key_grad_s[...] * SCALE).astype(jnp.bfloat16).reshape(shape)
 
 
-def attention_forward(halo, where, message, own, other, seg, readout):
+def attention_forward(halo, where, message, own, other, seg, lines):
     heads, depth = message.shape[0], message.shape[2]
-    key_tokens = own.shape[0] * own.shape[1]
+    key_tokens = own.shape[0] * 128
     count = message.shape[0] * 128 // QUERIES
     return pl.pallas_call(
         functools.partial(forward_kernel, halo),
         out_shape=(
             jax.ShapeDtypeStruct((count, QUERIES), jnp.float32),
-            jax.ShapeDtypeStruct((heads, own.shape[1]), jnp.float32),
+            jax.ShapeDtypeStruct((heads, 128), jnp.float32),
             jax.ShapeDtypeStruct((4,), jnp.int32),
         ),
         in_specs=[SMEM] + [VMEM] * 5,
@@ -269,27 +252,29 @@
             transcendentals=BLOCK * QUERIES * count * REACH,
         ),
         name="attention_forward",
-    )(where, message, own, other, seg, readout)
-
-
-def attention_backward(halo, where, starts, message, own, other, grad, readout, reward, flag, total):
+    )(where, message, own, other, seg, lines)
+
+
+def attention_backward(
+    halo, where, starts, message, own, other, later, own_value, other_value, readout, reward, flag, total
+):
     heads, depth = message.shape[0], message.shape[2]
-    key_tokens = own.shape[0] * own.shape[1]
+    key_tokens = own.shape[0] * 128
     count = message.shape[0] * 128 // QUERIES
     return pl.pallas_call(
         functools.partial(backward_kernel, halo),
         out_shape=(
-            jax.ShapeDtypeStruct(grad.shape, jnp.bfloat16),
-            jax.ShapeDtypeStruct(own.shape, jnp.bfloat16),
-            jax.ShapeDtypeStruct(own.shape, jnp.bfloat16),
+            jax.ShapeDtypeStruct((heads, 128, depth), jnp.bfloat16),
+            jax.ShapeDtypeStruct((own.shape[0], 128, depth), jnp.bfloat16),
+            jax.ShapeDtypeStruct((own.shape[0], 128, depth), jnp.bfloat16),
         ),
-        in_specs=[SMEM, SMEM] + [VMEM] * 8,
+        in_specs=[SMEM, SMEM] + [VMEM] * 10,
         out_specs=(VMEM, VMEM, VMEM),
         scratch_shapes=[
             pltpu.VMEM((key_tokens, depth), jnp.bfloat16),
             pltpu.VMEM((depth, key_tokens), jnp.bfloat16),
             pltpu.VMEM((key_tokens, depth), jnp.bfloat16),
-            pltpu.VMEM(grad.shape, jnp.bfloat16),
+            pltpu.VMEM((heads, 128, depth), jnp.bfloat16),
             pltpu.VMEM((count, QUERIES), jnp.int32),
             pltpu.VMEM((key_tokens, depth), jnp.float32),
             pltpu.VMEM((key_tokens, depth), jnp.float32),
@@ -301,69 +286,116 @@
             transcendentals=0,
         ),
         name="attention_backward",
-    )(where, starts, message, own, other, grad, readout, reward, flag, total)
+    )(
+        where, starts, message, own, other, later, own_value, other_value,
+        readout, reward, flag, total,
+    )
+
+
+def halves_into(target, start, heads):
+    half = heads.shape[1] // 2
+    for h in range(2 * heads.shape[0]):
+        part = h % 2 * half
+        target[h, start : start + half, :] = heads[h // 2, part : part + half]
 
 
 def pack_kernel(
-    segments_ref, mask_ref, labels_ref, queries_ref, keys_ref, values_ref,
-    message_ref, query_s, key_s, value_s, message_s, in_sems, out_sems,
+    readout_ref, segments_ref, mask_ref, labels_ref, queries_ref, keys_ref, values_ref,
+    message_ref, segments_s, mask_s, labels_s, query_s, key_s, value_s, message_s, in_sems, out_sems,
 ):
     rows, kv_heads = keys_ref.shape[:2]
+    pairs = [
+        (values_ref, value_s), (keys_ref, key_s), (queries_ref, query_s),
+        (segments_ref, segments_s), (mask_ref, mask_s), (labels_ref, labels_s),
+    ]
     copies = [
         pltpu.make_async_copy(source, target, in_sems.at[n])
-        for n, (source, target) in enumerate(
-            [(queries_ref, query_s), (keys_ref, key_s), (values_ref, value_s)]
-        )
+        for n, (source, target) in enumerate(pairs)
     ]
     for copy in copies:
         copy.start()
-    line = lax.broadcasted_iota(jnp.int32, (AUX, rows), 0)
-    flags = jnp.where(line == 1, mask_ref[...].reshape(1, rows), labels_ref[...].reshape(1, rows))
-    flags = jnp.where(line == 0, segments_ref[...].reshape(1, rows), flags)
-    flags = flags.astype(jnp.float32).astype(jnp.bfloat16)
-    for h in range(2 * kv_heads):
-        message_s[h, 2 * rows :, :] = flags
 
     def send(n, first, last):
         part = (slice(None), slice(first, last))
         return pltpu.make_async_copy(message_s.at[part], message_ref.at[part], out_sems.at[n])
 
+    readout = readout_ref[...]
+    high = readout.astype(jnp.bfloat16).astype(jnp.float32)
+    middle = (readout - high).astype(jnp.bfloat16).astype(jnp.float32)
+    rest = readout - high - middle
+    spare = jnp.zeros((2, readout.shape[1]), jnp.float32)
     copies[0].wait()
+    values = jnp.swapaxes(value_s[...], 0, 1)
+    worths = []
+    for c in range(kv_heads):
+        parts = [p[h : h + 1] for h in (2 * c, 2 * c + 1) for p in (high, middle, rest)]
+        weights = jnp.concatenate(parts + [spare], axis=0).astype(jnp.bfloat16)
+        product = dot(weights, values[c], NT)
+        worths += [product[0:1] + product[1:2] + product[2:3]]
+        worths += [product[3:4] + product[4:5] + product[5:6]]
+    copies[1].wait()
+    halves_into(message_s, rows, jnp.swapaxes(key_s[...], 0, 1))
+    for copy in copies[3:]:
+        copy.wait()
+    line = lax.broadcasted_iota(jnp.int32, (AUX, rows), 0)
+    flags = jnp.ones((AUX, rows), jnp.float32)
+    for n, source in ((SEGMENT, segments_s), (MASK, mask_s), (LABEL, labels_s)):
+        flags = jnp.where(line == n, source[...].reshape(1, rows).astype(jnp.float32), flags)
+    for h, worth in enumerate(worths):
+        worth_high = worth.astype(jnp.bfloat16).astype(jnp.float32)
+        lines = jnp.where(line == 0, worth_high, jnp.where(line == 1, worth - worth_high, flags))
+        message_s[h, rows + rows // 2 :, :] = lines.astype(jnp.bfloat16)
+    first = send(0, rows, rows + rows // 2 + AUX)
+    first.start()
+    copies[2].wait()
     message_s[:, :rows, :] = jnp.swapaxes(query_s[...], 0, 1)
-    first = send(0, 0, rows)
-    first.start()
-    copies[1].wait()
-    keys = jnp.swapaxes(key_s[...], 0, 1)
-    copies[2].wait()
-    values = jnp.swapaxes(value_s[...], 0, 1)
-    for h in range(kv_heads):
-        message_s[2 * h, rows : 2 * rows, :] = keys[h]
-        message_s[2 * h + 1, rows : 2 * rows, :] = values[h]
-    second = send(1, rows, 2 * rows + AUX)
+    second = send(1, 0, rows)
     second.start()
     first.wait()
     second.wait()
 
 
-def pack(segments, loss_mask, labels, queries, keys, values):
+def pack(readout, segments, loss_mask, labels, queries, keys, values):
     rows, heads, depth = queries.shape
-    shape = (heads, 2 * rows + AUX, depth)
+    shape = (heads, rows + rows // 2 + AUX, depth)
     return pl.pallas_call(
         pack_kernel,
         out_shape=jax.ShapeDtypeStruct(shape, jnp.bfloat16),
-        in_specs=[VMEM] * 3 + [ANY] * 3,
+        in_specs=[VMEM] + [ANY] * 6,
         out_specs=ANY,
         scratch_shapes=[
+            pltpu.VMEM(segments.shape, jnp.int32),
+            pltpu.VMEM(segments.shape, jnp.int32),
+            pltpu.VMEM(segments.shape, jnp.int32),
             pltpu.VMEM(queries.shape, jnp.bfloat16),
             pltpu.VMEM(keys.shape, jnp.bfloat16),
             pltpu.VMEM(values.shape, jnp.bfloat16),
             pltpu.VMEM(shape, jnp.bfloat16),
-            pltpu.SemaphoreType.DMA((3,)),
+            pltpu.SemaphoreType.DMA((6,)),
             pltpu.SemaphoreType.DMA((2,)),
         ],
         compiler_params=pltpu.CompilerParams(vmem_limit_bytes=60 << 20),
         name="pack",
-    )(segments, loss_mask, labels, queries, keys, values)
+    )(readout, segments, loss_mask, labels, queries, keys, values)
+
+
+def pack_later_kernel(grad_ref, values_ref, message_ref):
+    rows = grad_ref.shape[0]
+    message_ref[:, :rows, :] = jnp.swapaxes(grad_ref[...], 0, 1)
+    halves_into(message_ref, rows, jnp.swapaxes(values_ref[...], 0, 1))
+
+
+def pack_later(grad_out, values):
+    rows, heads, depth = grad_out.shape
+    return pl.pallas_call(
+        pack_later_kernel,
+        out_shape=jax.ShapeDtypeStruct((heads, rows + rows // 2, depth), jnp.bfloat16),
+        in_specs=[VMEM] * 2,
+        out_specs=VMEM,
+        compiler_params=pltpu.CompilerParams(vmem_limit_bytes=16 << 20),
+        cost_estimate=pl.CostEstimate(flops=0, bytes_accessed=3 << 20, transcendentals=0),
+        name="pack_later",
+    )(grad_out, values)
 
 
 def unpack_kernel(home_ref, query_ref, key_ref, value_ref):
@@ -404,32 +436,40 @@
     def swap(array):
         return lax.ppermute(array, "context", pairs)
 
-    message = pack(segments, loss_mask, labels, queries, keys, values)
-    message = exchange(message)
-    later, message = lax.optimization_barrier((jnp.transpose(grad_out, (1, 0, 2)), message))
-    grad = exchange(later)
-    own = message[:, rows : 2 * rows]
-    other = swap(own)
-    flags = message[:, 2 * rows :]
-    seg = flags[:, 0].astype(jnp.int32)
-    flag = jnp.stack([flags[:, 1], flags[:, 2]]).astype(f32)
+    def split(array):
+        own = array[:, rows : rows + rows // 2]
+        return own, swap(own)
+
+    def from_before(array):
+        if not many:
+            return array
+        ahead = [(i, i + heads) for i in range(devices - heads)]
+        far = lax.ppermute(array[-blocks:], "context", ahead)
+        return jnp.concatenate([far, array], axis=0)
+
+    blocks = halo // rows
+    message = exchange(pack(readout, segments, loss_mask, labels, queries, keys, values))
+    later, message = lax.optimization_barrier((pack_later(grad_out, values), message))
+    later = exchange(later)
+    own, other = split(message)
+    lines = message[:, rows + rows // 2 :]
+    flag = jnp.stack([lines[:, MASK], lines[:, LABEL]]).astype(f32)
+    lines, own, other = from_before(lines), from_before(own), from_before(other)
+    seg = lines[:, SEGMENT].astype(jnp.int32)
     if many:
-        ahead = [(i, i + heads) for i in range(devices - heads)]
-        blocks = halo // rows
-        far = lax.ppermute((own[-blocks:], other[-blocks:], flags[-blocks:, 0]), "context", ahead)
-        own = jnp.concatenate([far[0], own], axis=0)
-        other = jnp.concatenate([far[1], other], axis=0)
-        far_seg = jnp.where(index < heads, -1, far[2].astype(jnp.int32))
-        seg = jnp.concatenate([far_seg, seg], axis=0)
-
+        place_of = jnp.arange(blocks + heads, dtype=jnp.int32)[:, None]
+        seg = jnp.where((index < heads) & (place_of < blocks), -1, seg)
     where = jnp.reshape(index, (1,)).astype(jnp.int32)
-    total, reward, starts = attention_forward(halo, where, message, own, other, seg, readout)
+    total, reward, starts = attention_forward(halo, where, message, own, other, seg, lines)
 
     for step in (1, 2, 4, 8):
         reward = reward + lax.ppermute(reward, "context", [(i, i ^ step) for i in range(devices)])
 
+    later, reward = lax.optimization_barrier((later, reward))
+    own_value, other_value = split(later)
     query_grad, keep, send = attention_backward(
-        halo, where, starts, message, own, other, grad, readout, reward, flag, total
+        halo, where, starts, message, own, other, later, from_before(own_value),
+        from_before(other_value), readout, reward, flag, total,
     )
     total = keep.astype(f32) + swap(send).astype(f32)
     if many:

time: 104 us -> 98.6 us (0.948); the launches traced: 102 us -> 98 us
  waiting for transfers between devices: 32.3 us -> 29.8 us
  blocking collectives: 31.2 us -> 29.3 us
    all_to_all x2, waiting for transfers between devices: 22.8 us -> 18 us  [exchange(): lax.all_to_all(array, 'context', 0, 0, tiled=True, axis_index_groups=clus...]
    ppermute x4, starting transfers between devices: 4.88 us -> 7.19 us  [local(): lax.ppermute(reward, 'context', [(i, i ^ step) for i in range(devices)])]
    all_to_all x1, blocking collectives: 31.2 us -> 29.3 us  [exchange(): lax.all_to_all(array, 'context', 0, 0, tiled=True, axis_index_groups=clus...]
    ppermute x4, waiting for transfers between devices: 6.25 us -> 7.78 us  [local(): lax.ppermute(reward, 'context', [(i, i ^ step) for i in range(devices)])]
    pallas_call x0 -> x1, Pallas kernels: none -> 1.09 us  [pack_later(): pl.pallas_call(pack_later_kernel, out_shape=jax.ShapeDtypeStruct((heads,...]
    ppermute x2 -> x3, waiting for transfers between devices: 3.19 us -> 4.01 us  [swap(): return lax.ppermute(array, 'context', pairs)]
    ppermute x2 -> x3, starting transfers between devices: 2.4 us -> 1.83 us  [swap(): return lax.ppermute(array, 'context', pairs)]
  transfers between devices with their start and end apart: 8 -> 9, of which waited for: 7 -> 8; matrix products, arithmetic and copies ran while one was open for 1% -> 0% of each run, Pallas kernels for 4% -> 5%
where the time goes in v6:
time: 98.6 us; the launch traced here: 98 us
  waiting for transfers between devices  29.8 us (30%)
  blocking collectives  29.3 us (30%)
  starting transfers between devices  22.3 us (23%)
  Pallas kernels  15.5 us (16%)
    all_to_all x1, blocking collectives, exchange(): lax.all_to_all(array, 'context', 0, 0, tiled=True, axis_index_groups=clus...  29.3 us
    all_to_all x2, waiting for transfers between devices, exchange(): lax.all_to_all(array, 'context', 0, 0, tiled=True, axis_index_groups=clus...  18 us
    all_to_all x2, starting transfers between devices, exchange(): lax.all_to_all(array, 'context', 0, 0, tiled=True, axis_index_groups=clus...  13.3 us
    ppermute x4, waiting for transfers between devices, local(): lax.ppermute(reward, 'context', [(i, i ^ step) for i in range(devices)])  7.78 us
    ppermute x4, starting transfers between devices, local(): lax.ppermute(reward, 'context', [(i, i ^ step) for i in range(devices)])  7.19 us
    pallas_call x1, Pallas kernels, attention_backward(): pl.pallas_call(functools.partial(backward_kernel, halo), out_shape=(jax.S...  6.66 us
    ppermute x3, waiting for transfers between devices, swap(): return lax.ppermute(array, 'context', pairs)  4.01 us
    pallas_call x1, Pallas kernels, attention_forward(): pl.pallas_call(functools.partial(forward_kernel, halo), out_shape=(jax.Sh...  3.6 us
  transfers between devices with their start and end apart: 9, of which 8 were waited for; matrix products, arithmetic and copies ran while one was open for 0% of the time, Pallas kernels for 5%

profile of v6, /device:TPU:1, one launch (start us, length us, event | category | flops | bytes accessed | tf_op | source)
XLA Modules:
  0.0 98.0 jit_solution(12661659094702415644)
XLA Ops:
  0.6 3.1 %pack.1 = bf16[16,200,128]{2,1,0:T(8,128)(2,1)} custom-call(f32[16,128]{1,0:T(8,128)} %readout_ref.3, s32[128]{0:T(128)} %segments_ref.1, s32[128]{0:T(128)} %mask_ref.1, s32[128]{0:T(128)} %labels_ref.1, bf16[128,16,128]{2,1,0:T(8,128)(2,1)} %queries_ref.1, bf16[128,8,128]{2,1,0:T(8,128)(2,1)} %keys_ref.1, bf16[128,8,128]{2,1,0:T(8,128)(2,1)} %values_ref.3), custom_call_target="tpu_custom_call" | custom-call | tf_op jit(solution)/shard_map/pack/pallas_call | solution.py:361
  3.7 0.0 copy-start
  3.7 0.0 copy-start.1
  3.7 7.5 %all-to-all-start = ((bf16[16,200,128]{2,1,0:T(8,128)(2,1)}), bf16[16,200,128]{2,1,0:T(8,128)(2,1)S(1)}, u32[]{:S(2)}, u32[]{:S(2)}) async-start(bf16[16,200,128]{2,1,0:T(8,128)(2,1)} %pack.1), calls=%async_computation | async-start | bytes 1638400 | tf_op jit(solution)/shard_map/all_to_all | solution.py:432
  11.2 0.0 copy-done
  11.2 0.0 copy-done.1
  11.2 1.1 %pack_later.1 = bf16[16,192,128]{2,1,0:T(8,128)(2,1)} custom-call(bf16[128,16,128]{2,1,0:T(8,128)(2,1)S(1)} %copy-done.1, bf16[128,8,128]{2,1,0:T(8,128)(2,1)S(1)} %copy-done), custom_call_target="tpu_custom_call" | custom-call | bytes 3145728 | tf_op jit(solution)/shard_map/pack_later/pallas_call | solution.py:390
  12.3 18.0 %all-to-all-done.message_ref = bf16[16,200,128]{2,1,0:T(8,128)(2,1)S(1)} async-done(((bf16[16,200,128]{2,1,0:T(8,128)(2,1)}), bf16[16,200,128]{2,1,0:T(8,128)(2,1)S(1)}, u32[]{:S(2)}, u32[]{:S(2)}) %all-to-all-start) | async-done | bytes 819232 | tf_op jit(solution)/shard_map/all_to_all | solution.py:432
  30.3 5.8 %all-to-all-start.1 = ((bf16[16,192,128]{2,1,0:T(8,128)(2,1)}), bf16[16,192,128]{2,1,0:T(8,128)(2,1)S(1)}, u32[]{:S(2)}, u32[]{:S(2)}) async-start(bf16[16,192,128]{2,1,0:T(8,128)(2,1)} %pack_later.1), calls=%async_computation.1 | async-start | bytes 1572864 | tf_op jit(solution)/shard_map/all_to_all | solution.py:432
  36.1 0.2 collective-permute-start
  36.3 0.1 copy.19
  36.4 1.3 %collective-permute-done.other_ref = bf16[16,64,128]{2,1,0:T(8,128)(2,1)S(1)} collective-permute-done((bf16[16,64,128]{2,1,0:T(8,128)(2,1)S(1)}, bf16[16,64,128]{2,1,0:T(8,128)(2,1)S(1)}, u32[]{:S(2)}, u32[]{:S(2)}) %collective-permute-start) | collective-permute-done | bytes 262176 | tf_op jit(solution)/shard_map/ppermute | solution.py:437
  37.7 3.6 %attention_forward.1 = (f32[4,512]{1,0:T(4,128)S(1)}, f32[16,128]{1,0:T(8,128)S(1)}, s32[4]{0:T(128)S(1)}) custom-call(s32[1]{0:T(128)} %bitcast.index_ref, bf16[16,200,128]{2,1,0:T(8,128)(2,1)S(1)} %all-to-all-done.message_ref, bf16[16,64,128]{2,1,0:T(8,128)(2,1)S(1)} %slice.21.own_ref, bf16[16,64,128]{2,1,0:T(8,128)(2,1)S(1)} %collective-permute-done.other_ref, ...), custom_call_target="tpu_custom_call" | custom-call | flops 1610612736 | bytes 16777216 | tf_op jit(solution)/shard_map/attention_forward/pallas_call | solution.py:234
  41.4 0.2 collective-permute-start.1
  41.6 1.0 %collective-permute-done.1 = f32[16,128]{1,0:T(8,128)S(1)} collective-permute-done((f32[16,128]{1,0:T(8,128)S(1)}, f32[16,128]{1,0:T(8,128)S(1)}, u32[]{:S(2)}, u32[]{:S(2)}) %collective-permute-start.1) | collective-permute-done | bytes 8224 | tf_op jit(solution)/shard_map/ppermute | solution.py:466
  42.6 1.4 %collective-permute-start.2 = (f32[16,128]{1,0:T(8,128)S(1)}, f32[16,128]{1,0:T(8,128)S(1)}, u32[]{:S(2)}, u32[]{:S(2)}) collective-permute-start(f32[16,128]{1,0:T(8,128)S(1)} %add.15), channel_id=1, source_target_pairs={{0,2},{1,3},{2,0},{3,1},{4,6},{5,7},{6,4},{7,5},{8,10},{9,11},{10,... | collective-permute-start | bytes 24584 | tf_op jit(solution)/shard_map/ppermute | solution.py:466
  44.0 1.4 %collective-permute-done.2 = f32[16,128]{1,0:T(8,128)S(1)} collective-permute-done((f32[16,128]{1,0:T(8,128)S(1)}, f32[16,128]{1,0:T(8,128)S(1)}, u32[]{:S(2)}, u32[]{:S(2)}) %collective-permute-start.2) | collective-permute-done | bytes 8224 | tf_op jit(solution)/shard_map/ppermute | solution.py:466
  45.4 1.7 %collective-permute-start.3 = (f32[16,128]{1,0:T(8,128)S(1)}, f32[16,128]{1,0:T(8,128)S(1)}, u32[]{:S(2)}, u32[]{:S(2)}) collective-permute-start(f32[16,128]{1,0:T(8,128)S(1)} %add.16), channel_id=1, source_target_pairs={{0,4},{1,5},{2,6},{3,7},{4,0},{5,1},{6,2},{7,3},{8,12},{9,13},{10,... | collective-permute-start | bytes 24584 | tf_op jit(solution)/shard_map/ppermute | solution.py:466
  47.1 2.4 %collective-permute-done.3 = f32[16,128]{1,0:T(8,128)S(1)} collective-permute-done((f32[16,128]{1,0:T(8,128)S(1)}, f32[16,128]{1,0:T(8,128)S(1)}, u32[]{:S(2)}, u32[]{:S(2)}) %collective-permute-start.3) | collective-permute-done | bytes 8224 | tf_op jit(solution)/shard_map/ppermute | solution.py:466
  49.5 3.8 %collective-permute-start.4 = (f32[16,128]{1,0:T(8,128)S(1)}, f32[16,128]{1,0:T(8,128)S(1)}, u32[]{:S(2)}, u32[]{:S(2)}) collective-permute-start(f32[16,128]{1,0:T(8,128)S(1)} %add.17), channel_id=1, source_target_pairs={{0,8},{1,9},{2,10},{3,11},{4,12},{5,13},{6,14},{7,15},{8,0},{9,1},... | collective-permute-start | bytes 24584 | tf_op jit(solution)/shard_map/ppermute | solution.py:466
  53.4 2.9 %collective-permute-done.4 = f32[16,128]{1,0:T(8,128)S(1)} collective-permute-done((f32[16,128]{1,0:T(8,128)S(1)}, f32[16,128]{1,0:T(8,128)S(1)}, u32[]{:S(2)}, u32[]{:S(2)}) %collective-permute-start.4) | collective-permute-done | bytes 8224 | tf_op jit(solution)/shard_map/ppermute | solution.py:466
  56.3 0.0 all-to-all-done.1.later_ref
  56.4 1.2 %collective-permute-start.5 = (bf16[16,64,128]{2,1,0:T(8,128)(2,1)S(1)}, bf16[16,64,128]{2,1,0:T(8,128)(2,1)S(1)}, u32[]{:S(2)}, u32[]{:S(2)}) collective-permute-start(bf16[16,64,128]{2,1,0:T(8,128)(2,1)S(1)} %slice.24.own_value_ref), channel_id=1, source_target_pairs={{0,1},{1,0},{2,3},{3,2},{4,5},{5,4},{6,7},{7,6},{8,9},{9,8},{10,11... | collective-permute-start | bytes 786440 | tf_op jit(solution)/shard_map/ppermute | solution.py:437
  57.6 1.2 %collective-permute-done.5.other_value_ref = bf16[16,64,128]{2,1,0:T(8,128)(2,1)S(1)} collective-permute-done((bf16[16,64,128]{2,1,0:T(8,128)(2,1)S(1)}, bf16[16,64,128]{2,1,0:T(8,128)(2,1)S(1)}, u32[]{:S(2)}, u32[]{:S(2)}) %collective-permute-start.5) | collective-permute-done | bytes 262176 | tf_op jit(solution)/shard_map/ppermute | solution.py:437
  58.8 0.0 copy-done.2
  58.8 6.7 %attention_backward.1 = (bf16[16,128,128]{2,1,0:T(8,128)(2,1)S(1)}, bf16[16,128,128]{2,1,0:T(8,128)(2,1)S(1)}, bf16[16,128,128]{2,1,0:T(8,128)(2,1)S(1)}) custom-call(s32[1]{0:T(128)} %bitcast.index_ref, s32[4]{0:T(128)S(1)} %get-tuple-element.14.starts_ref, bf16[16,200,128]{2,1,0:T(8,128)(2,1)S(1)} %all-to-all-done.message_ref, ...), custom_call_target="tpu_custom_call" | custom-call | flops 4026531840 | bytes 16777216 | tf_op jit(solution)/shard_map/attention_backward/pallas_call | solution.py:264
  65.4 0.4 collective-permute-start.6
  65.9 1.5 %collective-permute-done.6 = bf16[16,128,128]{2,1,0:T(8,128)(2,1)S(1)} collective-permute-done((bf16[16,128,128]{2,1,0:T(8,128)(2,1)S(1)}, bf16[16,128,128]{2,1,0:T(8,128)(2,1)S(1)}, u32[]{:S(2)}, u32[]{:S(2)}) %collective-permute-start.6) | collective-permute-done | bytes 524320 | tf_op jit(solution)/shard_map/ppermute | solution.py:437
  67.4 0.1 add_convert_fusion
  67.6 0.1 pad_maximum_fusion
  67.7 29.3 %all_to_all.15.home_ref = bf16[16,256,128]{2,1,0:T(8,128)(2,1)S(1)} all-to-all(bf16[16,256,128]{2,1,0:T(8,128)(2,1)S(1)} %pad_maximum_fusion), channel_id=1, replica_groups=mesh['groups'=2,'context'=16] {'context'}, dimensions={0} | all-to-all | bytes 2097152 | tf_op jit(solution)/shard_map/all_to_all | solution.py:432
  96.9 1.0 %unpack.1 = (bf16[128,16,128]{2,1,0:T(8,128)(2,1)}, bf16[128,8,128]{2,1,0:T(8,128)(2,1)}, bf16[128,8,128]{2,1,0:T(8,128)(2,1)}) custom-call(bf16[16,256,128]{2,1,0:T(8,128)(2,1)S(1)} %all_to_all.15.home_ref), custom_call_target="tpu_custom_call" | custom-call | tf_op jit(solution)/shard_map/unpack/pallas_call | solution.py:411
  (10 shorter events, 0.1 us)
Async XLA Ops:
  3.7 7.5 %copy-start = (bf16[128,8,128]{2,1,0:T(8,128)(2,1)S(1)}, bf16[128,8,128]{2,1,0:T(8,128)(2,1)}, u32[]{:S(2)}) copy-start(bf16[128,8,128]{2,1,0:T(8,128)(2,1)} %values_ref.3) | copy-start | bytes 786436
  3.7 7.5 %copy-start.1 = (bf16[128,16,128]{2,1,0:T(8,128)(2,1)S(1)}, bf16[128,16,128]{2,1,0:T(8,128)(2,1)}, u32[]{:S(2)}) copy-start(bf16[128,16,128]{2,1,0:T(8,128)(2,1)} %grad_ref.1) | copy-start | bytes 1572868
  3.7 26.6 %all-to-all-start = ((bf16[16,200,128]{2,1,0:T(8,128)(2,1)}), bf16[16,200,128]{2,1,0:T(8,128)(2,1)S(1)}, u32[]{:S(2)}, u32[]{:S(2)}) async-start(bf16[16,200,128]{2,1,0:T(8,128)(2,1)} %pack.1), calls=%async_computation | async-start | bytes 1638400 | tf_op jit(solution)/shard_map/all_to_all | solution.py:432
  30.3 26.0 %all-to-all-start.1 = ((bf16[16,192,128]{2,1,0:T(8,128)(2,1)}), bf16[16,192,128]{2,1,0:T(8,128)(2,1)S(1)}, u32[]{:S(2)}, u32[]{:S(2)}) async-start(bf16[16,192,128]{2,1,0:T(8,128)(2,1)} %pack_later.1), calls=%async_computation.1 | async-start | bytes 1572864 | tf_op jit(solution)/shard_map/all_to_all | solution.py:432
  36.1 1.6 %collective-permute-start = (bf16[16,64,128]{2,1,0:T(8,128)(2,1)S(1)}, bf16[16,64,128]{2,1,0:T(8,128)(2,1)S(1)}, u32[]{:S(2)}, u32[]{:S(2)}) collective-permute-start(bf16[16,64,128]{2,1,0:T(8,128)(2,1)S(1)} %slice.21.own_ref), channel_id=1, source_target_pairs={{0,1},{1,0},{2,3},{3,2},{4,5},{5,4},{6,7},{7,6},{8,9},{9,8},{10,11... | collective-permute-start | bytes 786440 | tf_op jit(solution)/shard_map/ppermute | solution.py:437
  37.7 21.0 %copy-start.2 = (f32[16,128]{1,0:T(8,128)S(1)}, f32[16,128]{1,0:T(8,128)}, u32[]{:S(2)}) copy-start(f32[16,128]{1,0:T(8,128)} %readout_ref.3) | copy-start | bytes 24580
  41.4 1.2 %collective-permute-start.1 = (f32[16,128]{1,0:T(8,128)S(1)}, f32[16,128]{1,0:T(8,128)S(1)}, u32[]{:S(2)}, u32[]{:S(2)}) collective-permute-start(f32[16,128]{1,0:T(8,128)S(1)} %get-tuple-element.16), channel_id=1, source_target_pairs={{0,1},{1,0},{2,3},{3,2},{4,5},{5,4},{6,7},{7,6},{8,9},{9,8},{10,11... | collective-permute-start | bytes 24584 | tf_op jit(solution)/shard_map/ppermute | solution.py:466
  42.6 2.8 %collective-permute-start.2 = (f32[16,128]{1,0:T(8,128)S(1)}, f32[16,128]{1,0:T(8,128)S(1)}, u32[]{:S(2)}, u32[]{:S(2)}) collective-permute-start(f32[16,128]{1,0:T(8,128)S(1)} %add.15), channel_id=1, source_target_pairs={{0,2},{1,3},{2,0},{3,1},{4,6},{5,7},{6,4},{7,5},{8,10},{9,11},{10,... | collective-permute-start | bytes 24584 | tf_op jit(solution)/shard_map/ppermute | solution.py:466
  45.4 4.1 %collective-permute-start.3 = (f32[16,128]{1,0:T(8,128)S(1)}, f32[16,128]{1,0:T(8,128)S(1)}, u32[]{:S(2)}, u32[]{:S(2)}) collective-permute-start(f32[16,128]{1,0:T(8,128)S(1)} %add.16), channel_id=1, source_target_pairs={{0,4},{1,5},{2,6},{3,7},{4,0},{5,1},{6,2},{7,3},{8,12},{9,13},{10,... | collective-permute-start | bytes 24584 | tf_op jit(solution)/shard_map/ppermute | solution.py:466
  49.5 6.8 %collective-permute-start.4 = (f32[16,128]{1,0:T(8,128)S(1)}, f32[16,128]{1,0:T(8,128)S(1)}, u32[]{:S(2)}, u32[]{:S(2)}) collective-permute-start(f32[16,128]{1,0:T(8,128)S(1)} %add.17), channel_id=1, source_target_pairs={{0,8},{1,9},{2,10},{3,11},{4,12},{5,13},{6,14},{7,15},{8,0},{9,1},... | collective-permute-start | bytes 24584 | tf_op jit(solution)/shard_map/ppermute | solution.py:466
  56.4 2.4 %collective-permute-start.5 = (bf16[16,64,128]{2,1,0:T(8,128)(2,1)S(1)}, bf16[16,64,128]{2,1,0:T(8,128)(2,1)S(1)}, u32[]{:S(2)}, u32[]{:S(2)}) collective-permute-start(bf16[16,64,128]{2,1,0:T(8,128)(2,1)S(1)} %slice.24.own_value_ref), channel_id=1, source_target_pairs={{0,1},{1,0},{2,3},{3,2},{4,5},{5,4},{6,7},{7,6},{8,9},{9,8},{10,11... | collective-permute-start | bytes 786440 | tf_op jit(solution)/shard_map/ppermute | solution.py:437
  65.4 2.0 %collective-permute-start.6 = (bf16[16,128,128]{2,1,0:T(8,128)(2,1)S(1)}, bf16[16,128,128]{2,1,0:T(8,128)(2,1)S(1)}, u32[]{:S(2)}, u32[]{:S(2)}) collective-permute-start(bf16[16,128,128]{2,1,0:T(8,128)(2,1)S(1)} %get-tuple-element.22), channel_id=1, source_target_pairs={{0,1},{1,0},{2,3},{3,2},{4,5},{5,4},{6,7},{7,6},{8,9},{9,8},{10,11... | collective-permute-start | bytes 1572872 | tf_op jit(solution)/shard_map/ppermute | solution.py:437

commit v7 on v6

--- a/solution.py
+++ b/solution.py
@@ -301,11 +301,12 @@
 
 def pack_kernel(
     readout_ref, segments_ref, mask_ref, labels_ref, queries_ref, keys_ref, values_ref,
-    message_ref, segments_s, mask_s, labels_s, query_s, key_s, value_s, message_s, in_sems, out_sems,
+    message_ref, readout_s, segments_s, mask_s, labels_s, query_s, key_s, value_s, message_s,
+    in_sems, out_sems,
 ):
     rows, kv_heads = keys_ref.shape[:2]
     pairs = [
-        (values_ref, value_s), (keys_ref, key_s), (queries_ref, query_s),
+        (queries_ref, query_s), (values_ref, value_s), (keys_ref, key_s), (readout_ref, readout_s),
         (segments_ref, segments_s), (mask_ref, mask_s), (labels_ref, labels_s),
     ]
     copies = [
@@ -319,40 +320,42 @@
         part = (slice(None), slice(first, last))
         return pltpu.make_async_copy(message_s.at[part], message_ref.at[part], out_sems.at[n])
 
-    readout = readout_ref[...]
+    copies[0].wait()
+    message_s[:, :rows, :] = jnp.swapaxes(query_s[...], 0, 1)
+    first = send(0, 0, rows)
+    first.start()
+    copies[2].wait()
+    halves_into(message_s, rows, jnp.swapaxes(key_s[...], 0, 1))
+    second = send(1, rows, rows + rows // 2)
+    second.start()
+    for copy in copies[3:]:
+        copy.wait()
+    readout = readout_s[...]
     high = readout.astype(jnp.bfloat16).astype(jnp.float32)
     middle = (readout - high).astype(jnp.bfloat16).astype(jnp.float32)
     rest = readout - high - middle
     spare = jnp.zeros((2, readout.shape[1]), jnp.float32)
-    copies[0].wait()
+    line = lax.broadcasted_iota(jnp.int32, (AUX, rows), 0)
+    flags = jnp.ones((AUX, rows), jnp.float32)
+    for n, source in ((SEGMENT, segments_s), (MASK, mask_s), (LABEL, labels_s)):
+        flags = jnp.where(line == n, source[...].reshape(1, rows).astype(jnp.float32), flags)
+    copies[1].wait()
     values = jnp.swapaxes(value_s[...], 0, 1)
-    worths = []
     for c in range(kv_heads):
         parts = [p[h : h + 1] for h in (2 * c, 2 * c + 1) for p in (high, middle, rest)]
         weights = jnp.concatenate(parts + [spare], axis=0).astype(jnp.bfloat16)
         product = dot(weights, values[c], NT)
-        worths += [product[0:1] + product[1:2] + product[2:3]]
-        worths += [product[3:4] + product[4:5] + product[5:6]]
-    copies[1].wait()
-    halves_into(message_s, rows, jnp.swapaxes(key_s[...], 0, 1))
-    for copy in copies[3:]:
-        copy.wait()
-    line = lax.broadcasted_iota(jnp.int32, (AUX, rows), 0)
-    flags = jnp.ones((AUX, rows), jnp.float32)
-    for n, source in ((SEGMENT, segments_s), (MASK, mask_s), (LABEL, labels_s)):
-        flags = jnp.where(line == n, source[...].reshape(1, rows).astype(jnp.float32), flags)
-    for h, worth in enumerate(worths):
-        worth_high = worth.astype(jnp.bfloat16).astype(jnp.float32)
-        lines = jnp.where(line == 0, worth_high, jnp.where(line == 1, worth - worth_high, flags))
-        message_s[h, rows + rows // 2 :, :] = lines.astype(jnp.bfloat16)
-    first = send(0, rows, rows + rows // 2 + AUX)
-    first.start()
-    copies[2].wait()
-    message_s[:, :rows, :] = jnp.swapaxes(query_s[...], 0, 1)
-    second = send(1, 0, rows)
-    second.start()
+        for h in range(2):
+            worth = product[3 * h : 3 * h + 1] + product[3 * h + 1 : 3 * h + 2]
+            worth = worth + product[3 * h + 2 : 3 * h + 3]
+            worth_high = worth.astype(jnp.bfloat16).astype(jnp.float32)
+            lines = jnp.where(line == 0, worth_high, jnp.where(line == 1, worth - worth_high, flags))
+            message_s[2 * c + h, rows + rows // 2 :, :] = lines.astype(jnp.bfloat16)
+    third = send(2, rows + rows // 2, rows + rows // 2 + AUX)
+    third.start()
     first.wait()
     second.wait()
+    third.wait()
 
 
 def pack(readout, segments, loss_mask, labels, queries, keys, values):
@@ -361,9 +364,10 @@
     return pl.pallas_call(
         pack_kernel,
         out_shape=jax.ShapeDtypeStruct(shape, jnp.bfloat16),
-        in_specs=[VMEM] + [ANY] * 6,
+        in_specs=[ANY] * 7,
         out_specs=ANY,
         scratch_shapes=[
+            pltpu.VMEM(readout.shape, jnp.float32),
             pltpu.VMEM(segments.shape, jnp.int32),
             pltpu.VMEM(segments.shape, jnp.int32),
             pltpu.VMEM(segments.shape, jnp.int32),
@@ -371,8 +375,8 @@
             pltpu.VMEM(keys.shape, jnp.bfloat16),
             pltpu.VMEM(values.shape, jnp.bfloat16),
             pltpu.VMEM(shape, jnp.bfloat16),
-            pltpu.SemaphoreType.DMA((6,)),
-            pltpu.SemaphoreType.DMA((2,)),
+            pltpu.SemaphoreType.DMA((7,)),
+            pltpu.SemaphoreType.DMA((3,)),
         ],
         compiler_params=pltpu.CompilerParams(vmem_limit_bytes=60 << 20),
         name="pack",

time: 98.6 us -> 98.7 us (level)
  Pallas kernels: 15.5 us -> 17.2 us
    pallas_call x1, Pallas kernels: 6.66 us -> 8.2 us  [attention_backward(): pl.pallas_call(functools.partial(backward_kernel, halo), out_shape=(jax.S...]
  transfers between devices with their start and end apart: 9 -> 9, of which waited for: 8 -> 8; matrix products, arithmetic and copies ran while one was open for 0% -> 0% of each run, Pallas kernels for 5% -> 6%
where the time goes in v7:
time: 98.7 us; the launch traced here: 98.8 us
  blocking collectives  29.3 us (30%)
  waiting for transfers between devices  29.2 us (30%)
  starting transfers between devices  21.9 us (22%)
  Pallas kernels  17.2 us (17%)
    all_to_all x1, blocking collectives, exchange(): lax.all_to_all(array, 'context', 0, 0, tiled=True, axis_index_groups=clus...  29.3 us
    all_to_all x2, waiting for transfers between devices, exchange(): lax.all_to_all(array, 'context', 0, 0, tiled=True, axis_index_groups=clus...  18 us
    all_to_all x2, starting transfers between devices, exchange(): lax.all_to_all(array, 'context', 0, 0, tiled=True, axis_index_groups=clus...  13.3 us
    pallas_call x1, Pallas kernels, attention_backward(): pl.pallas_call(functools.partial(backward_kernel, halo), out_shape=(jax.S...  8.2 us
    ppermute x4, waiting for transfers between devices, local(): lax.ppermute(reward, 'context', [(i, i ^ step) for i in range(devices)])  7.16 us
    ppermute x4, starting transfers between devices, local(): lax.ppermute(reward, 'context', [(i, i ^ step) for i in range(devices)])  6.84 us
    pallas_call x1, Pallas kernels, attention_forward(): pl.pallas_call(functools.partial(forward_kernel, halo), out_shape=(jax.Sh...  4.57 us
    ppermute x3, waiting for transfers between devices, swap(): return lax.ppermute(array, 'context', pairs)  4 us
  transfers between devices with their start and end apart: 9, of which 8 were waited for; matrix products, arithmetic and copies ran while one was open for 0% of the time, Pallas kernels for 6%

profile of v7, /device:TPU:1, one launch (start us, length us, event | category | flops | bytes accessed | tf_op | source)
XLA Modules:
  0.0 98.8 jit_solution(605502234366257277)
XLA Ops:
  0.6 2.3 %pack.1 = bf16[16,200,128]{2,1,0:T(8,128)(2,1)} custom-call(f32[16,128]{1,0:T(8,128)} %readout_ref.3, s32[128]{0:T(128)} %segments_ref.1, s32[128]{0:T(128)} %mask_ref.1, s32[128]{0:T(128)} %labels_ref.1, bf16[128,16,128]{2,1,0:T(8,128)(2,1)} %queries_ref.1, bf16[128,8,128]{2,1,0:T(8,128)(2,1)} %keys_ref.1, bf16[128,8,128]{2,1,0:T(8,128)(2,1)} %values_ref.3), custom_call_target="tpu_custom_call" | custom-call | tf_op jit(solution)/shard_map/pack/pallas_call | solution.py:364
  2.9 0.0 copy-start
  2.9 0.0 copy-start.1
  2.9 7.5 %all-to-all-start = ((bf16[16,200,128]{2,1,0:T(8,128)(2,1)}), bf16[16,200,128]{2,1,0:T(8,128)(2,1)S(1)}, u32[]{:S(2)}, u32[]{:S(2)}) async-start(bf16[16,200,128]{2,1,0:T(8,128)(2,1)} %pack.1), calls=%async_computation | async-start | bytes 1638400 | tf_op jit(solution)/shard_map/all_to_all | solution.py:436
  10.4 0.0 copy-done
  10.4 0.0 copy-done.1
  10.4 1.1 %pack_later.1 = bf16[16,192,128]{2,1,0:T(8,128)(2,1)} custom-call(bf16[128,16,128]{2,1,0:T(8,128)(2,1)S(1)} %copy-done.1, bf16[128,8,128]{2,1,0:T(8,128)(2,1)S(1)} %copy-done), custom_call_target="tpu_custom_call" | custom-call | bytes 3145728 | tf_op jit(solution)/shard_map/pack_later/pallas_call | solution.py:394
  11.5 18.0 %all-to-all-done.message_ref = bf16[16,200,128]{2,1,0:T(8,128)(2,1)S(1)} async-done(((bf16[16,200,128]{2,1,0:T(8,128)(2,1)}), bf16[16,200,128]{2,1,0:T(8,128)(2,1)S(1)}, u32[]{:S(2)}, u32[]{:S(2)}) %all-to-all-start) | async-done | bytes 819232 | tf_op jit(solution)/shard_map/all_to_all | solution.py:436
  29.6 5.8 %all-to-all-start.1 = ((bf16[16,192,128]{2,1,0:T(8,128)(2,1)}), bf16[16,192,128]{2,1,0:T(8,128)(2,1)S(1)}, u32[]{:S(2)}, u32[]{:S(2)}) async-start(bf16[16,192,128]{2,1,0:T(8,128)(2,1)} %pack_later.1), calls=%async_computation.1 | async-start | bytes 1572864 | tf_op jit(solution)/shard_map/all_to_all | solution.py:436
  35.4 0.2 collective-permute-start
  35.5 0.1 copy.19
  35.6 1.3 %collective-permute-done.other_ref = bf16[16,64,128]{2,1,0:T(8,128)(2,1)S(1)} collective-permute-done((bf16[16,64,128]{2,1,0:T(8,128)(2,1)S(1)}, bf16[16,64,128]{2,1,0:T(8,128)(2,1)S(1)}, u32[]{:S(2)}, u32[]{:S(2)}) %collective-permute-start) | collective-permute-done | bytes 262176 | tf_op jit(solution)/shard_map/ppermute | solution.py:441
  37.0 4.6 %attention_forward.1 = (f32[4,512]{1,0:T(4,128)S(1)}, f32[16,128]{1,0:T(8,128)S(1)}, s32[4]{0:T(128)S(1)}) custom-call(s32[1]{0:T(128)} %bitcast.index_ref, bf16[16,200,128]{2,1,0:T(8,128)(2,1)S(1)} %all-to-all-done.message_ref, bf16[16,64,128]{2,1,0:T(8,128)(2,1)S(1)} %slice.21.own_ref, bf16[16,64,128]{2,1,0:T(8,128)(2,1)S(1)} %collective-permute-done.other_ref, ...), custom_call_target="tpu_custom_call" | custom-call | flops 1610612736 | bytes 16777216 | tf_op jit(solution)/shard_map/attention_forward/pallas_call | solution.py:234
  41.5 0.2 collective-permute-start.1
  41.7 1.0 %collective-permute-done.1 = f32[16,128]{1,0:T(8,128)S(1)} collective-permute-done((f32[16,128]{1,0:T(8,128)S(1)}, f32[16,128]{1,0:T(8,128)S(1)}, u32[]{:S(2)}, u32[]{:S(2)}) %collective-permute-start.1) | collective-permute-done | bytes 8224 | tf_op jit(solution)/shard_map/ppermute | solution.py:470
  42.8 1.4 %collective-permute-start.2 = (f32[16,128]{1,0:T(8,128)S(1)}, f32[16,128]{1,0:T(8,128)S(1)}, u32[]{:S(2)}, u32[]{:S(2)}) collective-permute-start(f32[16,128]{1,0:T(8,128)S(1)} %add.15), channel_id=1, source_target_pairs={{0,2},{1,3},{2,0},{3,1},{4,6},{5,7},{6,4},{7,5},{8,10},{9,11},{10,... | collective-permute-start | bytes 24584 | tf_op jit(solution)/shard_map/ppermute | solution.py:470
  44.2 1.4 %collective-permute-done.2 = f32[16,128]{1,0:T(8,128)S(1)} collective-permute-done((f32[16,128]{1,0:T(8,128)S(1)}, f32[16,128]{1,0:T(8,128)S(1)}, u32[]{:S(2)}, u32[]{:S(2)}) %collective-permute-start.2) | collective-permute-done | bytes 8224 | tf_op jit(solution)/shard_map/ppermute | solution.py:470
  45.6 1.4 %collective-permute-start.3 = (f32[16,128]{1,0:T(8,128)S(1)}, f32[16,128]{1,0:T(8,128)S(1)}, u32[]{:S(2)}, u32[]{:S(2)}) collective-permute-start(f32[16,128]{1,0:T(8,128)S(1)} %add.16), channel_id=1, source_target_pairs={{0,4},{1,5},{2,6},{3,7},{4,0},{5,1},{6,2},{7,3},{8,12},{9,13},{10,... | collective-permute-start | bytes 24584 | tf_op jit(solution)/shard_map/ppermute | solution.py:470
  47.0 1.8 %collective-permute-done.3 = f32[16,128]{1,0:T(8,128)S(1)} collective-permute-done((f32[16,128]{1,0:T(8,128)S(1)}, f32[16,128]{1,0:T(8,128)S(1)}, u32[]{:S(2)}, u32[]{:S(2)}) %collective-permute-start.3) | collective-permute-done | bytes 8224 | tf_op jit(solution)/shard_map/ppermute | solution.py:470
  48.8 3.8 %collective-permute-start.4 = (f32[16,128]{1,0:T(8,128)S(1)}, f32[16,128]{1,0:T(8,128)S(1)}, u32[]{:S(2)}, u32[]{:S(2)}) collective-permute-start(f32[16,128]{1,0:T(8,128)S(1)} %add.17), channel_id=1, source_target_pairs={{0,8},{1,9},{2,10},{3,11},{4,12},{5,13},{6,14},{7,15},{8,0},{9,1},... | collective-permute-start | bytes 24584 | tf_op jit(solution)/shard_map/ppermute | solution.py:470
  52.6 2.9 %collective-permute-done.4 = f32[16,128]{1,0:T(8,128)S(1)} collective-permute-done((f32[16,128]{1,0:T(8,128)S(1)}, f32[16,128]{1,0:T(8,128)S(1)}, u32[]{:S(2)}, u32[]{:S(2)}) %collective-permute-start.4) | collective-permute-done | bytes 8224 | tf_op jit(solution)/shard_map/ppermute | solution.py:470
  55.5 0.0 all-to-all-done.1.later_ref
  55.6 1.2 %collective-permute-start.5 = (bf16[16,64,128]{2,1,0:T(8,128)(2,1)S(1)}, bf16[16,64,128]{2,1,0:T(8,128)(2,1)S(1)}, u32[]{:S(2)}, u32[]{:S(2)}) collective-permute-start(bf16[16,64,128]{2,1,0:T(8,128)(2,1)S(1)} %slice.24.own_value_ref), channel_id=1, source_target_pairs={{0,1},{1,0},{2,3},{3,2},{4,5},{5,4},{6,7},{7,6},{8,9},{9,8},{10,11... | collective-permute-start | bytes 786440 | tf_op jit(solution)/shard_map/ppermute | solution.py:441
  56.8 1.2 %collective-permute-done.5.other_value_ref = bf16[16,64,128]{2,1,0:T(8,128)(2,1)S(1)} collective-permute-done((bf16[16,64,128]{2,1,0:T(8,128)(2,1)S(1)}, bf16[16,64,128]{2,1,0:T(8,128)(2,1)S(1)}, u32[]{:S(2)}, u32[]{:S(2)}) %collective-permute-start.5) | collective-permute-done | bytes 262176 | tf_op jit(solution)/shard_map/ppermute | solution.py:441
  58.0 0.0 copy-done.2
  58.0 8.2 %attention_backward.1 = (bf16[16,128,128]{2,1,0:T(8,128)(2,1)S(1)}, bf16[16,128,128]{2,1,0:T(8,128)(2,1)S(1)}, bf16[16,128,128]{2,1,0:T(8,128)(2,1)S(1)}) custom-call(s32[1]{0:T(128)} %bitcast.index_ref, s32[4]{0:T(128)S(1)} %get-tuple-element.14.starts_ref, bf16[16,200,128]{2,1,0:T(8,128)(2,1)S(1)} %all-to-all-done.message_ref, ...), custom_call_target="tpu_custom_call" | custom-call | flops 4026531840 | bytes 16777216 | tf_op jit(solution)/shard_map/attention_backward/pallas_call | solution.py:264
  66.2 0.4 collective-permute-start.6
  66.6 1.5 %collective-permute-done.6 = bf16[16,128,128]{2,1,0:T(8,128)(2,1)S(1)} collective-permute-done((bf16[16,128,128]{2,1,0:T(8,128)(2,1)S(1)}, bf16[16,128,128]{2,1,0:T(8,128)(2,1)S(1)}, u32[]{:S(2)}, u32[]{:S(2)}) %collective-permute-start.6) | collective-permute-done | bytes 524320 | tf_op jit(solution)/shard_map/ppermute | solution.py:441
  68.2 0.1 add_convert_fusion
  68.3 0.1 pad_maximum_fusion
  68.4 29.3 %all_to_all.15.home_ref = bf16[16,256,128]{2,1,0:T(8,128)(2,1)S(1)} all-to-all(bf16[16,256,128]{2,1,0:T(8,128)(2,1)S(1)} %pad_maximum_fusion), channel_id=1, replica_groups=mesh['groups'=2,'context'=16] {'context'}, dimensions={0} | all-to-all | bytes 2097152 | tf_op jit(solution)/shard_map/all_to_all | solution.py:436
  97.7 1.0 %unpack.1 = (bf16[128,16,128]{2,1,0:T(8,128)(2,1)}, bf16[128,8,128]{2,1,0:T(8,128)(2,1)}, bf16[128,8,128]{2,1,0:T(8,128)(2,1)}) custom-call(bf16[16,256,128]{2,1,0:T(8,128)(2,1)S(1)} %all_to_all.15.home_ref), custom_call_target="tpu_custom_call" | custom-call | tf_op jit(solution)/shard_map/unpack/pallas_call | solution.py:415
  (10 shorter events, 0.1 us)
Async XLA Ops:
  2.9 7.5 %copy-start = (bf16[128,8,128]{2,1,0:T(8,128)(2,1)S(1)}, bf16[128,8,128]{2,1,0:T(8,128)(2,1)}, u32[]{:S(2)}) copy-start(bf16[128,8,128]{2,1,0:T(8,128)(2,1)} %values_ref.3) | copy-start | bytes 786436
  2.9 7.5 %copy-start.1 = (bf16[128,16,128]{2,1,0:T(8,128)(2,1)S(1)}, bf16[128,16,128]{2,1,0:T(8,128)(2,1)}, u32[]{:S(2)}) copy-start(bf16[128,16,128]{2,1,0:T(8,128)(2,1)} %grad_ref.1) | copy-start | bytes 1572868
  2.9 26.6 %all-to-all-start = ((bf16[16,200,128]{2,1,0:T(8,128)(2,1)}), bf16[16,200,128]{2,1,0:T(8,128)(2,1)S(1)}, u32[]{:S(2)}, u32[]{:S(2)}) async-start(bf16[16,200,128]{2,1,0:T(8,128)(2,1)} %pack.1), calls=%async_computation | async-start | bytes 1638400 | tf_op jit(solution)/shard_map/all_to_all | solution.py:436
  29.6 26.0 %all-to-all-start.1 = ((bf16[16,192,128]{2,1,0:T(8,128)(2,1)}), bf16[16,192,128]{2,1,0:T(8,128)(2,1)S(1)}, u32[]{:S(2)}, u32[]{:S(2)}) async-start(bf16[16,192,128]{2,1,0:T(8,128)(2,1)} %pack_later.1), calls=%async_computation.1 | async-start | bytes 1572864 | tf_op jit(solution)/shard_map/all_to_all | solution.py:436
  35.4 1.6 %collective-permute-start = (bf16[16,64,128]{2,1,0:T(8,128)(2,1)S(1)}, bf16[16,64,128]{2,1,0:T(8,128)(2,1)S(1)}, u32[]{:S(2)}, u32[]{:S(2)}) collective-permute-start(bf16[16,64,128]{2,1,0:T(8,128)(2,1)S(1)} %slice.21.own_ref), channel_id=1, source_target_pairs={{0,1},{1,0},{2,3},{3,2},{4,5},{5,4},{6,7},{7,6},{8,9},{9,8},{10,11... | collective-permute-start | bytes 786440 | tf_op jit(solution)/shard_map/ppermute | solution.py:441
  37.0 21.0 %copy-start.2 = (f32[16,128]{1,0:T(8,128)S(1)}, f32[16,128]{1,0:T(8,128)}, u32[]{:S(2)}) copy-start(f32[16,128]{1,0:T(8,128)} %readout_ref.3) | copy-start | bytes 24580
  41.5 1.2 %collective-permute-start.1 = (f32[16,128]{1,0:T(8,128)S(1)}, f32[16,128]{1,0:T(8,128)S(1)}, u32[]{:S(2)}, u32[]{:S(2)}) collective-permute-start(f32[16,128]{1,0:T(8,128)S(1)} %get-tuple-element.16), channel_id=1, source_target_pairs={{0,1},{1,0},{2,3},{3,2},{4,5},{5,4},{6,7},{7,6},{8,9},{9,8},{10,11... | collective-permute-start | bytes 24584 | tf_op jit(solution)/shard_map/ppermute | solution.py:470
  42.8 2.8 %collective-permute-start.2 = (f32[16,128]{1,0:T(8,128)S(1)}, f32[16,128]{1,0:T(8,128)S(1)}, u32[]{:S(2)}, u32[]{:S(2)}) collective-permute-start(f32[16,128]{1,0:T(8,128)S(1)} %add.15), channel_id=1, source_target_pairs={{0,2},{1,3},{2,0},{3,1},{4,6},{5,7},{6,4},{7,5},{8,10},{9,11},{10,... | collective-permute-start | bytes 24584 | tf_op jit(solution)/shard_map/ppermute | solution.py:470
  45.6 3.2 %collective-permute-start.3 = (f32[16,128]{1,0:T(8,128)S(1)}, f32[16,128]{1,0:T(8,128)S(1)}, u32[]{:S(2)}, u32[]{:S(2)}) collective-permute-start(f32[16,128]{1,0:T(8,128)S(1)} %add.16), channel_id=1, source_target_pairs={{0,4},{1,5},{2,6},{3,7},{4,0},{5,1},{6,2},{7,3},{8,12},{9,13},{10,... | collective-permute-start | bytes 24584 | tf_op jit(solution)/shard_map/ppermute | solution.py:470
  48.8 6.8 %collective-permute-start.4 = (f32[16,128]{1,0:T(8,128)S(1)}, f32[16,128]{1,0:T(8,128)S(1)}, u32[]{:S(2)}, u32[]{:S(2)}) collective-permute-start(f32[16,128]{1,0:T(8,128)S(1)} %add.17), channel_id=1, source_target_pairs={{0,8},{1,9},{2,10},{3,11},{4,12},{5,13},{6,14},{7,15},{8,0},{9,1},... | collective-permute-start | bytes 24584 | tf_op jit(solution)/shard_map/ppermute | solution.py:470
  55.6 2.4 %collective-permute-start.5 = (bf16[16,64,128]{2,1,0:T(8,128)(2,1)S(1)}, bf16[16,64,128]{2,1,0:T(8,128)(2,1)S(1)}, u32[]{:S(2)}, u32[]{:S(2)}) collective-permute-start(bf16[16,64,128]{2,1,0:T(8,128)(2,1)S(1)} %slice.24.own_value_ref), channel_id=1, source_target_pairs={{0,1},{1,0},{2,3},{3,2},{4,5},{5,4},{6,7},{7,6},{8,9},{9,8},{10,11... | collective-permute-start | bytes 786440 | tf_op jit(solution)/shard_map/ppermute | solution.py:441
  66.2 2.0 %collective-permute-start.6 = (bf16[16,128,128]{2,1,0:T(8,128)(2,1)S(1)}, bf16[16,128,128]{2,1,0:T(8,128)(2,1)S(1)}, u32[]{:S(2)}, u32[]{:S(2)}) collective-permute-start(bf16[16,128,128]{2,1,0:T(8,128)(2,1)S(1)} %get-tuple-element.22), channel_id=1, source_target_pairs={{0,1},{1,0},{2,3},{3,2},{4,5},{5,4},{6,7},{7,6},{8,9},{9,8},{10,11... | collective-permute-start | bytes 1572872 | tf_op jit(solution)/shard_map/ppermute | solution.py:441

commit v8 on v7

--- a/solution.py
+++ b/solution.py
@@ -55,7 +55,9 @@
 
 
 def late(j, n):
-    return slice(BLOCK, QUERIES) if j == n - 1 else slice(0, QUERIES)
+    if j == n - 1:
+        return slice(BLOCK, QUERIES)
+    return slice(0, BLOCK if j == 0 and n == REACH else QUERIES)
 
 
 def valid_of(key_iota, causal, bound, j, n):
@@ -69,8 +71,11 @@
 def fold(parts, combine, reduce):
     if reduce is not None:
         parts = [reduce(p.reshape(p.shape[0] // 8, 8, p.shape[1]), axis=0) for p in parts]
-    whole = functools.reduce(combine, parts[:-1])
-    return jnp.concatenate([whole[:, :BLOCK], combine(whole[:, BLOCK:], parts[-1])], axis=1)
+    whole = functools.reduce(combine, [p for p in parts if p.shape[1] == QUERIES])
+    early, later = whole[:, :BLOCK], combine(whole[:, BLOCK:], parts[-1])
+    if parts[0].shape[1] == BLOCK:
+        early = combine(early, parts[0])
+    return jnp.concatenate([early, later], axis=1)
 
 
 def place(even, own_ref, other_ref, put):
@@ -182,12 +187,20 @@
             bound = bound_s[pl.ds(i, 1), :] - first * BLOCK
             total = total_ref[pl.ds(i, 1), :]
             probs, grad_probs, deltas = [], [], []
+
+            def dots(j):
+                rows, span = rows_of(first + j), late(j, n)
+                return dot(key_s[rows, :], query[span], NT), dot(value_s[rows, :], grad[span], NT)
+
+            ahead = dots(0)
             for j in range(n):
                 rows, span = rows_of(first + j), late(j, n)
-                score = dot(key_s[rows, :], query[span], NT) * (SCALE * LOG2E) - total[:, span]
+                score, grad_prob = ahead
+                if j < n - 1:
+                    ahead = dots(j + 1)
+                score = score * (SCALE * LOG2E) - total[:, span]
                 valid = valid_of(key_iota, causal, bound, j, n)
                 prob = jnp.exp2(jnp.where(valid, score, NEGATIVE))
-                grad_prob = dot(value_s[rows, :], grad[span], NT)
                 deltas.append(prob * grad_prob)
                 value_grad = dot(prob.astype(jnp.bfloat16), grad[span], NN)
                 if j >= n - 2:

time: 98.7 us -> 98.1 us (level)
  Pallas kernels: 17.2 us -> 15.5 us
    pallas_call x1, Pallas kernels: 8.2 us -> 7.14 us  [attention_backward(): pl.pallas_call(functools.partial(backward_kernel, halo), out_shape=(jax.S...]
  transfers between devices with their start and end apart: 9 -> 9, of which waited for: 8 -> 8; matrix products, arithmetic and copies ran while one was open for 0% -> 0% of each run, Pallas kernels for 6% -> 5%
where the time goes in v8:
time: 98.1 us; the launch traced here: 97.7 us
  waiting for transfers between devices  29.6 us (30%)
  blocking collectives  29.3 us (30%)
  starting transfers between devices  22.1 us (23%)
  Pallas kernels  15.5 us (16%)
    all_to_all x1, blocking collectives, exchange(): lax.all_to_all(array, 'context', 0, 0, tiled=True, axis_index_groups=clus...  29.3 us
    all_to_all x2, waiting for transfers between devices, exchange(): lax.all_to_all(array, 'context', 0, 0, tiled=True, axis_index_groups=clus...  18 us
    all_to_all x2, starting transfers between devices, exchange(): lax.all_to_all(array, 'context', 0, 0, tiled=True, axis_index_groups=clus...  13.3 us
    ppermute x4, waiting for transfers between devices, local(): lax.ppermute(reward, 'context', [(i, i ^ step) for i in range(devices)])  7.58 us
    pallas_call x1, Pallas kernels, attention_backward(): pl.pallas_call(functools.partial(backward_kernel, halo), out_shape=(jax.S...  7.14 us
    ppermute x4, starting transfers between devices, local(): lax.ppermute(reward, 'context', [(i, i ^ step) for i in range(devices)])  7.01 us
    ppermute x3, waiting for transfers between devices, swap(): return lax.ppermute(array, 'context', pairs)  4 us
    pallas_call x1, Pallas kernels, attention_forward(): pl.pallas_call(functools.partial(forward_kernel, halo), out_shape=(jax.Sh...  3.98 us
  transfers between devices with their start and end apart: 9, of which 8 were waited for; matrix products, arithmetic and copies ran while one was open for 0% of the time, Pallas kernels for 5%

profile of v8, /device:TPU:1, one launch (start us, length us, event | category | flops | bytes accessed | tf_op | source)
XLA Modules:
  0.0 97.7 jit_solution(2627664288894716298)
XLA Ops:
  0.6 2.3 %pack.1 = bf16[16,200,128]{2,1,0:T(8,128)(2,1)} custom-call(f32[16,128]{1,0:T(8,128)} %readout_ref.3, s32[128]{0:T(128)} %segments_ref.1, s32[128]{0:T(128)} %mask_ref.1, s32[128]{0:T(128)} %labels_ref.1, bf16[128,16,128]{2,1,0:T(8,128)(2,1)} %queries_ref.1, bf16[128,8,128]{2,1,0:T(8,128)(2,1)} %keys_ref.1, bf16[128,8,128]{2,1,0:T(8,128)(2,1)} %values_ref.3), custom_call_target="tpu_custom_call" | custom-call | tf_op jit(solution)/shard_map/pack/pallas_call | solution.py:377
  2.9 0.0 copy-start
  2.9 0.0 copy-start.1
  2.9 7.5 %all-to-all-start = ((bf16[16,200,128]{2,1,0:T(8,128)(2,1)}), bf16[16,200,128]{2,1,0:T(8,128)(2,1)S(1)}, u32[]{:S(2)}, u32[]{:S(2)}) async-start(bf16[16,200,128]{2,1,0:T(8,128)(2,1)} %pack.1), calls=%async_computation | async-start | bytes 1638400 | tf_op jit(solution)/shard_map/all_to_all | solution.py:449
  10.4 0.0 copy-done
  10.4 0.0 copy-done.1
  10.4 1.1 %pack_later.1 = bf16[16,192,128]{2,1,0:T(8,128)(2,1)} custom-call(bf16[128,16,128]{2,1,0:T(8,128)(2,1)S(1)} %copy-done.1, bf16[128,8,128]{2,1,0:T(8,128)(2,1)S(1)} %copy-done), custom_call_target="tpu_custom_call" | custom-call | bytes 3145728 | tf_op jit(solution)/shard_map/pack_later/pallas_call | solution.py:407
  11.5 18.0 %all-to-all-done.message_ref = bf16[16,200,128]{2,1,0:T(8,128)(2,1)S(1)} async-done(((bf16[16,200,128]{2,1,0:T(8,128)(2,1)}), bf16[16,200,128]{2,1,0:T(8,128)(2,1)S(1)}, u32[]{:S(2)}, u32[]{:S(2)}) %all-to-all-start) | async-done | bytes 819232 | tf_op jit(solution)/shard_map/all_to_all | solution.py:449
  29.6 5.8 %all-to-all-start.1 = ((bf16[16,192,128]{2,1,0:T(8,128)(2,1)}), bf16[16,192,128]{2,1,0:T(8,128)(2,1)S(1)}, u32[]{:S(2)}, u32[]{:S(2)}) async-start(bf16[16,192,128]{2,1,0:T(8,128)(2,1)} %pack_later.1), calls=%async_computation.1 | async-start | bytes 1572864 | tf_op jit(solution)/shard_map/all_to_all | solution.py:449
  35.4 0.2 collective-permute-start
  35.5 0.1 copy.19
  35.6 1.3 %collective-permute-done.other_ref = bf16[16,64,128]{2,1,0:T(8,128)(2,1)S(1)} collective-permute-done((bf16[16,64,128]{2,1,0:T(8,128)(2,1)S(1)}, bf16[16,64,128]{2,1,0:T(8,128)(2,1)S(1)}, u32[]{:S(2)}, u32[]{:S(2)}) %collective-permute-start) | collective-permute-done | bytes 262176 | tf_op jit(solution)/shard_map/ppermute | solution.py:454
  37.0 4.0 %attention_forward.1 = (f32[4,512]{1,0:T(4,128)S(1)}, f32[16,128]{1,0:T(8,128)S(1)}, s32[4]{0:T(128)S(1)}) custom-call(s32[1]{0:T(128)} %bitcast.index_ref, bf16[16,200,128]{2,1,0:T(8,128)(2,1)S(1)} %all-to-all-done.message_ref, bf16[16,64,128]{2,1,0:T(8,128)(2,1)S(1)} %slice.21.own_ref, bf16[16,64,128]{2,1,0:T(8,128)(2,1)S(1)} %collective-permute-done.other_ref, ...), custom_call_target="tpu_custom_call" | custom-call | flops 1610612736 | bytes 16777216 | tf_op jit(solution)/shard_map/attention_forward/pallas_call | solution.py:247
  40.9 0.2 collective-permute-start.1
  41.1 1.0 %collective-permute-done.1 = f32[16,128]{1,0:T(8,128)S(1)} collective-permute-done((f32[16,128]{1,0:T(8,128)S(1)}, f32[16,128]{1,0:T(8,128)S(1)}, u32[]{:S(2)}, u32[]{:S(2)}) %collective-permute-start.1) | collective-permute-done | bytes 8224 | tf_op jit(solution)/shard_map/ppermute | solution.py:483
  42.2 1.4 %collective-permute-start.2 = (f32[16,128]{1,0:T(8,128)S(1)}, f32[16,128]{1,0:T(8,128)S(1)}, u32[]{:S(2)}, u32[]{:S(2)}) collective-permute-start(f32[16,128]{1,0:T(8,128)S(1)} %add.15), channel_id=1, source_target_pairs={{0,2},{1,3},{2,0},{3,1},{4,6},{5,7},{6,4},{7,5},{8,10},{9,11},{10,... | collective-permute-start | bytes 24584 | tf_op jit(solution)/shard_map/ppermute | solution.py:483
  43.6 1.3 %collective-permute-done.2 = f32[16,128]{1,0:T(8,128)S(1)} collective-permute-done((f32[16,128]{1,0:T(8,128)S(1)}, f32[16,128]{1,0:T(8,128)S(1)}, u32[]{:S(2)}, u32[]{:S(2)}) %collective-permute-start.2) | collective-permute-done | bytes 8224 | tf_op jit(solution)/shard_map/ppermute | solution.py:483
  44.9 1.6 %collective-permute-start.3 = (f32[16,128]{1,0:T(8,128)S(1)}, f32[16,128]{1,0:T(8,128)S(1)}, u32[]{:S(2)}, u32[]{:S(2)}) collective-permute-start(f32[16,128]{1,0:T(8,128)S(1)} %add.16), channel_id=1, source_target_pairs={{0,4},{1,5},{2,6},{3,7},{4,0},{5,1},{6,2},{7,3},{8,12},{9,13},{10,... | collective-permute-start | bytes 24584 | tf_op jit(solution)/shard_map/ppermute | solution.py:483
  46.4 2.3 %collective-permute-done.3 = f32[16,128]{1,0:T(8,128)S(1)} collective-permute-done((f32[16,128]{1,0:T(8,128)S(1)}, f32[16,128]{1,0:T(8,128)S(1)}, u32[]{:S(2)}, u32[]{:S(2)}) %collective-permute-start.3) | collective-permute-done | bytes 8224 | tf_op jit(solution)/shard_map/ppermute | solution.py:483
  48.8 3.8 %collective-permute-start.4 = (f32[16,128]{1,0:T(8,128)S(1)}, f32[16,128]{1,0:T(8,128)S(1)}, u32[]{:S(2)}, u32[]{:S(2)}) collective-permute-start(f32[16,128]{1,0:T(8,128)S(1)} %add.17), channel_id=1, source_target_pairs={{0,8},{1,9},{2,10},{3,11},{4,12},{5,13},{6,14},{7,15},{8,0},{9,1},... | collective-permute-start | bytes 24584 | tf_op jit(solution)/shard_map/ppermute | solution.py:483
  52.6 2.9 %collective-permute-done.4 = f32[16,128]{1,0:T(8,128)S(1)} collective-permute-done((f32[16,128]{1,0:T(8,128)S(1)}, f32[16,128]{1,0:T(8,128)S(1)}, u32[]{:S(2)}, u32[]{:S(2)}) %collective-permute-start.4) | collective-permute-done | bytes 8224 | tf_op jit(solution)/shard_map/ppermute | solution.py:483
  55.5 0.0 all-to-all-done.1.later_ref
  55.6 1.2 %collective-permute-start.5 = (bf16[16,64,128]{2,1,0:T(8,128)(2,1)S(1)}, bf16[16,64,128]{2,1,0:T(8,128)(2,1)S(1)}, u32[]{:S(2)}, u32[]{:S(2)}) collective-permute-start(bf16[16,64,128]{2,1,0:T(8,128)(2,1)S(1)} %slice.24.own_value_ref), channel_id=1, source_target_pairs={{0,1},{1,0},{2,3},{3,2},{4,5},{5,4},{6,7},{7,6},{8,9},{9,8},{10,11... | collective-permute-start | bytes 786440 | tf_op jit(solution)/shard_map/ppermute | solution.py:454
  56.8 1.2 %collective-permute-done.5.other_value_ref = bf16[16,64,128]{2,1,0:T(8,128)(2,1)S(1)} collective-permute-done((bf16[16,64,128]{2,1,0:T(8,128)(2,1)S(1)}, bf16[16,64,128]{2,1,0:T(8,128)(2,1)S(1)}, u32[]{:S(2)}, u32[]{:S(2)}) %collective-permute-start.5) | collective-permute-done | bytes 262176 | tf_op jit(solution)/shard_map/ppermute | solution.py:454
  58.0 0.0 copy-done.2
  58.0 7.1 %attention_backward.1 = (bf16[16,128,128]{2,1,0:T(8,128)(2,1)S(1)}, bf16[16,128,128]{2,1,0:T(8,128)(2,1)S(1)}, bf16[16,128,128]{2,1,0:T(8,128)(2,1)S(1)}) custom-call(s32[1]{0:T(128)} %bitcast.index_ref, s32[4]{0:T(128)S(1)} %get-tuple-element.14.starts_ref, bf16[16,200,128]{2,1,0:T(8,128)(2,1)S(1)} %all-to-all-done.message_ref, ...), custom_call_target="tpu_custom_call" | custom-call | flops 4026531840 | bytes 16777216 | tf_op jit(solution)/shard_map/attention_backward/pallas_call | solution.py:277
  65.1 0.5 collective-permute-start.6
  65.6 1.5 %collective-permute-done.6 = bf16[16,128,128]{2,1,0:T(8,128)(2,1)S(1)} collective-permute-done((bf16[16,128,128]{2,1,0:T(8,128)(2,1)S(1)}, bf16[16,128,128]{2,1,0:T(8,128)(2,1)S(1)}, u32[]{:S(2)}, u32[]{:S(2)}) %collective-permute-start.6) | collective-permute-done | bytes 524320 | tf_op jit(solution)/shard_map/ppermute | solution.py:454
  67.1 0.1 add_convert_fusion
  67.3 0.1 pad_maximum_fusion
  67.4 29.3 %all_to_all.15.home_ref = bf16[16,256,128]{2,1,0:T(8,128)(2,1)S(1)} all-to-all(bf16[16,256,128]{2,1,0:T(8,128)(2,1)S(1)} %pad_maximum_fusion), channel_id=1, replica_groups=mesh['groups'=2,'context'=16] {'context'}, dimensions={0} | all-to-all | bytes 2097152 | tf_op jit(solution)/shard_map/all_to_all | solution.py:449
  96.6 1.0 %unpack.1 = (bf16[128,16,128]{2,1,0:T(8,128)(2,1)}, bf16[128,8,128]{2,1,0:T(8,128)(2,1)}, bf16[128,8,128]{2,1,0:T(8,128)(2,1)}) custom-call(bf16[16,256,128]{2,1,0:T(8,128)(2,1)S(1)} %all_to_all.15.home_ref), custom_call_target="tpu_custom_call" | custom-call | tf_op jit(solution)/shard_map/unpack/pallas_call | solution.py:428
  (10 shorter events, 0.1 us)
Async XLA Ops:
  2.9 7.5 %copy-start = (bf16[128,8,128]{2,1,0:T(8,128)(2,1)S(1)}, bf16[128,8,128]{2,1,0:T(8,128)(2,1)}, u32[]{:S(2)}) copy-start(bf16[128,8,128]{2,1,0:T(8,128)(2,1)} %values_ref.3) | copy-start | bytes 786436
  2.9 7.5 %copy-start.1 = (bf16[128,16,128]{2,1,0:T(8,128)(2,1)S(1)}, bf16[128,16,128]{2,1,0:T(8,128)(2,1)}, u32[]{:S(2)}) copy-start(bf16[128,16,128]{2,1,0:T(8,128)(2,1)} %grad_ref.1) | copy-start | bytes 1572868
  2.9 26.6 %all-to-all-start = ((bf16[16,200,128]{2,1,0:T(8,128)(2,1)}), bf16[16,200,128]{2,1,0:T(8,128)(2,1)S(1)}, u32[]{:S(2)}, u32[]{:S(2)}) async-start(bf16[16,200,128]{2,1,0:T(8,128)(2,1)} %pack.1), calls=%async_computation | async-start | bytes 1638400 | tf_op jit(solution)/shard_map/all_to_all | solution.py:449
  29.6 26.0 %all-to-all-start.1 = ((bf16[16,192,128]{2,1,0:T(8,128)(2,1)}), bf16[16,192,128]{2,1,0:T(8,128)(2,1)S(1)}, u32[]{:S(2)}, u32[]{:S(2)}) async-start(bf16[16,192,128]{2,1,0:T(8,128)(2,1)} %pack_later.1), calls=%async_computation.1 | async-start | bytes 1572864 | tf_op jit(solution)/shard_map/all_to_all | solution.py:449
  35.4 1.6 %collective-permute-start = (bf16[16,64,128]{2,1,0:T(8,128)(2,1)S(1)}, bf16[16,64,128]{2,1,0:T(8,128)(2,1)S(1)}, u32[]{:S(2)}, u32[]{:S(2)}) collective-permute-start(bf16[16,64,128]{2,1,0:T(8,128)(2,1)S(1)} %slice.21.own_ref), channel_id=1, source_target_pairs={{0,1},{1,0},{2,3},{3,2},{4,5},{5,4},{6,7},{7,6},{8,9},{9,8},{10,11... | collective-permute-start | bytes 786440 | tf_op jit(solution)/shard_map/ppermute | solution.py:454
  37.0 21.0 %copy-start.2 = (f32[16,128]{1,0:T(8,128)S(1)}, f32[16,128]{1,0:T(8,128)}, u32[]{:S(2)}) copy-start(f32[16,128]{1,0:T(8,128)} %readout_ref.3) | copy-start | bytes 24580
  40.9 1.2 %collective-permute-start.1 = (f32[16,128]{1,0:T(8,128)S(1)}, f32[16,128]{1,0:T(8,128)S(1)}, u32[]{:S(2)}, u32[]{:S(2)}) collective-permute-start(f32[16,128]{1,0:T(8,128)S(1)} %get-tuple-element.16), channel_id=1, source_target_pairs={{0,1},{1,0},{2,3},{3,2},{4,5},{5,4},{6,7},{7,6},{8,9},{9,8},{10,11... | collective-permute-start | bytes 24584 | tf_op jit(solution)/shard_map/ppermute | solution.py:483
  42.2 2.7 %collective-permute-start.2 = (f32[16,128]{1,0:T(8,128)S(1)}, f32[16,128]{1,0:T(8,128)S(1)}, u32[]{:S(2)}, u32[]{:S(2)}) collective-permute-start(f32[16,128]{1,0:T(8,128)S(1)} %add.15), channel_id=1, source_target_pairs={{0,2},{1,3},{2,0},{3,1},{4,6},{5,7},{6,4},{7,5},{8,10},{9,11},{10,... | collective-permute-start | bytes 24584 | tf_op jit(solution)/shard_map/ppermute | solution.py:483
  44.9 3.9 %collective-permute-start.3 = (f32[16,128]{1,0:T(8,128)S(1)}, f32[16,128]{1,0:T(8,128)S(1)}, u32[]{:S(2)}, u32[]{:S(2)}) collective-permute-start(f32[16,128]{1,0:T(8,128)S(1)} %add.16), channel_id=1, source_target_pairs={{0,4},{1,5},{2,6},{3,7},{4,0},{5,1},{6,2},{7,3},{8,12},{9,13},{10,... | collective-permute-start | bytes 24584 | tf_op jit(solution)/shard_map/ppermute | solution.py:483
  48.8 6.8 %collective-permute-start.4 = (f32[16,128]{1,0:T(8,128)S(1)}, f32[16,128]{1,0:T(8,128)S(1)}, u32[]{:S(2)}, u32[]{:S(2)}) collective-permute-start(f32[16,128]{1,0:T(8,128)S(1)} %add.17), channel_id=1, source_target_pairs={{0,8},{1,9},{2,10},{3,11},{4,12},{5,13},{6,14},{7,15},{8,0},{9,1},... | collective-permute-start | bytes 24584 | tf_op jit(solution)/shard_map/ppermute | solution.py:483
  55.6 2.4 %collective-permute-start.5 = (bf16[16,64,128]{2,1,0:T(8,128)(2,1)S(1)}, bf16[16,64,128]{2,1,0:T(8,128)(2,1)S(1)}, u32[]{:S(2)}, u32[]{:S(2)}) collective-permute-start(bf16[16,64,128]{2,1,0:T(8,128)(2,1)S(1)} %slice.24.own_value_ref), channel_id=1, source_target_pairs={{0,1},{1,0},{2,3},{3,2},{4,5},{5,4},{6,7},{7,6},{8,9},{9,8},{10,11... | collective-permute-start | bytes 786440 | tf_op jit(solution)/shard_map/ppermute | solution.py:454
  65.1 2.0 %collective-permute-start.6 = (bf16[16,128,128]{2,1,0:T(8,128)(2,1)S(1)}, bf16[16,128,128]{2,1,0:T(8,128)(2,1)S(1)}, u32[]{:S(2)}, u32[]{:S(2)}) collective-permute-start(bf16[16,128,128]{2,1,0:T(8,128)(2,1)S(1)} %get-tuple-element.22), channel_id=1, source_target_pairs={{0,1},{1,0},{2,3},{3,2},{4,5},{5,4},{6,7},{7,6},{8,9},{9,8},{10,11... | collective-permute-start | bytes 1572872 | tf_op jit(solution)/shard_map/ppermute | solution.py:454

commit v9 on v8

--- a/solution.py
+++ b/solution.py
@@ -479,7 +479,7 @@
     where = jnp.reshape(index, (1,)).astype(jnp.int32)
     total, reward, starts = attention_forward(halo, where, message, own, other, seg, lines)
 
-    for step in (1, 2, 4, 8):
+    for step in (2, 1, 4, 8):
         reward = reward + lax.ppermute(reward, "context", [(i, i ^ step) for i in range(devices)])
 
     later, reward = lax.optimization_barrier((later, reward))

time: 98.1 us -> 98.5 us (level)
  Pallas kernels: 15.5 us -> 17 us
  waiting for transfers between devices: 29.6 us -> 28.3 us
    ppermute x4, waiting for transfers between devices: 7.58 us -> 6.26 us  [local(): lax.ppermute(reward, 'context', [(i, i ^ step) for i in range(devices)])]
    pallas_call x1, Pallas kernels: 7.14 us -> 8.15 us  [attention_backward(): pl.pallas_call(functools.partial(backward_kernel, halo), out_shape=(jax.S...]
  transfers between devices with their start and end apart: 9 -> 9, of which waited for: 8 -> 8; matrix products, arithmetic and copies ran while one was open for 0% -> 0% of each run, Pallas kernels for 5% -> 6%
where the time goes in v9:
time: 98.5 us; the launch traced here: 98.7 us
  blocking collectives  29.3 us (30%)
  waiting for transfers between devices  28.3 us (29%)
  starting transfers between devices  22.9 us (23%)
  Pallas kernels  17 us (17%)
    all_to_all x1, blocking collectives, exchange(): lax.all_to_all(array, 'context', 0, 0, tiled=True, axis_index_groups=clus...  29.3 us
    all_to_all x2, waiting for transfers between devices, exchange(): lax.all_to_all(array, 'context', 0, 0, tiled=True, axis_index_groups=clus...  18 us
    all_to_all x2, starting transfers between devices, exchange(): lax.all_to_all(array, 'context', 0, 0, tiled=True, axis_index_groups=clus...  13.3 us
    pallas_call x1, Pallas kernels, attention_backward(): pl.pallas_call(functools.partial(backward_kernel, halo), out_shape=(jax.S...  8.15 us
    ppermute x4, starting transfers between devices, local(): lax.ppermute(reward, 'context', [(i, i ^ step) for i in range(devices)])  7.82 us
    ppermute x4, waiting for transfers between devices, local(): lax.ppermute(reward, 'context', [(i, i ^ step) for i in range(devices)])  6.26 us
    pallas_call x1, Pallas kernels, attention_forward(): pl.pallas_call(functools.partial(forward_kernel, halo), out_shape=(jax.Sh...  4.48 us
    ppermute x3, waiting for transfers between devices, swap(): return lax.ppermute(array, 'context', pairs)  4 us
  transfers between devices with their start and end apart: 9, of which 8 were waited for; matrix products, arithmetic and copies ran while one was open for 0% of the time, Pallas kernels for 6%

profile of v9, /device:TPU:1, one launch (start us, length us, event | category | flops | bytes accessed | tf_op | source)
XLA Modules:
  0.0 98.7 jit_solution(744465294938502537)
XLA Ops:
  0.6 2.3 %pack.1 = bf16[16,200,128]{2,1,0:T(8,128)(2,1)} custom-call(f32[16,128]{1,0:T(8,128)} %readout_ref.3, s32[128]{0:T(128)} %segments_ref.1, s32[128]{0:T(128)} %mask_ref.1, s32[128]{0:T(128)} %labels_ref.1, bf16[128,16,128]{2,1,0:T(8,128)(2,1)} %queries_ref.1, bf16[128,8,128]{2,1,0:T(8,128)(2,1)} %keys_ref.1, bf16[128,8,128]{2,1,0:T(8,128)(2,1)} %values_ref.3), custom_call_target="tpu_custom_call" | custom-call | tf_op jit(solution)/shard_map/pack/pallas_call | solution.py:377
  2.9 0.0 copy-start
  2.9 0.0 copy-start.1
  2.9 7.5 %all-to-all-start = ((bf16[16,200,128]{2,1,0:T(8,128)(2,1)}), bf16[16,200,128]{2,1,0:T(8,128)(2,1)S(1)}, u32[]{:S(2)}, u32[]{:S(2)}) async-start(bf16[16,200,128]{2,1,0:T(8,128)(2,1)} %pack.1), calls=%async_computation | async-start | bytes 1638400 | tf_op jit(solution)/shard_map/all_to_all | solution.py:449
  10.4 0.0 copy-done
  10.4 0.0 copy-done.1
  10.4 1.1 %pack_later.1 = bf16[16,192,128]{2,1,0:T(8,128)(2,1)} custom-call(bf16[128,16,128]{2,1,0:T(8,128)(2,1)S(1)} %copy-done.1, bf16[128,8,128]{2,1,0:T(8,128)(2,1)S(1)} %copy-done), custom_call_target="tpu_custom_call" | custom-call | bytes 3145728 | tf_op jit(solution)/shard_map/pack_later/pallas_call | solution.py:407
  11.5 18.0 %all-to-all-done.message_ref = bf16[16,200,128]{2,1,0:T(8,128)(2,1)S(1)} async-done(((bf16[16,200,128]{2,1,0:T(8,128)(2,1)}), bf16[16,200,128]{2,1,0:T(8,128)(2,1)S(1)}, u32[]{:S(2)}, u32[]{:S(2)}) %all-to-all-start) | async-done | bytes 819232 | tf_op jit(solution)/shard_map/all_to_all | solution.py:449
  29.6 5.8 %all-to-all-start.1 = ((bf16[16,192,128]{2,1,0:T(8,128)(2,1)}), bf16[16,192,128]{2,1,0:T(8,128)(2,1)S(1)}, u32[]{:S(2)}, u32[]{:S(2)}) async-start(bf16[16,192,128]{2,1,0:T(8,128)(2,1)} %pack_later.1), calls=%async_computation.1 | async-start | bytes 1572864 | tf_op jit(solution)/shard_map/all_to_all | solution.py:449
  35.4 0.2 collective-permute-start
  35.5 0.1 copy.19
  35.6 1.3 %collective-permute-done.other_ref = bf16[16,64,128]{2,1,0:T(8,128)(2,1)S(1)} collective-permute-done((bf16[16,64,128]{2,1,0:T(8,128)(2,1)S(1)}, bf16[16,64,128]{2,1,0:T(8,128)(2,1)S(1)}, u32[]{:S(2)}, u32[]{:S(2)}) %collective-permute-start) | collective-permute-done | bytes 262176 | tf_op jit(solution)/shard_map/ppermute | solution.py:454
  37.0 4.5 %attention_forward.1 = (f32[4,512]{1,0:T(4,128)S(1)}, f32[16,128]{1,0:T(8,128)S(1)}, s32[4]{0:T(128)S(1)}) custom-call(s32[1]{0:T(128)} %bitcast.index_ref, bf16[16,200,128]{2,1,0:T(8,128)(2,1)S(1)} %all-to-all-done.message_ref, bf16[16,64,128]{2,1,0:T(8,128)(2,1)S(1)} %slice.21.own_ref, bf16[16,64,128]{2,1,0:T(8,128)(2,1)S(1)} %collective-permute-done.other_ref, ...), custom_call_target="tpu_custom_call" | custom-call | flops 1610612736 | bytes 16777216 | tf_op jit(solution)/shard_map/attention_forward/pallas_call | solution.py:247
  41.4 1.4 %collective-permute-start.1 = (f32[16,128]{1,0:T(8,128)S(1)}, f32[16,128]{1,0:T(8,128)S(1)}, u32[]{:S(2)}, u32[]{:S(2)}) collective-permute-start(f32[16,128]{1,0:T(8,128)S(1)} %get-tuple-element.16), channel_id=1, source_target_pairs={{0,2},{1,3},{2,0},{3,1},{4,6},{5,7},{6,4},{7,5},{8,10},{9,11},{10,... | collective-permute-start | bytes 24584 | tf_op jit(solution)/shard_map/ppermute | solution.py:483
  42.9 1.4 %collective-permute-done.1 = f32[16,128]{1,0:T(8,128)S(1)} collective-permute-done((f32[16,128]{1,0:T(8,128)S(1)}, f32[16,128]{1,0:T(8,128)S(1)}, u32[]{:S(2)}, u32[]{:S(2)}) %collective-permute-start.1) | collective-permute-done | bytes 8224 | tf_op jit(solution)/shard_map/ppermute | solution.py:483
  44.3 1.0 collective-permute-start.2
  45.3 0.8 collective-permute-done.2
  46.1 1.6 %collective-permute-start.3 = (f32[16,128]{1,0:T(8,128)S(1)}, f32[16,128]{1,0:T(8,128)S(1)}, u32[]{:S(2)}, u32[]{:S(2)}) collective-permute-start(f32[16,128]{1,0:T(8,128)S(1)} %add.16), channel_id=1, source_target_pairs={{0,4},{1,5},{2,6},{3,7},{4,0},{5,1},{6,2},{7,3},{8,12},{9,13},{10,... | collective-permute-start | bytes 24584 | tf_op jit(solution)/shard_map/ppermute | solution.py:483
  47.8 1.1 %collective-permute-done.3 = f32[16,128]{1,0:T(8,128)S(1)} collective-permute-done((f32[16,128]{1,0:T(8,128)S(1)}, f32[16,128]{1,0:T(8,128)S(1)}, u32[]{:S(2)}, u32[]{:S(2)}) %collective-permute-start.3) | collective-permute-done | bytes 8224 | tf_op jit(solution)/shard_map/ppermute | solution.py:483
  48.8 3.8 %collective-permute-start.4 = (f32[16,128]{1,0:T(8,128)S(1)}, f32[16,128]{1,0:T(8,128)S(1)}, u32[]{:S(2)}, u32[]{:S(2)}) collective-permute-start(f32[16,128]{1,0:T(8,128)S(1)} %add.17), channel_id=1, source_target_pairs={{0,8},{1,9},{2,10},{3,11},{4,12},{5,13},{6,14},{7,15},{8,0},{9,1},... | collective-permute-start | bytes 24584 | tf_op jit(solution)/shard_map/ppermute | solution.py:483
  52.6 2.9 %collective-permute-done.4 = f32[16,128]{1,0:T(8,128)S(1)} collective-permute-done((f32[16,128]{1,0:T(8,128)S(1)}, f32[16,128]{1,0:T(8,128)S(1)}, u32[]{:S(2)}, u32[]{:S(2)}) %collective-permute-start.4) | collective-permute-done | bytes 8224 | tf_op jit(solution)/shard_map/ppermute | solution.py:483
  55.5 0.0 all-to-all-done.1.later_ref
  55.6 1.2 %collective-permute-start.5 = (bf16[16,64,128]{2,1,0:T(8,128)(2,1)S(1)}, bf16[16,64,128]{2,1,0:T(8,128)(2,1)S(1)}, u32[]{:S(2)}, u32[]{:S(2)}) collective-permute-start(bf16[16,64,128]{2,1,0:T(8,128)(2,1)S(1)} %slice.24.own_value_ref), channel_id=1, source_target_pairs={{0,1},{1,0},{2,3},{3,2},{4,5},{5,4},{6,7},{7,6},{8,9},{9,8},{10,11... | collective-permute-start | bytes 786440 | tf_op jit(solution)/shard_map/ppermute | solution.py:454
  56.8 1.2 %collective-permute-done.5.other_value_ref = bf16[16,64,128]{2,1,0:T(8,128)(2,1)S(1)} collective-permute-done((bf16[16,64,128]{2,1,0:T(8,128)(2,1)S(1)}, bf16[16,64,128]{2,1,0:T(8,128)(2,1)S(1)}, u32[]{:S(2)}, u32[]{:S(2)}) %collective-permute-start.5) | collective-permute-done | bytes 262176 | tf_op jit(solution)/shard_map/ppermute | solution.py:454
  58.0 0.0 copy-done.2
  58.0 8.1 %attention_backward.1 = (bf16[16,128,128]{2,1,0:T(8,128)(2,1)S(1)}, bf16[16,128,128]{2,1,0:T(8,128)(2,1)S(1)}, bf16[16,128,128]{2,1,0:T(8,128)(2,1)S(1)}) custom-call(s32[1]{0:T(128)} %bitcast.index_ref, s32[4]{0:T(128)S(1)} %get-tuple-element.14.starts_ref, bf16[16,200,128]{2,1,0:T(8,128)(2,1)S(1)} %all-to-all-done.message_ref, ...), custom_call_target="tpu_custom_call" | custom-call | flops 4026531840 | bytes 16777216 | tf_op jit(solution)/shard_map/attention_backward/pallas_call | solution.py:277
  66.1 0.4 collective-permute-start.6
  66.6 1.5 %collective-permute-done.6 = bf16[16,128,128]{2,1,0:T(8,128)(2,1)S(1)} collective-permute-done((bf16[16,128,128]{2,1,0:T(8,128)(2,1)S(1)}, bf16[16,128,128]{2,1,0:T(8,128)(2,1)S(1)}, u32[]{:S(2)}, u32[]{:S(2)}) %collective-permute-start.6) | collective-permute-done | bytes 524320 | tf_op jit(solution)/shard_map/ppermute | solution.py:454
  68.1 0.1 add_convert_fusion
  68.3 0.1 pad_maximum_fusion
  68.4 29.3 %all_to_all.15.home_ref = bf16[16,256,128]{2,1,0:T(8,128)(2,1)S(1)} all-to-all(bf16[16,256,128]{2,1,0:T(8,128)(2,1)S(1)} %pad_maximum_fusion), channel_id=1, replica_groups=mesh['groups'=2,'context'=16] {'context'}, dimensions={0} | all-to-all | bytes 2097152 | tf_op jit(solution)/shard_map/all_to_all | solution.py:449
  97.6 1.0 %unpack.1 = (bf16[128,16,128]{2,1,0:T(8,128)(2,1)}, bf16[128,8,128]{2,1,0:T(8,128)(2,1)}, bf16[128,8,128]{2,1,0:T(8,128)(2,1)}) custom-call(bf16[16,256,128]{2,1,0:T(8,128)(2,1)S(1)} %all_to_all.15.home_ref), custom_call_target="tpu_custom_call" | custom-call | tf_op jit(solution)/shard_map/unpack/pallas_call | solution.py:428
  (10 shorter events, 0.1 us)
Async XLA Ops:
  2.9 7.5 %copy-start = (bf16[128,8,128]{2,1,0:T(8,128)(2,1)S(1)}, bf16[128,8,128]{2,1,0:T(8,128)(2,1)}, u32[]{:S(2)}) copy-start(bf16[128,8,128]{2,1,0:T(8,128)(2,1)} %values_ref.3) | copy-start | bytes 786436
  2.9 7.5 %copy-start.1 = (bf16[128,16,128]{2,1,0:T(8,128)(2,1)S(1)}, bf16[128,16,128]{2,1,0:T(8,128)(2,1)}, u32[]{:S(2)}) copy-start(bf16[128,16,128]{2,1,0:T(8,128)(2,1)} %grad_ref.1) | copy-start | bytes 1572868
  2.9 26.6 %all-to-all-start = ((bf16[16,200,128]{2,1,0:T(8,128)(2,1)}), bf16[16,200,128]{2,1,0:T(8,128)(2,1)S(1)}, u32[]{:S(2)}, u32[]{:S(2)}) async-start(bf16[16,200,128]{2,1,0:T(8,128)(2,1)} %pack.1), calls=%async_computation | async-start | bytes 1638400 | tf_op jit(solution)/shard_map/all_to_all | solution.py:449
  29.6 26.0 %all-to-all-start.1 = ((bf16[16,192,128]{2,1,0:T(8,128)(2,1)}), bf16[16,192,128]{2,1,0:T(8,128)(2,1)S(1)}, u32[]{:S(2)}, u32[]{:S(2)}) async-start(bf16[16,192,128]{2,1,0:T(8,128)(2,1)} %pack_later.1), calls=%async_computation.1 | async-start | bytes 1572864 | tf_op jit(solution)/shard_map/all_to_all | solution.py:449
  35.4 1.6 %collective-permute-start = (bf16[16,64,128]{2,1,0:T(8,128)(2,1)S(1)}, bf16[16,64,128]{2,1,0:T(8,128)(2,1)S(1)}, u32[]{:S(2)}, u32[]{:S(2)}) collective-permute-start(bf16[16,64,128]{2,1,0:T(8,128)(2,1)S(1)} %slice.21.own_ref), channel_id=1, source_target_pairs={{0,1},{1,0},{2,3},{3,2},{4,5},{5,4},{6,7},{7,6},{8,9},{9,8},{10,11... | collective-permute-start | bytes 786440 | tf_op jit(solution)/shard_map/ppermute | solution.py:454
  37.0 21.0 %copy-start.2 = (f32[16,128]{1,0:T(8,128)S(1)}, f32[16,128]{1,0:T(8,128)}, u32[]{:S(2)}) copy-start(f32[16,128]{1,0:T(8,128)} %readout_ref.3) | copy-start | bytes 24580
  41.4 2.9 %collective-permute-start.1 = (f32[16,128]{1,0:T(8,128)S(1)}, f32[16,128]{1,0:T(8,128)S(1)}, u32[]{:S(2)}, u32[]{:S(2)}) collective-permute-start(f32[16,128]{1,0:T(8,128)S(1)} %get-tuple-element.16), channel_id=1, source_target_pairs={{0,2},{1,3},{2,0},{3,1},{4,6},{5,7},{6,4},{7,5},{8,10},{9,11},{10,... | collective-permute-start | bytes 24584 | tf_op jit(solution)/shard_map/ppermute | solution.py:483
  44.3 1.8 %collective-permute-start.2 = (f32[16,128]{1,0:T(8,128)S(1)}, f32[16,128]{1,0:T(8,128)S(1)}, u32[]{:S(2)}, u32[]{:S(2)}) collective-permute-start(f32[16,128]{1,0:T(8,128)S(1)} %add.15), channel_id=1, source_target_pairs={{0,1},{1,0},{2,3},{3,2},{4,5},{5,4},{6,7},{7,6},{8,9},{9,8},{10,11... | collective-permute-start | bytes 24584 | tf_op jit(solution)/shard_map/ppermute | solution.py:483
  46.1 2.7 %collective-permute-start.3 = (f32[16,128]{1,0:T(8,128)S(1)}, f32[16,128]{1,0:T(8,128)S(1)}, u32[]{:S(2)}, u32[]{:S(2)}) collective-permute-start(f32[16,128]{1,0:T(8,128)S(1)} %add.16), channel_id=1, source_target_pairs={{0,4},{1,5},{2,6},{3,7},{4,0},{5,1},{6,2},{7,3},{8,12},{9,13},{10,... | collective-permute-start | bytes 24584 | tf_op jit(solution)/shard_map/ppermute | solution.py:483
  48.8 6.7 %collective-permute-start.4 = (f32[16,128]{1,0:T(8,128)S(1)}, f32[16,128]{1,0:T(8,128)S(1)}, u32[]{:S(2)}, u32[]{:S(2)}) collective-permute-start(f32[16,128]{1,0:T(8,128)S(1)} %add.17), channel_id=1, source_target_pairs={{0,8},{1,9},{2,10},{3,11},{4,12},{5,13},{6,14},{7,15},{8,0},{9,1},... | collective-permute-start | bytes 24584 | tf_op jit(solution)/shard_map/ppermute | solution.py:483
  55.6 2.4 %collective-permute-start.5 = (bf16[16,64,128]{2,1,0:T(8,128)(2,1)S(1)}, bf16[16,64,128]{2,1,0:T(8,128)(2,1)S(1)}, u32[]{:S(2)}, u32[]{:S(2)}) collective-permute-start(bf16[16,64,128]{2,1,0:T(8,128)(2,1)S(1)} %slice.24.own_value_ref), channel_id=1, source_target_pairs={{0,1},{1,0},{2,3},{3,2},{4,5},{5,4},{6,7},{7,6},{8,9},{9,8},{10,11... | collective-permute-start | bytes 786440 | tf_op jit(solution)/shard_map/ppermute | solution.py:454
  66.1 2.0 %collective-permute-start.6 = (bf16[16,128,128]{2,1,0:T(8,128)(2,1)S(1)}, bf16[16,128,128]{2,1,0:T(8,128)(2,1)S(1)}, u32[]{:S(2)}, u32[]{:S(2)}) collective-permute-start(bf16[16,128,128]{2,1,0:T(8,128)(2,1)S(1)} %get-tuple-element.22), channel_id=1, source_target_pairs={{0,1},{1,0},{2,3},{3,2},{4,5},{5,4},{6,7},{7,6},{8,9},{9,8},{10,11... | collective-permute-start | bytes 1572872 | tf_op jit(solution)/shard_map/ppermute | solution.py:454
